TPU v7x, 32 devices: a whole 2x2x4 slice. The times are simulated.
32 devices in a mesh: replica: 8 (over z, core), group: 4 (over y, x).
Axes of the slice: x: 2, y: 2, z: 4, core: 2. Of those that a mesh axis runs over, the one named last changes fastest.
Arguments:
- tokens: bfloat16 [4096, 2048], P(('replica', 'group')), may hold values from -6 to 6
- lengths: int32 [8], P('replica'), may hold values from 128 to 512, as said below
- exit_layers: int32 [4096], P(('replica', 'group')), may hold values from 7 to 20, as said below
- pre_gain: bfloat16 [2048], P('group'), may hold values from 0.099609375 to 1.8984375
- pre_shift: bfloat16 [2048], P('group'), may hold values from -3 to 3
- query_weight: bfloat16 [2048, 2048], P('group'), may hold values from -0.1875 to 0.1875
- query_bias: bfloat16 [2048], P('group'), may hold values from -3 to 3
- key_weight: bfloat16 [2048, 2048], P('group'), may hold values from -0.1875 to 0.1875
- value_weight: bfloat16 [2048, 2048], P('group'), may hold values from -0.125 to 0.125
- value_bias: bfloat16 [2048], P('group'), may hold values from -3 to 3
- out_weight: bfloat16 [2048, 2048], P('group'), may hold values from -0.5 to 0.5
- out_bias: bfloat16 [2048], P('group'), may hold values from -1.75 to 1.75
- mid_gain: bfloat16 [2048], P('group'), may hold values from 0.099609375 to 1.8984375
- mid_shift: bfloat16 [2048], P('group'), may hold values from -3 to 3
- up_weight: bfloat16 [2048, 8192], P(None, 'group'), may hold values from -0.125 to 0.125
- up_bias: bfloat16 [8192], P('group'), may hold values from -3 to 3
- down_weight: bfloat16 [8192, 2048], P('group'), may hold values from -0.0625 to 0.0625
- down_bias: bfloat16 [2048], P('group'), may hold values from -1.75 to 1.75
- cotangent: bfloat16 [4096, 2048], P(('replica', 'group')), may hold values from -6 to 6
Outputs:
- output: bfloat16 [4096, 2048], P(('replica', 'group'))
- token_grad: bfloat16 [4096, 2048], P(('replica', 'group'))
- pre_gain_grad: float32 [2048], P('group')
- pre_shift_grad: float32 [2048], P('group')
- query_weight_grad: float32 [2048, 2048], P('group')
- query_bias_grad: float32 [2048], P('group')
- key_weight_grad: float32 [2048, 2048], P('group')
- value_weight_grad: float32 [2048, 2048], P('group')
- value_bias_grad: float32 [2048], P('group')
- out_weight_grad: float32 [2048, 2048], P('group')
- out_bias_grad: float32 [2048], P('group')
- mid_gain_grad: float32 [2048], P('group')
- mid_shift_grad: float32 [2048], P('group')
- up_weight_grad: float32 [2048, 8192], P(None, 'group')
- up_bias_grad: float32 [8192], P('group')
- down_weight_grad: float32 [8192, 2048], P('group')
- down_bias_grad: float32 [2048], P('group')
Inputs may be any that keep to these rules, and one draw needn't show every extreme that they name: `lengths`: some sequence has length 512 and some other has length 128. Within each sequence, exit_layers never rise from one position to the next.
All inputs are finite; a program needn't handle non-finite values.
Results may differ from a plain program's by a relative error of at most 0.02.
Values may be sent and summed in bfloat16 or wider, within the bound.
No kernel may reach another device: no remote copies, remote signals or barrier semaphores. Data moves between devices by JAX's collectives and lax.ppermute only.
A program may use at most 640 MiB of HBM per device.

v0:
```python
import jax
import jax.numpy as jnp
from jax import lax
from jax.sharding import PartitionSpec as P

D = 2048
H = 32
HD = 64
LAYER = 12


def layer_norm(values):
    center = values - jnp.mean(values, -1, keepdims=True)
    spread = jnp.mean(center * center, -1, keepdims=True)
    factor = lax.rsqrt(spread + 1e-05)
    return (center * factor, factor)


def norm_back(grad, normal, factor):
    return factor * (
        grad
        - jnp.mean(grad, -1, keepdims=True)
        - normal * jnp.mean(grad * normal, -1, keepdims=True)
    )


def gelu(values):
    return (
        0.5
        * values
        * (1.0 + jnp.tanh(0.7978845608 * (values + 0.044715 * values * values * values)))
    )


def gelu_back(values, grad):
    inner = 0.7978845608 * (values + 0.044715 * values * values * values)
    tangent = jnp.tanh(inner)
    slope = 0.5 * (1.0 + tangent) + 0.5 * values * (1.0 - tangent * tangent) * 0.7978845608 * (
        1.0 + 3.0 * 0.044715 * values * values
    )
    return grad * slope


def split_heads(matrix):
    groups = max(1, H // 8)
    return matrix.reshape(matrix.shape[0], groups, H // groups, HD).transpose(1, 0, 2, 3)


def join_heads(heads):
    return heads.transpose(1, 0, 2, 3).reshape(heads.shape[1], D)


def score_block(query_group, key_group, allowed):
    scores = (
        jnp.einsum("qhd,khd->hqk", query_group, key_group, preferred_element_type=jnp.float32)
        * 0.125
    )
    return jnp.where(allowed[None], scores, -1e30)


def matmul(left, right):
    return jnp.dot(left, right, preferred_element_type=jnp.float32)


def column_sums(matrix):
    return jnp.sum(matrix.astype(jnp.float32), 0)


def shards(
    tokens,
    lengths,
    exit_layers,
    pre_gain,
    pre_shift,
    query_weight,
    query_bias,
    key_weight,
    value_weight,
    value_bias,
    out_weight,
    out_bias,
    mid_gain,
    mid_shift,
    up_weight,
    up_bias,
    down_weight,
    down_bias,
    cotangent,
):
    local_rows = tokens.shape[0]
    group_count = lax.axis_size("group")
    seq_rows = local_rows * group_count
    member = lax.axis_index("group")
    position = member * local_rows + jnp.arange(local_rows, dtype=jnp.int32)
    active = ((position < lengths[0]) & (exit_layers > LAYER)).astype(jnp.float32)[:, None]
    allowed = jnp.arange(seq_rows, dtype=jnp.int32)[None, :] <= position[:, None]
    (
        gain_one,
        shift_one,
        gain_two,
        shift_two,
        query_full,
        key_full,
        value_full,
        out_full,
        qbias_full,
        vbias_full,
        obias_full,
    ) = (
        lax.all_gather(pre_gain, "group", axis=0, tiled=True),
        lax.all_gather(pre_shift, "group", axis=0, tiled=True),
        lax.all_gather(mid_gain, "group", axis=0, tiled=True),
        lax.all_gather(mid_shift, "group", axis=0, tiled=True),
        lax.all_gather(query_weight, "group", axis=0, tiled=True),
        lax.all_gather(key_weight, "group", axis=0, tiled=True),
        lax.all_gather(value_weight, "group", axis=0, tiled=True),
        lax.all_gather(out_weight, "group", axis=0, tiled=True),
        lax.all_gather(query_bias, "group", axis=0, tiled=True),
        lax.all_gather(value_bias, "group", axis=0, tiled=True),
        lax.all_gather(out_bias, "group", axis=0, tiled=True),
    )
    inputs = tokens.astype(jnp.float32)
    normed_one, factor_one = layer_norm(inputs)
    attn_in = (normed_one * gain_one.astype(jnp.float32) + shift_one.astype(jnp.float32)).astype(
        jnp.bfloat16
    )
    queries = (matmul(attn_in, query_full) + qbias_full.astype(jnp.float32)).astype(jnp.bfloat16)
    keys_local = matmul(attn_in, key_full).astype(jnp.bfloat16)
    values_local = (matmul(attn_in, value_full) + vbias_full.astype(jnp.float32)).astype(
        jnp.bfloat16
    )
    keys_all, values_all = (
        lax.all_gather(keys_local, "group", axis=0, tiled=True),
        lax.all_gather(values_local, "group", axis=0, tiled=True),
    )
    query_heads = split_heads(queries)
    key_heads = split_heads(keys_all)
    value_heads = split_heads(values_all)

    def forward_group(operands):
        query_group, key_group, value_group = operands
        scores = score_block(query_group, key_group, allowed)
        top = jnp.max(scores, -1, keepdims=True)
        logsum = top + jnp.log(jnp.sum(jnp.exp(scores - top), -1, keepdims=True))
        weights = jnp.exp(scores - logsum).astype(jnp.bfloat16)
        context_part = jnp.einsum(
            "hqk,khd->qhd", weights, value_group, preferred_element_type=jnp.float32
        )
        return (context_part, logsum[..., 0])

    context_heads, logsums = lax.map(forward_group, (query_heads, key_heads, value_heads))
    context_low = join_heads(context_heads).astype(jnp.bfloat16)
    attn_out = matmul(context_low, out_full) + obias_full.astype(jnp.float32)
    hidden = inputs + active * attn_out
    normed_two, factor_two = layer_norm(hidden)
    ffn_in = (normed_two * gain_two.astype(jnp.float32) + shift_two.astype(jnp.float32)).astype(
        jnp.bfloat16
    )
    up_full, upbias_full, down_full, downbias_full = (
        lax.all_gather(up_weight, "group", axis=1, tiled=True),
        lax.all_gather(up_bias, "group", axis=0, tiled=True),
        lax.all_gather(down_weight, "group", axis=0, tiled=True),
        lax.all_gather(down_bias, "group", axis=0, tiled=True),
    )
    pre_act = matmul(ffn_in, up_full) + upbias_full.astype(jnp.float32)
    act_low = gelu(pre_act).astype(jnp.bfloat16)
    branch = matmul(act_low, down_full) + downbias_full.astype(jnp.float32)
    output = (hidden + active * branch).astype(jnp.bfloat16)
    first_gain, second_gain, query_back, key_back, value_back, out_back = (
        lax.all_gather(pre_gain, "group", axis=0, tiled=True),
        lax.all_gather(mid_gain, "group", axis=0, tiled=True),
        lax.all_gather(query_weight, "group", axis=0, tiled=True),
        lax.all_gather(key_weight, "group", axis=0, tiled=True),
        lax.all_gather(value_weight, "group", axis=0, tiled=True),
        lax.all_gather(out_weight, "group", axis=0, tiled=True),
    )
    grad_out = cotangent.astype(jnp.float32)
    branch_grad = (active * grad_out).astype(jnp.bfloat16)
    up_back, down_back = (
        lax.all_gather(up_weight, "group", axis=1, tiled=True),
        lax.all_gather(down_weight, "group", axis=0, tiled=True),
    )
    act_grad = matmul(branch_grad, down_back.T)
    pre_grad = gelu_back(pre_act, act_grad).astype(jnp.bfloat16)
    ffn_in_grad = matmul(pre_grad, up_back.T)
    up_grad, up_bias_grad, down_grad, down_bias_grad = (
        lax.psum_scatter(
            matmul(ffn_in.T, pre_grad).astype(jnp.bfloat16),
            "group",
            scatter_dimension=1,
            tiled=True,
        ).astype(jnp.float32),
        lax.psum_scatter(
            column_sums(pre_grad).astype(jnp.bfloat16), "group", scatter_dimension=0, tiled=True
        ).astype(jnp.float32),
        lax.psum_scatter(
            matmul(act_low.T, branch_grad).astype(jnp.bfloat16),
            "group",
            scatter_dimension=0,
            tiled=True,
        ).astype(jnp.float32),
        lax.psum_scatter(
            column_sums(branch_grad).astype(jnp.bfloat16), "group", scatter_dimension=0, tiled=True
        ).astype(jnp.float32),
    )
    mid_gain_part = jnp.sum(ffn_in_grad * normed_two, 0)
    mid_shift_part = jnp.sum(ffn_in_grad, 0)
    hidden_grad = grad_out + norm_back(
        ffn_in_grad * second_gain.astype(jnp.float32), normed_two, factor_two
    )
    attn_grad = (active * hidden_grad).astype(jnp.bfloat16)
    context_grad = matmul(attn_grad, out_back.T).astype(jnp.bfloat16)
    out_bias_part = column_sums(attn_grad)

    def backward_group(operands):
        query_group, key_group, value_group, grad_group, logsum_group = operands
        scores = score_block(query_group, key_group, allowed)
        probs = jnp.exp(scores - logsum_group[..., None])
        probs_grad = jnp.einsum(
            "qhd,khd->hqk", grad_group, value_group, preferred_element_type=jnp.float32
        )
        delta = jnp.sum(probs * probs_grad, -1, keepdims=True)
        score_grad = (probs * (probs_grad - delta)).astype(jnp.bfloat16)
        query_part = (
            jnp.einsum("hqk,khd->qhd", score_grad, key_group, preferred_element_type=jnp.float32)
            * 0.125
        )
        key_part = (
            jnp.einsum("hqk,qhd->khd", score_grad, query_group, preferred_element_type=jnp.float32)
            * 0.125
        )
        value_part = jnp.einsum(
            "hqk,qhd->khd",
            probs.astype(jnp.bfloat16),
            grad_group,
            preferred_element_type=jnp.float32,
        )
        return (query_part, key_part, value_part)

    query_parts, key_parts, value_parts = lax.map(
        backward_group, (query_heads, key_heads, value_heads, split_heads(context_grad), logsums)
    )
    query_grad = join_heads(query_parts).astype(jnp.bfloat16)
    key_sum, value_sum = (
        lax.psum_scatter(
            join_heads(key_parts).astype(jnp.bfloat16), "group", scatter_dimension=0, tiled=True
        ).astype(jnp.float32),
        lax.psum_scatter(
            join_heads(value_parts).astype(jnp.bfloat16), "group", scatter_dimension=0, tiled=True
        ).astype(jnp.float32),
    )
    key_grad = key_sum.astype(jnp.bfloat16)
    value_grad = value_sum.astype(jnp.bfloat16)
    in_grad = (
        matmul(query_grad, query_back.T)
        + matmul(key_grad, key_back.T)
        + matmul(value_grad, value_back.T)
    )
    pre_gain_part = jnp.sum(in_grad * normed_one, 0)
    pre_shift_part = jnp.sum(in_grad, 0)
    token_grad = (
        hidden_grad + norm_back(in_grad * first_gain.astype(jnp.float32), normed_one, factor_one)
    ).astype(jnp.bfloat16)
    (
        pre_gain_grad,
        pre_shift_grad,
        mid_gain_grad,
        mid_shift_grad,
        query_wgrad,
        key_wgrad,
        value_wgrad,
        out_wgrad,
        query_bgrad,
        value_bgrad,
        out_bgrad,
    ) = (
        lax.psum_scatter(
            pre_gain_part.astype(jnp.bfloat16), "group", scatter_dimension=0, tiled=True
        ).astype(jnp.float32),
        lax.psum_scatter(
            pre_shift_part.astype(jnp.bfloat16), "group", scatter_dimension=0, tiled=True
        ).astype(jnp.float32),
        lax.psum_scatter(
            mid_gain_part.astype(jnp.bfloat16), "group", scatter_dimension=0, tiled=True
        ).astype(jnp.float32),
        lax.psum_scatter(
            mid_shift_part.astype(jnp.bfloat16), "group", scatter_dimension=0, tiled=True
        ).astype(jnp.float32),
        lax.psum_scatter(
            matmul(attn_in.T, query_grad).astype(jnp.bfloat16),
            "group",
            scatter_dimension=0,
            tiled=True,
        ).astype(jnp.float32),
        lax.psum_scatter(
            matmul(attn_in.T, key_grad).astype(jnp.bfloat16),
            "group",
            scatter_dimension=0,
            tiled=True,
        ).astype(jnp.float32),
        lax.psum_scatter(
            matmul(attn_in.T, value_grad).astype(jnp.bfloat16),
            "group",
            scatter_dimension=0,
            tiled=True,
        ).astype(jnp.float32),
        lax.psum_scatter(
            matmul(context_low.T, attn_grad).astype(jnp.bfloat16),
            "group",
            scatter_dimension=0,
            tiled=True,
        ).astype(jnp.float32),
        lax.psum_scatter(
            column_sums(query_grad).astype(jnp.bfloat16), "group", scatter_dimension=0, tiled=True
        ).astype(jnp.float32),
        lax.psum_scatter(
            column_sums(value_grad).astype(jnp.bfloat16), "group", scatter_dimension=0, tiled=True
        ).astype(jnp.float32),
        lax.psum_scatter(
            out_bias_part.astype(jnp.bfloat16), "group", scatter_dimension=0, tiled=True
        ).astype(jnp.float32),
    )
    totals = (
        lax.psum(pre_gain_grad.astype(jnp.bfloat16), "replica").astype(jnp.float32),
        lax.psum(pre_shift_grad.astype(jnp.bfloat16), "replica").astype(jnp.float32),
        lax.psum(query_wgrad.astype(jnp.bfloat16), "replica").astype(jnp.float32),
        lax.psum(query_bgrad.astype(jnp.bfloat16), "replica").astype(jnp.float32),
        lax.psum(key_wgrad.astype(jnp.bfloat16), "replica").astype(jnp.float32),
        lax.psum(value_wgrad.astype(jnp.bfloat16), "replica").astype(jnp.float32),
        lax.psum(value_bgrad.astype(jnp.bfloat16), "replica").astype(jnp.float32),
        lax.psum(out_wgrad.astype(jnp.bfloat16), "replica").astype(jnp.float32),
        lax.psum(out_bgrad.astype(jnp.bfloat16), "replica").astype(jnp.float32),
        lax.psum(mid_gain_grad.astype(jnp.bfloat16), "replica").astype(jnp.float32),
        lax.psum(mid_shift_grad.astype(jnp.bfloat16), "replica").astype(jnp.float32),
        lax.psum(up_grad.astype(jnp.bfloat16), "replica").astype(jnp.float32),
        lax.psum(up_bias_grad.astype(jnp.bfloat16), "replica").astype(jnp.float32),
        lax.psum(down_grad.astype(jnp.bfloat16), "replica").astype(jnp.float32),
        lax.psum(down_bias_grad.astype(jnp.bfloat16), "replica").astype(jnp.float32),
    )
    return (
        output,
        token_grad,
        totals[0],
        totals[1],
        totals[2],
        totals[3],
        totals[4],
        totals[5],
        totals[6],
        totals[7],
        totals[8],
        totals[9],
        totals[10],
        totals[11],
        totals[12],
        totals[13],
        totals[14],
    )


def solution(mesh):
    return jax.shard_map(
        shards,
        mesh=mesh,
        in_specs=(
            P(("replica", "group"), None),
            P("replica"),
            P(("replica", "group")),
            P("group"),
            P("group"),
            P("group", None),
            P("group"),
            P("group", None),
            P("group", None),
            P("group"),
            P("group", None),
            P("group"),
            P("group"),
            P("group"),
            P(None, "group"),
            P("group"),
            P("group", None),
            P("group"),
            P(("replica", "group"), None),
        ),
        out_specs=(
            P(("replica", "group"), None),
            P(("replica", "group"), None),
            P("group"),
            P("group"),
            P("group", None),
            P("group"),
            P("group", None),
            P("group", None),
            P("group"),
            P("group", None),
            P("group"),
            P("group"),
            P("group"),
            P(None, "group"),
            P("group"),
            P("group", None),
            P("group"),
        ),
        check_vma=False,
    )
```

profile of v0, /device:TPU:0, one launch (start us, length us, event | category | flops | bytes accessed | tf_op | source)
XLA Modules:
  0.0 2687.4 jit_solution(7998907598796842740)
XLA Ops:
  9.5 9.5 all-gather.2
  34.8 65.6 %all-gather.17.cloned.1.call-done = bf16[2048,2048]{1,0:T(8,128)(2,1)} async-done(((bf16[512,2048]{1,0:T(8,128)(2,1)}), bf16[2048,2048]{1,0:T(8,128)(2,1)}) %all-gather.17.cloned.1.call-update) | async-done | bytes 8388624 | tf_op jit(solution)/shard_map/all_gather | solution.py:116
  105.9 83.9 %all-gather.23.cloned.1.call-done = bf16[2048,2048]{1,0:T(8,128)(2,1)} async-done(((bf16[512,2048]{1,0:T(8,128)(2,1)}), bf16[2048,2048]{1,0:T(8,128)(2,1)}) %all-gather.23.cloned.1.call-update) | async-done | bytes 8388624 | tf_op jit(solution)/shard_map/all_gather | solution.py:115
  213.5 8.3 all_gather.73
  237.1 42.5 %all-gather.21.cloned.1.call-done = bf16[2048,2048]{1,0:T(8,128)(2,1)} async-done(((bf16[512,2048]{1,0:T(8,128)(2,1)}), bf16[2048,2048]{1,0:T(8,128)(2,1)}) %all-gather.21.cloned.1.call-update) | async-done | bytes 8388624 | tf_op jit(solution)/shard_map/all_gather | solution.py:114
  284.6 32.6 %all-gather.19.cloned.1.call-done = bf16[512,2048]{1,0:T(8,128)(2,1)} async-done(((bf16[128,2048]{1,0:T(8,128)(2,1)}), bf16[512,2048]{1,0:T(8,128)(2,1)}) %all-gather.19.cloned.1.call-update) | async-done | bytes 2097168 | tf_op jit(solution)/shard_map/all_gather | solution.py:134
  321.3 33.5 %all-gather.25.cloned.1.call-done = bf16[512,2048]{1,0:T(8,128)(2,1)} async-done(((bf16[128,2048]{1,0:T(8,128)(2,1)}), bf16[512,2048]{1,0:T(8,128)(2,1)}) %all-gather.25.cloned.1.call-update) | async-done | bytes 2097168 | tf_op jit(solution)/shard_map/all_gather | solution.py:133
  358.6 15.8 while.28
  374.4 69.8 %all-gather.27.cloned.1.call-done = bf16[2048,2048]{1,0:T(8,128)(2,1)} async-done(((bf16[512,2048]{1,0:T(8,128)(2,1)}), bf16[2048,2048]{1,0:T(8,128)(2,1)}) %all-gather.27.cloned.1.call-update) | async-done | bytes 8388624 | tf_op jit(solution)/shard_map/all_gather | solution.py:117
  450.3 292.9 %all-gather.29.cloned.1.call-done = bf16[2048,8192]{1,0:T(8,128)(2,1)} async-done(((bf16[2048,2048]{1,0:T(8,128)(2,1)}), bf16[2048,8192]{1,0:T(8,128)(2,1)}) %all-gather.29.cloned.1.call-update) | async-done | bytes 33554448 | tf_op jit(solution)/shard_map/all_gather | solution.py:160
  743.3 20.8 convolution_add_fusion
  764.0 278.3 %all-gather.31.cloned.1.call-done = bf16[8192,2048]{1,0:T(8,128)(2,1)} async-done(((bf16[2048,2048]{1,0:T(8,128)(2,1)}), bf16[8192,2048]{1,0:T(8,128)(2,1)}) %all-gather.31.cloned.1.call-update) | async-done | bytes 33554448 | tf_op jit(solution)/shard_map/all_gather | solution.py:162
  1042.3 18.8 fusion.81
  1061.2 19.7 multiply_reduce_fusion.1
  1095.0 31.3 %while.29 = (s32[]{:T(128)}, bf16[4,128,8,64]{1,3,2,0:T(8,128)(2,1)}, bf16[4,512,8,64]{1,3,2,0:T(8,128)(2,1)}, bf16[4,512,8,64]{1,3,2,0:T(8,128)(2,1)}, bf16[4,5...) while((s32[]{:T(128)}, ...), condition=%wide.region_12.13_spmd.clone, body=%wide.region_10.12_spmd.clone.sunk | while | flops 340655104 | bytes 58091296 | solution.py:240
  1147.0 18.6 reduce-scatter.25.cloned.1.call-done
  1172.5 31.9 %reduce-scatter.27.cloned.1.call-done = bf16[128,2048]{1,0:T(8,128)(2,1)} async-done(((bf16[512,2048]{1,0:T(8,128)(2,1)}), bf16[128,2048]{1,0:T(8,128)(2,1)}) %reduce-scatter.27.cloned.1.call-update) | async-done | bytes 524304
  1212.4 15.7 convolution_convert_fusion
  1229.1 16.6 convolution_convert_fusion.1
  1245.8 48.8 %reduce-scatter.15.cloned.1.call-done = bf16[512,2048]{1,0:T(8,128)(2,1)} async-done(((bf16[2048,2048]{1,0:T(8,128)(2,1)}), bf16[512,2048]{1,0:T(8,128)(2,1)}) %reduce-scatter.15.cloned.1.call-update) | async-done | bytes 2097168 | tf_op jit(solution)/shard_map/reduce_scatter | solution.py:289
  1294.5 89.6 %reduce-scatter.21.cloned.1.call-done = bf16[512,2048]{1,0:T(8,128)(2,1)} async-done(((bf16[2048,2048]{1,0:T(8,128)(2,1)}), bf16[512,2048]{1,0:T(8,128)(2,1)}) %reduce-scatter.21.cloned.1.call-update) | async-done | bytes 2097168 | tf_op jit(solution)/shard_map/reduce_scatter | solution.py:307
  1384.2 90.1 %reduce-scatter.17.cloned.1.call-done = bf16[512,2048]{1,0:T(8,128)(2,1)} async-done(((bf16[2048,2048]{1,0:T(8,128)(2,1)}), bf16[512,2048]{1,0:T(8,128)(2,1)}) %reduce-scatter.17.cloned.1.call-update) | async-done | bytes 2097168 | tf_op jit(solution)/shard_map/reduce_scatter | solution.py:295
  1474.2 89.6 %reduce-scatter.19.cloned.1.call-done = bf16[512,2048]{1,0:T(8,128)(2,1)} async-done(((bf16[2048,2048]{1,0:T(8,128)(2,1)}), bf16[512,2048]{1,0:T(8,128)(2,1)}) %reduce-scatter.19.cloned.1.call-update) | async-done | bytes 2097168 | tf_op jit(solution)/shard_map/reduce_scatter | solution.py:301
  1563.9 291.6 %reduce-scatter.23.cloned.1.call-done = bf16[2048,2048]{1,0:T(8,128)(2,1)} async-done(((bf16[2048,8192]{1,0:T(8,128)(2,1)}), bf16[2048,2048]{1,0:T(8,128)(2,1)}) %reduce-scatter.23.cloned.1.call-update) | async-done | bytes 8388624 | tf_op jit(solution)/shard_map/reduce_scatter | solution.py:187
  1855.5 291.9 %reduce-scatter.29.cloned.1.call-done = bf16[2048,2048]{1,0:T(8,128)(2,1)} async-done(((bf16[8192,2048]{1,0:T(8,128)(2,1)}), bf16[2048,2048]{1,0:T(8,128)(2,1)}) %reduce-scatter.29.cloned.1.call-update) | async-done | bytes 8388624
  2148.0 8.1 all-gather.7
  2164.9 18.0 fusion.52
  2196.2 16.3 all-reduce.12
  2213.1 28.0 %all-reduce.10 = (bf16[512]{0:T(512)(128)(2,1)S(1)}, bf16[512]{0:T(512)(128)(2,1)S(1)}, bf16[512]{0:T(512)(128)(2,1)S(1)}, bf16[512]{0:T(512)(128)(2,1)S(1)}, bf...) all-reduce(bf16[512]{0:T(512)(128)(2,1)S(1)} %dynamic-slice.1, ...), channel_id=1, replica_groups=mesh['replica'=8,'group'=4] {'replica'}, use_global_device_ids=true, to_apply=%region_19.20 | all-reduce | flops 6144 | bytes 24576 | tf_op jit(solution)/shard_map/psum | solution.py:324
  2247.6 397.6 %all-reduce.15.cloned.1.call-done = (bf16[512,2048]{1,0:T(8,128)(2,1)}, bf16[512,2048]{1,0:T(8,128)(2,1)}, bf16[512,2048]{1,0:T(8,128)(2,1)}, bf16[512,2048]{1,0...) async-done(((bf16[512,2048]{1,0:T(8,128)(2,1)}, bf16[512,2048]{1,0:T(8,128)(2,1)}, bf16[512,2048]{1,0:T(8,128)(2,1)}, bf16[512,2048]{1,0:T(8,128)(2,1)}, ...) | async-done | bytes 25165840 | tf_op jit(solution)/shard_map/psum | solution.py:326
  2657.1 11.7 convert_element_type.296
  2668.8 11.7 convert_element_type.299
  (284 shorter events, 218.1 us)
Async XLA Ops:
  7.2 11.9 copy-start.23
  7.2 19.9 copy-start.24
  7.2 27.1 %copy-start = (bf16[128,2048]{1,0:T(8,128)(2,1)S(1)}, bf16[128,2048]{1,0:T(8,128)(2,1)}, u32[]{:S(2)}) copy-start(bf16[128,2048]{1,0:T(8,128)(2,1)} %param.23) | copy-start | bytes 1572868
  7.2 93.1 %all-gather.17.cloned.1.call-start = ((), (), s32[]{:S(2)}) async-start(), calls=%async_computation.8 | async-start | bytes 10485760 | tf_op jit(solution)/shard_map/all_gather | solution.py:116
  8.0 181.9 %all-gather.23.cloned.1.call-start = ((), (), s32[]{:S(2)}) async-start(), calls=%async_computation.11 | async-start | bytes 10485760 | tf_op jit(solution)/shard_map/all_gather | solution.py:115
  8.7 270.9 %all-gather.21.cloned.1.call-start = ((), (), s32[]{:S(2)}) async-start(), calls=%async_computation.10 | async-start | bytes 10485760 | tf_op jit(solution)/shard_map/all_gather | solution.py:114
  9.4 307.7 %all-gather.19.cloned.1.call-start = ((), (), s32[]{:S(2)}) async-start(), calls=%async_computation.9 | async-start | bytes 2621440 | tf_op jit(solution)/shard_map/all_gather | solution.py:134
  105.9 248.9 %all-gather.25.cloned.1.call-start = ((), (), s32[]{:S(2)}) async-start(), calls=%async_computation.12 | async-start | bytes 2621440 | tf_op jit(solution)/shard_map/all_gather | solution.py:133
  195.4 248.8 %all-gather.27.cloned.1.call-start = ((), (), s32[]{:S(2)}) async-start(), calls=%async_computation.13 | async-start | bytes 10485760 | tf_op jit(solution)/shard_map/all_gather | solution.py:117
  195.9 547.3 %all-gather.29.cloned.1.call-start = ((), (), s32[]{:S(2)}) async-start(), calls=%async_computation.14 | async-start | bytes 41943040 | tf_op jit(solution)/shard_map/all_gather | solution.py:160
  196.7 9.0 copy-start.26
  196.7 16.8 copy-start.21
  196.7 25.1 copy-start.27
  196.7 32.2 %copy-start.28 = (bf16[512]{0:T(512)(128)(2,1)S(1)}, bf16[512]{0:T(512)(128)(2,1)}, u32[]{:S(2)}) copy-start(bf16[512]{0:T(512)(128)(2,1)} %param.35) | copy-start | bytes 3076
  196.7 40.3 %copy-start.30 = (s32[128]{0:T(128)S(1)}, s32[128]{0:T(128)}, u32[]{:S(2)}) copy-start(s32[128]{0:T(128)} %param.25) | copy-start | bytes 1540
  196.8 845.6 %all-gather.31.cloned.1.call-start = ((), (), s32[]{:S(2)}) async-start(), calls=%async_computation.15 | async-start | bytes 41943040 | tf_op jit(solution)/shard_map/all_gather | solution.py:162
  197.5 968.0 %reduce-scatter.25.cloned.1.call-start = ((), (), s32[]{:S(2)}) async-start(), calls=%async_computation.21 | async-start | bytes 2621440
  1098.5 3.0 copy-start.7
  1106.3 3.0 copy-start.7
  1130.2 4.1 copy-start.8
  1130.2 74.2 %reduce-scatter.27.cloned.1.call-start = ((), (), s32[]{:S(2)}) async-start(), calls=%async_computation.22 | async-start | bytes 2621440
  1134.2 160.3 %reduce-scatter.15.cloned.1.call-start = ((), (), s32[]{:S(2)}) async-start(), calls=%async_computation.16 | async-start | bytes 10485760 | tf_op jit(solution)/shard_map/reduce_scatter | solution.py:289
  1140.2 244.0 %reduce-scatter.21.cloned.1.call-start = ((), (), s32[]{:S(2)}) async-start(), calls=%async_computation.19 | async-start | bytes 10485760 | tf_op jit(solution)/shard_map/reduce_scatter | solution.py:307
  1146.9 327.3 %reduce-scatter.17.cloned.1.call-start = ((), (), s32[]{:S(2)}) async-start(), calls=%async_computation.17 | async-start | bytes 10485760 | tf_op jit(solution)/shard_map/reduce_scatter | solution.py:295
  1172.5 391.4 %reduce-scatter.19.cloned.1.call-start = ((), (), s32[]{:S(2)}) async-start(), calls=%async_computation.18 | async-start | bytes 10485760 | tf_op jit(solution)/shard_map/reduce_scatter | solution.py:301
  1211.2 644.3 %reduce-scatter.23.cloned.1.call-start = ((), (), s32[]{:S(2)}) async-start(), calls=%async_computation.20 | async-start | bytes 41943040 | tf_op jit(solution)/shard_map/reduce_scatter | solution.py:187
  1228.1 919.2 %reduce-scatter.29.cloned.1.call-start = ((), (), s32[]{:S(2)}) async-start(), calls=%async_computation.23 | async-start | bytes 41943040
  1245.7 1399.5 %all-reduce.15.cloned.1.call-start = ((), (), s32[]{:S(2)}) async-start(), calls=%async_computation.24 | async-start | bytes 50331648 | tf_op jit(solution)/shard_map/psum | solution.py:326
  2147.4 8.8 copy-start.31
  2164.8 18.1 copy-start.9
  2189.5 56.9 %copy-start.12 = (f32[128,2048]{1,0:T(8,128)S(1)}, f32[128,2048]{1,0:T(8,128)}, u32[]{:S(2)}) copy-start(f32[128,2048]{1,0:T(8,128)} %get-tuple-element.224) | copy-start | bytes 3145732
  2645.2 4.3 copy-start.16
  (41 other events, 64.2 us)
Sparse Core Ops, SparseCore 0:
  9.9 90.3 all-gather.16
  102.2 87.5 all-gather.22
  191.7 87.8 all-gather.20
  281.8 35.3 all-gather.18
  319.5 35.2 all-gather.24
  356.5 87.5 all-gather.26
  446.0 297.2 all-gather.28
  745.1 297.2 all-gather.30
  1130.3 35.1 reduce-scatter.24
  1169.2 35.1 reduce-scatter.26
  1208.1 86.3 reduce-scatter.14
  1297.7 86.3 reduce-scatter.20
  1387.8 86.3 reduce-scatter.16
  1477.4 86.3 reduce-scatter.18
  1566.8 288.6 reduce-scatter.22
  1858.7 288.6 reduce-scatter.28
  2150.5 494.6 all-reduce.14
where the time goes:
time: 2690 us
  waiting for transfers between devices  2250 us (84%)
  matrix products  210 us (8%)
  blocking collectives  116 us (4%)
  other arithmetic  50.9 us (2%)
  local copies, waits for them, and re-layouts  39.5 us (1%)
    psum x1, waiting for transfers between devices, shards(): lax.psum(query_wgrad.astype(jnp.bfloat16), 'replica').astype(jnp.float32)  398 us
    unnamed x20, waiting for transfers between devices  346 us
    all_gather x1, waiting for transfers between devices, shards(): lax.all_gather(up_weight, 'group', axis=1, tiled=True)  293 us
    reduce_scatter x1, waiting for transfers between devices, shards(): lax.psum_scatter(matmul(ffn_in.T, pre_grad).astype(jnp.bfloat16), 'group'...  292 us
    all_gather x1, waiting for transfers between devices, shards(): lax.all_gather(down_weight, 'group', axis=0, tiled=True)  278 us
    dot_general x18, matrix products, matmul(): return jnp.dot(left, right, preferred_element_type=jnp.float32)  182 us
    reduce_scatter x1, waiting for transfers between devices, shards(): lax.psum_scatter(matmul(attn_in.T, key_grad).astype(jnp.bfloat16), 'group...  90.1 us
    reduce_scatter x1, waiting for transfers between devices, shards(): lax.psum_scatter(matmul(attn_in.T, value_grad).astype(jnp.bfloat16), 'gro...  89.6 us
  transfers between devices with their start and end apart: 17, of which 17 were waited for; matrix products, arithmetic and copies ran while one was open for 6% of the time, Pallas kernels for 0%

commit v1 on v0

v1 whole, which is shorter than its diff:
```python
import jax
import jax.numpy as jnp
from jax import lax
from jax.sharding import PartitionSpec as P

HD = 64
LAYER = 12

bf16 = jnp.bfloat16
f32 = jnp.float32


def layer_norm(values):
    center = values - jnp.mean(values, -1, keepdims=True)
    spread = jnp.mean(center * center, -1, keepdims=True)
    factor = lax.rsqrt(spread + 1e-05)
    return (center * factor, factor)


def norm_back(grad, normal, factor):
    return factor * (
        grad
        - jnp.mean(grad, -1, keepdims=True)
        - normal * jnp.mean(grad * normal, -1, keepdims=True)
    )


def gelu_both(values):
    inner = 0.7978845608 * (values + 0.044715 * values * values * values)
    tangent = jnp.tanh(inner)
    slope = 0.5 * (1.0 + tangent) + 0.5 * values * (1.0 - tangent * tangent) * 0.7978845608 * (
        1.0 + 3.0 * 0.044715 * values * values
    )
    return 0.5 * values * (1.0 + tangent), slope


def matmul(left, right):
    return jnp.dot(left, right, preferred_element_type=f32)


def matmul_nt(left, right):
    return lax.dot_general(left, right, (((1,), (1,)), ((), ())), preferred_element_type=f32)


def matmul_tn(left, right):
    return lax.dot_general(left, right, (((0,), (0,)), ((), ())), preferred_element_type=f32)


def column_sums(matrix):
    return jnp.sum(matrix.astype(f32), 0)


def swap(block, step):
    count = lax.axis_size("group")
    return lax.ppermute(block, "group", [(i, i ^ step) for i in range(count)])


def exchange(blocks):
    return [blocks[0]] + [swap(blocks[step], step) for step in range(1, len(blocks))]


def gather_blocks(block):
    return exchange([block] * lax.axis_size("group"))


def in_order(blocks):
    me = lax.axis_index("group")
    rows = blocks[0].shape[0]
    whole = jnp.zeros((len(blocks) * rows,) + blocks[0].shape[1:], blocks[0].dtype)
    for step, block in enumerate(blocks):
        start = ((me ^ step) * rows,) + (0,) * (block.ndim - 1)
        whole = lax.dynamic_update_slice(whole, block, start)
    return whole


def scatter_terms(partial):
    count = lax.axis_size("group")
    me = lax.axis_index("group")
    rows = partial.shape[0] // count
    terms = [lax.dynamic_slice_in_dim(partial, me * rows, rows, 0)]
    for step in range(1, count):
        sent = lax.dynamic_slice_in_dim(partial, (me ^ step) * rows, rows, 0)
        terms.append(swap(sent.astype(bf16), step).astype(f32))
    return terms


def scatter_sum(partial):
    return sum(scatter_terms(partial))


def gather_rows(block):
    return lax.all_gather(block, "group", axis=0, tiled=True)


def scatter_rows(partial):
    return lax.psum_scatter(
        partial.astype(bf16), "group", scatter_dimension=0, tiled=True
    ).astype(f32)


def reorder(stack):
    me = lax.axis_index("group")
    count = stack.shape[0]
    bit = 1
    while bit < count:
        pairs = stack.reshape((count // (2 * bit), 2, bit) + stack.shape[1:])
        pairs = jnp.where((me & bit) != 0, pairs[:, ::-1], pairs)
        stack = pairs.reshape(stack.shape)
        bit *= 2
    return stack


def after(value, *others):
    return lax.optimization_barrier((value,) + others)[0]


def core_swap(block):
    count = lax.axis_size("replica")
    return lax.ppermute(block, "replica", [(i, i ^ 1) for i in range(count)])


def core_join(mine, axis):
    core = lax.axis_index("replica") % 2
    other = core_swap(mine)
    first = jnp.where(core == 0, mine, other)
    second = jnp.where(core == 0, other, mine)
    return jnp.concatenate([first, second], axis)


class Order:
    def __init__(self):
        self.last = ()

    def __call__(self, *values):
        values = lax.optimization_barrier(values + self.last)[: len(values)]
        return values[0] if len(values) == 1 else values

    def mark(self, *values):
        self.last = values


def replica_sum_small(values):
    count = lax.axis_size("replica")
    step = 1
    while step < count:
        values = values + lax.ppermute(values, "replica", [(i, i ^ step) for i in range(count)])
        step *= 2
    return values


def shards(
    tokens,
    lengths,
    exit_layers,
    pre_gain,
    pre_shift,
    query_weight,
    query_bias,
    key_weight,
    value_weight,
    value_bias,
    out_weight,
    out_bias,
    mid_gain,
    mid_shift,
    up_weight,
    up_bias,
    down_weight,
    down_bias,
    cotangent,
):
    rows, width = tokens.shape
    count = lax.axis_size("group")
    me = lax.axis_index("group")
    cols = width // count
    heads = cols // HD
    local = me * rows + jnp.arange(rows, dtype=jnp.int32)
    active = ((local < lengths[0]) & (exit_layers > LAYER)).astype(f32)[:, None]
    position = jnp.arange(count * rows, dtype=jnp.int32)
    allowed = position[None, :] <= position[:, None]
    core = lax.axis_index("replica") % 2
    half = cols // 2

    grad_out = cotangent.astype(f32)
    branch_grad = (active * grad_out).astype(bf16)
    tokens_all = in_order(gather_blocks(tokens))

    vectors = jnp.concatenate([pre_gain, pre_shift, out_bias, mid_gain, mid_shift, down_bias])
    vectors = vectors.reshape(2, 3 * cols)

    def column_block(step, start, length):
        at = (start, (me ^ step) * cols)
        parts = [
            lax.dynamic_slice(w, at, (length, cols)) for w in (query_weight, key_weight, value_weight)
        ]
        return jnp.concatenate(parts, 1)

    blocks = [vectors] + [
        jnp.concatenate([column_block(step, core * half, half), vectors])
        for step in range(1, count)
    ]
    blocks = exchange(blocks)
    arrived = jnp.stack([block[:half] for block in blocks[1:]])
    vectors = in_order([block[-2:][None] for block in blocks]).reshape(count, 6, cols)
    vectors = vectors.transpose(1, 0, 2).reshape(6, width).astype(f32)
    gain_one, shift_one, obias, gain_two, shift_two, dbias = (vectors[i] for i in range(6))
    others = core_swap(arrived)
    qkv_weight = jnp.zeros((count, 2, half, 3 * cols), bf16)
    for step in range(1, count):
        for place, block in ((core, arrived), (1 - core, others)):
            qkv_weight = lax.dynamic_update_slice(
                qkv_weight, block[step - 1][None, None], (me ^ step, place, 0, 0)
            )
    own = column_block(0, 0, cols).reshape(1, 2, half, 3 * cols)
    qkv_weight = lax.dynamic_update_slice(qkv_weight, own, (me, 0, 0, 0))
    qkv_weight = qkv_weight.reshape(width, 3 * cols)
    branch_blocks = gather_blocks(after(branch_grad, arrived))
    branch_all = in_order(branch_blocks)
    everyone = ("replica", "group")
    branch_wide = lax.all_gather(branch_grad, everyone, axis=0, tiled=True)

    normed_all, _ = layer_norm(tokens_all.astype(f32))
    attn_in = (normed_all * gain_one + shift_one).astype(bf16)
    qkv_bias = jnp.concatenate([query_bias, jnp.zeros_like(query_bias), value_bias]).astype(f32)
    qkv = (matmul(attn_in, qkv_weight) + qkv_bias).astype(bf16)
    queries, keys, values = (
        qkv[:, k * cols : (k + 1) * cols].reshape(-1, heads, HD) for k in range(3)
    )

    def scores_of(query, key):
        scores = jnp.einsum("qhd,khd->hqk", query, key, preferred_element_type=f32) * 0.125
        return jnp.where(allowed[None], scores, -1e30)

    scores = scores_of(queries, keys)
    top = jnp.max(scores, -1, keepdims=True)
    logsum = top + jnp.log(jnp.sum(jnp.exp(scores - top), -1, keepdims=True))
    weights = jnp.exp(scores - logsum).astype(bf16)
    context = (
        jnp.einsum("hqk,khd->qhd", weights, values, preferred_element_type=f32)
        .astype(bf16)
        .reshape(-1, cols)
    )
    context = after(context, *branch_blocks)
    attn_out = scatter_sum(matmul(context, out_weight)) + obias
    hidden = tokens.astype(f32) + active * attn_out
    normed_two, factor_two = layer_norm(hidden)
    ffn_in = (normed_two * gain_two + shift_two).astype(bf16)
    act_grad = matmul_nt(branch_all, down_weight)
    ffn_all = in_order(gather_blocks(ffn_in))
    ffn_wide = lax.all_gather(ffn_in, everyone, axis=0, tiled=True)
    pre_act = matmul(ffn_all, up_weight) + up_bias.astype(f32)
    act, slope = gelu_both(pre_act)
    act_low, pre_grad = lax.optimization_barrier(
        (act.astype(bf16), (act_grad * slope).astype(bf16))
    )
    order = Order()
    split = up_weight.shape[1] // 2
    up_half = lax.dynamic_slice(up_weight, (0, core * split), (width, split))
    down_half = lax.dynamic_slice(down_weight, (core * split, 0), (split, width))
    bias_half = lax.dynamic_slice(up_bias, (core * split,), (split,)).astype(f32)

    partial = matmul_nt(pre_grad, up_weight)
    order.mark(partial)
    ffn_in_grad = scatter_terms(partial)
    wide_grad = matmul_nt(order(branch_wide), down_half)
    order.mark(wide_grad)

    ffn_in_grad = sum(order(*ffn_in_grad))
    hidden_grad = grad_out + norm_back(ffn_in_grad * gain_two, normed_two, factor_two)
    attn_grad = (active * hidden_grad).astype(bf16)
    order.mark(attn_grad)
    attn_blocks = gather_blocks(attn_grad)
    branch = matmul(order(act_low), down_weight)
    order.mark(branch)

    attn_all = in_order(list(order(*attn_blocks)))
    context_grad = matmul_nt(attn_all, out_weight).astype(bf16).reshape(-1, heads, HD)
    probs = jnp.exp(scores_of(queries, keys) - logsum)
    probs_grad = jnp.einsum("qhd,khd->hqk", context_grad, values, preferred_element_type=f32)
    delta = jnp.sum(probs * probs_grad, -1, keepdims=True)
    score_grad = (probs * (probs_grad - delta)).astype(bf16)
    query_grad = jnp.einsum("hqk,khd->qhd", score_grad, keys, preferred_element_type=f32) * 0.125
    key_grad = jnp.einsum("hqk,qhd->khd", score_grad, queries, preferred_element_type=f32) * 0.125
    value_grad = jnp.einsum(
        "hqk,qhd->khd", probs.astype(bf16), context_grad, preferred_element_type=f32
    )
    qkv_grad = jnp.concatenate(
        [part.astype(bf16).reshape(-1, cols) for part in (query_grad, key_grad, value_grad)], 1
    )

    qkv_part = matmul_tn(attn_in, qkv_grad).astype(bf16).reshape(count, cols, 3 * cols)
    piece = lax.psum_scatter(qkv_part, "replica", scatter_dimension=1, tiled=True)
    in_part = matmul_nt(after(qkv_grad, qkv_part), qkv_weight)
    order.mark(in_part)
    in_grad = scatter_terms(in_part)
    out_part = matmul_tn(order(context), attn_all).astype(bf16)
    out_grad = lax.psum(out_part, "replica")
    order.mark(out_part)

    wide_act, wide_slope = gelu_both(matmul(order(ffn_wide), up_half) + bias_half)
    wide_act, wide_grad = lax.optimization_barrier(
        (wide_act.astype(bf16), (wide_grad * wide_slope).astype(bf16))
    )
    order.mark(wide_act, wide_grad)

    shared = jnp.stack(
        [
            jnp.sum(in_part * normed_all, 0),
            jnp.sum(in_part, 0),
            jnp.sum(ffn_in_grad * normed_two, 0),
            jnp.sum(ffn_in_grad, 0),
        ]
    )
    shared = reorder(shared.reshape(4, count, cols).transpose(1, 0, 2))
    shared = sum(exchange([shared[k] for k in range(count)]))
    qkv_bias_part = column_sums(qkv_grad)
    small = jnp.concatenate(
        [
            shared.reshape(-1),
            lax.dynamic_slice(column_sums(attn_all), (me * cols,), (cols,)),
            qkv_bias_part[:cols],
            qkv_bias_part[2 * cols :],
        ]
    )
    small = replica_sum_small(small)
    small_parts = [small[k * cols : (k + 1) * cols] for k in range(7)]

    normed_one, factor_one = layer_norm(tokens.astype(f32))
    in_grad = sum(order(*in_grad))
    token_grad = (hidden_grad + norm_back(in_grad * gain_one, normed_one, factor_one)).astype(bf16)
    order.mark(token_grad)

    down_grad = matmul_tn(order(wide_act), branch_wide).astype(bf16)
    order.mark(down_grad)
    piece = reorder(order(piece))
    piece = reorder(jnp.stack(exchange([piece[k] for k in range(count)])))
    piece = piece.reshape(count, -1, 3, cols).transpose(1, 2, 0, 3).reshape(-1, 3 * width)
    order.mark(piece)
    qkv_wgrad = lax.all_gather(piece, "replica", axis=0, tiled=True)
    up_grad = matmul_tn(order(ffn_wide), wide_grad).astype(bf16)
    order.mark(up_grad)
    down_grad = core_join(down_grad, 0).astype(f32)
    up_grad = core_join(up_grad, 1).astype(f32)
    up_bias_grad = core_join(column_sums(wide_grad), 0)
    down_bias_grad = lax.dynamic_slice(column_sums(branch_wide), (me * cols,), (cols,))

    branch = scatter_sum(branch) + dbias
    output = (hidden + active * branch).astype(bf16)
    qkv_wgrad = order(qkv_wgrad)
    out_grad = order(out_grad).astype(f32)
    return (
        output,
        token_grad,
        small_parts[0],
        small_parts[1],
        qkv_wgrad[:, :width].astype(f32),
        small_parts[5],
        qkv_wgrad[:, width : 2 * width].astype(f32),
        qkv_wgrad[:, 2 * width :].astype(f32),
        small_parts[6],
        out_grad,
        small_parts[4],
        small_parts[2],
        small_parts[3],
        up_grad,
        up_bias_grad,
        down_grad,
        down_bias_grad,
    )


def solution(mesh):
    both = P(("replica", "group"), None)
    vector, by_rows, by_cols = P("group"), P("group", None), P(None, "group")
    return jax.shard_map(
        shards,
        mesh=mesh,
        in_specs=(
            both,
            P("replica"),
            P(("replica", "group")),
            vector,
            vector,
            by_rows,
            vector,
            by_rows,
            by_rows,
            vector,
            by_rows,
            vector,
            vector,
            vector,
            by_cols,
            vector,
            by_rows,
            vector,
            both,
        ),
        out_specs=(
            both,
            both,
            vector,
            vector,
            by_rows,
            vector,
            by_rows,
            by_rows,
            vector,
            by_rows,
            vector,
            vector,
            vector,
            by_cols,
            vector,
            by_rows,
            vector,
        ),
        check_vma=False,
    )
```

time: 2690 us -> 607 us (0.23)
  waiting for transfers between devices: 2250 us -> 167 us
  blocking collectives: 116 us -> 0 us
  starting transfers between devices: 0.86 us -> 48.6 us
  other arithmetic: 50.9 us -> 95.2 us
  local copies, waits for them, and re-layouts: 39.5 us -> 80.3 us
    all_gather x8 -> x3, waiting for transfers between devices: 899 us -> 24 us  [the longest x1 24 us: shards(): qkv_wgrad = lax.all_gather(piece, 'replica', axis=0, tiled=True)]
    reduce_scatter x5 -> x1, waiting for transfers between devices: 610 us -> 0.01 us  [shards(): lax.psum_scatter(qkv_part, 'replica', scatter_dimension=1, tiled=True)]
    psum x1, waiting for transfers between devices: 398 us -> 0.01 us  [shards(): out_grad = lax.psum(out_part, 'replica')]
    unnamed x20 -> x5, waiting for transfers between devices: 346 us -> 0.08 us
    ppermute x0 -> x40, waiting for transfers between devices: none -> 142 us  [the longest x33 142 us: swap(): return lax.ppermute(block, 'group', [(i, i ^ step) for i in range(count)])]
    all_gather x9 -> x0, blocking collectives: 71.4 us -> none  [the longest x1 9.52 us: shards(): lax.all_gather(value_bias, 'group', axis=0, tiled=True)]
    ppermute x0 -> x40, starting transfers between devices: none -> 48 us  [the longest x33 43 us: swap(): return lax.ppermute(block, 'group', [(i, i ^ step) for i in range(count)])]
    psum x1 -> x0, blocking collectives: 28 us -> none  [shards(): lax.psum(pre_gain_grad.astype(jnp.bfloat16), 'replica').astype(jnp.float32)]
  transfers between devices with their start and end apart: 17 -> 45, of which waited for: 17 -> 16; matrix products, arithmetic and copies ran while one was open for 6% -> 58% of each run, Pallas kernels for 0% -> 0%
where the time goes in v1:
time: 607 us; the launch traced here: 596 us
  matrix products  189 us (31%)
  waiting for transfers between devices  167 us (28%)
  other arithmetic  95.2 us (16%)
  local copies, waits for them, and re-layouts  80.3 us (13%)
  starting transfers between devices  48.6 us (8%)
  between operations  16.2 us (3%)
    ppermute x33, waiting for transfers between devices, swap(): return lax.ppermute(block, 'group', [(i, i ^ step) for i in range(count)])  142 us
    dot_general x5, matrix products, matmul(): return jnp.dot(left, right, preferred_element_type=f32)  66.8 us
    dot_general x4, matrix products, matmul_tn(): lax.dot_general(left, right, (((0,), (0,)), ((), ())), preferred_element_...  60.3 us
    dot_general x5, matrix products, matmul_nt(): lax.dot_general(left, right, (((1,), (1,)), ((), ())), preferred_element_...  48.8 us
    ppermute x33, starting transfers between devices, swap(): return lax.ppermute(block, 'group', [(i, i ^ step) for i in range(count)])  43 us
    unnamed x105, local copies, waits for them, and re-layouts  27.7 us
    all_gather x1, waiting for transfers between devices, shards(): qkv_wgrad = lax.all_gather(piece, 'replica', axis=0, tiled=True)  24 us
    dynamic_update_slice x19, local copies, waits for them, and re-layouts, in_order(): whole = lax.dynamic_update_slice(whole, block, start)  15.2 us
  transfers between devices with their start and end apart: 45, of which 16 were waited for; matrix products, arithmetic and copies ran while one was open for 58% of the time, Pallas kernels for 0%

profile of v1, /device:TPU:0, one launch (start us, length us, event | category | flops | bytes accessed | tf_op | source)
XLA Modules:
  0.0 595.6 jit_solution(12875367554709756749)
XLA Ops:
  36.6 6.9 %collective-permute-done.1 = bf16[128,2048]{1,0:T(8,128)(2,1)} collective-permute-done((bf16[128,2048]{1,0:T(8,128)(2,1)}, bf16[128,2048]{1,0:T(8,128)(2,1)}, u32[]{:S(2)}, u32[]{:S(2)}) %collective-permute-start.1) | collective-permute-done | bytes 524320 | tf_op jit(solution)/shard_map/ppermute | solution.py:55
  49.2 42.6 %collective-permute-done.5 = bf16[258,1536]{1,0:T(8,128)(2,1)S(1)} collective-permute-done((bf16[258,1536]{1,0:T(8,128)(2,1)}, bf16[258,1536]{1,0:T(8,128)(2,1)S(1)}, u32[]{:S(2)}, u32[]{:S(2)}) %collective-permute-start.5) | collective-permute-done | bytes 792608 | tf_op jit(solution)/shard_map/ppermute | solution.py:55
  111.5 6.6 %fusion.28 = bf16[512,1536]{1,0:T(8,128)(2,1)S(1)} fusion(bf16[2048,1536]{1,0:T(8,128)(2,1)S(1)} %bitcast.151, f32[1536]{0:T(1024)S(1)} %maximum_convert_fusion.2, bf16[512,2048]{1,0:T(8,128)(2,1)} %constant_dynamic-update-slice_fusion.17, f32[2048]{0:T(1024)S(1)} %bitcast.191, f32[2048]{0:T(1024)S(1)} %bitcast.184, f32[512]{0:T(512)S(1)} %add_rsqrt_fusion, ...), kind=kOutput, calls=%fused_computation.56 | convolution fusion | flops 3229089792 | bytes 9988096 | tf_op jit(solution)/shard_map/dot_general | solution.py:38
  132.5 10.3 %collective-permute-done.9 = bf16[128,2048]{1,0:T(8,128)(2,1)} collective-permute-done((bf16[128,2048]{1,0:T(8,128)(2,1)}, bf16[128,2048]{1,0:T(8,128)(2,1)}, u32[]{:S(2)}, u32[]{:S(2)}) %collective-permute-start.9) | collective-permute-done | bytes 524320 | tf_op jit(solution)/shard_map/ppermute | solution.py:55
  148.6 17.2 %collective-permute-done.12 = bf16[128,2048]{1,0:T(8,128)(2,1)S(1)} collective-permute-done((bf16[128,2048]{1,0:T(8,128)(2,1)S(1)}, bf16[128,2048]{1,0:T(8,128)(2,1)S(1)}, u32[]{:S(2)}, u32[]{:S(2)}) %collective-permute-start.12) | collective-permute-done | bytes 524320 | tf_op jit(solution)/shard_map/ppermute | solution.py:55
  165.8 12.0 %collective-permute-done.11 = bf16[128,2048]{1,0:T(8,128)(2,1)S(1)} collective-permute-done((bf16[128,2048]{1,0:T(8,128)(2,1)S(1)}, bf16[128,2048]{1,0:T(8,128)(2,1)S(1)}, u32[]{:S(2)}, u32[]{:S(2)}) %collective-permute-start.11) | collective-permute-done | bytes 524320 | tf_op jit(solution)/shard_map/ppermute | solution.py:55
  190.1 8.2 %collective-permute-done.13 = bf16[128,2048]{1,0:T(8,128)(2,1)S(1)} collective-permute-done((bf16[128,2048]{1,0:T(8,128)(2,1)}, bf16[128,2048]{1,0:T(8,128)(2,1)S(1)}, u32[]{:S(2)}, u32[]{:S(2)}) %collective-permute-start.13) | collective-permute-done | bytes 524320 | tf_op jit(solution)/shard_map/ppermute | solution.py:55
  199.1 12.6 %collective-permute-done.14 = bf16[128,2048]{1,0:T(8,128)(2,1)S(1)} collective-permute-done((bf16[128,2048]{1,0:T(8,128)(2,1)S(1)}, bf16[128,2048]{1,0:T(8,128)(2,1)S(1)}, u32[]{:S(2)}, u32[]{:S(2)}) %collective-permute-start.14) | collective-permute-done | bytes 524320 | tf_op jit(solution)/shard_map/ppermute | solution.py:55
  213.4 12.2 %multiply_convert_fusion.2 = (bf16[512,2048]{1,0:T(8,128)(2,1)}, f32[512,2048]{1,0:T(8,128)}) fusion(f32[2048]{0:T(1024)S(1)} %convert_element_type.238, bf16[512,2048]{1,0:T(8,128)(2,1)} %constant_dynamic-update-slice_fusion.8, bf16[2048,2048]{1,0:T(8,128)(2,1)} %param.33), kind=kOutput, calls=%fused_computation.46 | convolution fusion | flops 4305453056 | bytes 16785408 | tf_op jit(solution)/shard_map/dot_general | solution.py:38
  225.6 9.0 %fusion.23 = bf16[512,2048]{1,0:T(8,128)(2,1)S(1)} fusion(f32[512,2048]{1,0:T(8,128)} %get-tuple-element.206, bf16[512,2048]{1,0:T(8,128)(2,1)S(1)} %constant_dynamic-update-slice_fusion.4, bf16[2048,2048]{1,0:T(8,128)(2,1)S(1)} %bitcast.196, f32[2048]{0:T(1024)S(1)} %convert_element_type.238), kind=kOutput, calls=%fused_computation.40 | convolution fusion | flops 4315938816 | bytes 16785408 | tf_op jit(solution)/shard_map/dot_general | solution.py:42
  234.6 7.2 %fusion.70 = f32[512,2048]{1,0:T(8,128)S(1)} fusion(bf16[512,2048]{1,0:T(8,128)(2,1)S(1)} %fusion.23, bf16[2048,2048]{1,0:T(8,128)(2,1)} %param.33), kind=kOutput, calls=%fused_computation.207 | convolution fusion | flops 4294967296 | bytes 14680064 | tf_op jit(solution)/shard_map/dot_general | solution.py:42
  251.0 9.4 %collective-permute-done.16 = bf16[128,2048]{1,0:T(8,128)(2,1)} collective-permute-done((bf16[128,2048]{1,0:T(8,128)(2,1)}, bf16[128,2048]{1,0:T(8,128)(2,1)}, u32[]{:S(2)}, u32[]{:S(2)}) %collective-permute-start.16) | collective-permute-done | bytes 524320 | tf_op jit(solution)/shard_map/ppermute | solution.py:55
  262.7 3.9 collective-permute-done.17
  268.7 8.2 %collective-permute-done.18 = bf16[128,2048]{1,0:T(8,128)(2,1)} collective-permute-done((bf16[128,2048]{1,0:T(8,128)(2,1)}, bf16[128,2048]{1,0:T(8,128)(2,1)}, u32[]{:S(2)}, u32[]{:S(2)}) %collective-permute-start.18) | collective-permute-done | bytes 524320 | tf_op jit(solution)/shard_map/ppermute | solution.py:55
  279.0 23.8 %fusion.26 = f32[4096,1024]{1,0:T(8,128)} fusion(bf16[4096,2048]{1,0:T(8,128)(2,1)} %all-gather.4.cloned.1.call-done, bf16[2048,2048]{1,0:T(8,128)(2,1)} %param.35, s32[]{:T(128)S(6)} %select_n.218), kind=kOutput, calls=%fused_computation.44 | convolution fusion | flops 17179869184 | bytes 37748740 | tf_op jit(solution)/shard_map/dot_general | solution.py:42
  305.4 4.1 collective-permute-start.23
  309.5 9.9 %fusion.71 = f32[512,2048]{1,0:T(8,128)} fusion(bf16[512,2048]{1,0:T(8,128)(2,1)S(1)} %copy-done.42, bf16[2048,2048]{1,0:T(8,128)(2,1)} %param.35), kind=kOutput, calls=%fused_computation.208 | convolution fusion | flops 4294967296 | bytes 14680064 | tf_op jit(solution)/shard_map/dot_general | solution.py:38
  334.7 8.9 %convolution_convert_fusion = bf16[2048,1536]{1,0:T(8,128)(2,1)} fusion(bf16[512,1536]{0,1:T(8,128)(2,1)S(1)} %get-tuple-element.59, bf16[512,2048]{1,0:T(8,128)(2,1)} %constant_dynamic-update-slice_fusion.17, f32[2048]{0:T(1024)S(1)} %bitcast.192, f32[2048]{0:T(1024)S(1)} %bitcast.185, f32[512]{0:T(512)S(1)} %add_rsqrt_fusion, ...), kind=kOutput, calls=%fused_computation.19 | convolution fusion | flops 3230662656 | bytes 9981952 | tf_op jit(solution)/shard_map/dot_general | solution.py:46
  345.0 7.5 %fusion.15 = (f32[2048]{0:T(1024)S(1)}, f32[2048]{0:T(1024)S(1)}, f32[512,2048]{1,0:T(8,128)S(1)}) fusion(bf16[512,2048]{1,0:T(8,128)(2,1)} %constant_dynamic-update-slice_fusion.17, f32[512]{0:T(512)S(1)} %add_rsqrt_fusion, f32[512]{0:T(512)S(1)} %broadcast_multiply_fusion, bf16[512,1536]{0,1:T(8,128)(2,1)S(1)} %copy-done.31, bf16[2048,1536]{1,0:T(8,128)(2,1)} %bitcast.152), kind=kOutput, calls=%fused_computation.32 | convolution fusion | flops 3227512832 | bytes 14176256 | tf_op jit(solution)/shard_map/dot_general | solution.py:42
  372.8 36.8 %fusion.6 = (bf16[4096,1024]{1,0:T(8,128)(2,1)}, bf16[4096,1024]{1,0:T(8,128)(2,1)}) fusion(f32[4096,1024]{1,0:T(8,128)} %fusion.26, f32[1024]{0:T(1024)S(1)} %dynamic-slice_convert_fusion.12, bf16[4096,2048]{1,0:T(8,128)(2,1)} %all-gather.6.cloned.1.call-done, bf16[2048,2048]{1,0:T(8,128)(2,1)} %param.33, s32[]{:T(128)S(6)} %select_n.218), kind=kOutput, calls=%fused_computation.9 | convolution fusion | flops 17272143872 | bytes 54530052 | tf_op jit(solution)/shard_map/dot_general | solution.py:38
  412.1 24.1 %convolution_convert_fusion.2 = bf16[1024,2048]{1,0:T(8,128)(2,1)} fusion(bf16[4096,1024]{1,0:T(8,128)(2,1)} %get-tuple-element.68, bf16[4096,2048]{1,0:T(8,128)(2,1)} %all-gather.4.cloned.1.call-done), kind=kOutput, calls=%fused_computation.52 | convolution fusion | flops 17181966336 | bytes 29360128 | tf_op jit(solution)/shard_map/dot_general | solution.py:46
  438.0 3.9 collective-permute-start.36
  458.8 24.7 %convolution_convert_fusion.1 = bf16[2048,1024]{0,1:T(8,128)(2,1)} fusion(bf16[4096,2048]{1,0:T(8,128)(2,1)} %all-gather.6.cloned.1.call-done, bf16[4096,1024]{1,0:T(8,128)(2,1)} %get-tuple-element.63), kind=kOutput, calls=%fused_computation.51 | convolution fusion | flops 17181966336 | bytes 29360128 | tf_op jit(solution)/shard_map/dot_general | solution.py:46
  483.7 7.7 %convert_reduce_fusion = f32[2048]{0:T(1024)S(1)} fusion(bf16[4096,2048]{1,0:T(8,128)(2,1)} %all-gather.4.cloned.1.call-done), kind=kLoop, calls=%fused_computation | loop fusion | flops 16775168 | bytes 16785408 | tf_op jit(solution)/shard_map/reduce_sum | solution.py:50
  500.5 3.9 broadcast_select_fusion.1
  504.4 11.9 %maximum_convert_fusion.1 = f32[2048,2048]{1,0:T(8,128)} fusion(bf16[1024,2048]{1,0:T(8,128)(2,1)} %get-tuple-element.145, bf16[1024,2048]{1,0:T(8,128)(2,1)} %get-tuple-element.144), kind=kLoop, calls=%fused_computation.13 | loop fusion | flops 16777216 | bytes 25165824 | tf_op jit(solution)/shard_map/convert_element_type | solution.py:342
  516.3 4.1 convert_element_type.282
  520.5 6.9 %broadcast_select_fusion.3 = (bf16[2048,1024]{0,1:T(8,128)(2,1)}, bf16[2048,1024]{0,1:T(8,128)(2,1)}) fusion(bf16[2048,1024]{0,1:T(8,128)(2,1)} %convolution_convert_fusion.1, bf16[2048,1024]{0,1:T(8,128)(2,1)} %collective-permute-done.37, pred[]{:T(512)S(6)} %eq.7), kind=kLoop, calls=%fused_computation.50 | loop fusion | flops 4194304 | bytes 16777216 | tf_op jit(solution)/shard_map/jit(_where)/select_n | solution.py:125
  527.3 11.5 %maximum_convert_fusion = f32[2048,2048]{0,1:T(8,128)} fusion(bf16[2048,1024]{0,1:T(8,128)(2,1)} %get-tuple-element.147, bf16[2048,1024]{0,1:T(8,128)(2,1)} %get-tuple-element.146), kind=kLoop, calls=%fused_computation.12 | loop fusion | flops 16777216 | bytes 25165824 | tf_op jit(solution)/shard_map/convert_element_type | solution.py:343
  538.8 17.7 %copy.63 = f32[2048,2048]{1,0:T(8,128)} copy(f32[2048,2048]{0,1:T(8,128)} %maximum_convert_fusion) | data formatting | bytes 33554432
  556.5 24.0 %all-gather.8.cloned.1.call-done = bf16[512,6144]{1,0:T(8,128)(2,1)} async-done(((bf16[64,6144]{1,0:T(8,128)(2,1)}), bf16[512,6144]{1,0:T(8,128)(2,1)}) %all-gather.8.cloned.1.call-update) | async-done | bytes 6291472 | tf_op jit(solution)/shard_map/all_gather | solution.py:339
  580.4 8.2 %slice_convert_fusion = (f32[512,2048]{1,0:T(8,128)}, f32[512,2048]{1,0:T(8,128)}, f32[512,2048]{1,0:T(8,128)}) fusion(bf16[512,6144]{1,0:T(8,128)(2,1)} %all-gather.8.cloned.1.call-done), kind=kLoop, calls=%fused_computation.58 | loop fusion | flops 3145728 | bytes 18874368 | tf_op jit(solution)/shard_map/convert_element_type | solution.py:359
  (320 shorter events, 173.7 us)
Async XLA Ops:
  7.2 271.8 %all-gather.4.cloned.1.call-start = ((), (), s32[]{:S(2)}) async-start(), calls=%async_computation.1 | async-start | bytes 17301504 | tf_op jit(solution)/shard_map/all_gather | solution.py:220
  10.7 362.1 %all-gather.6.cloned.1.call-start = ((), (), s32[]{:S(2)}) async-start(), calls=%async_computation.2 | async-start | bytes 17301504 | tf_op jit(solution)/shard_map/all_gather | solution.py:250
  10.8 23.8 %collective-permute-start = (bf16[128,2048]{1,0:T(8,128)(2,1)}, bf16[128,2048]{1,0:T(8,128)(2,1)}, u32[]{:S(2)}, u32[]{:S(2)}) collective-permute-start(bf16[128,2048]{1,0:T(8,128)(2,1)} %param.19), channel_id=1, source_target_pairs={{0,1},{1,0},{2,3},{3,2},{4,5},{5,4},{6,7},{7,6},{8,9},{9,8},{10,11... | collective-permute-start | bytes 1572872 | tf_op jit(solution)/shard_map/ppermute | solution.py:55
  13.8 29.6 %collective-permute-start.1 = (bf16[128,2048]{1,0:T(8,128)(2,1)}, bf16[128,2048]{1,0:T(8,128)(2,1)}, u32[]{:S(2)}, u32[]{:S(2)}) collective-permute-start(bf16[128,2048]{1,0:T(8,128)(2,1)} %param.19), channel_id=1, source_target_pairs={{0,2},{1,3},{2,0},{3,1},{4,6},{5,7},{6,4},{7,5},{8,10},{9,11},{10,... | collective-permute-start | bytes 1572872 | tf_op jit(solution)/shard_map/ppermute | solution.py:55
  15.3 30.0 %collective-permute-start.2 = (bf16[128,2048]{1,0:T(8,128)(2,1)}, bf16[128,2048]{1,0:T(8,128)(2,1)}, u32[]{:S(2)}, u32[]{:S(2)}) collective-permute-start(bf16[128,2048]{1,0:T(8,128)(2,1)} %param.19), channel_id=1, source_target_pairs={{0,3},{1,2},{2,1},{3,0},{4,7},{5,6},{6,5},{7,4},{8,11},{9,10},{10,... | collective-permute-start | bytes 1572872 | tf_op jit(solution)/shard_map/ppermute | solution.py:55
  24.8 68.5 %collective-permute-start.3 = (bf16[258,1536]{1,0:T(8,128)(2,1)}, bf16[258,1536]{1,0:T(8,128)(2,1)}, u32[]{:S(2)}, u32[]{:S(2)}) collective-permute-start(bf16[258,1536]{1,0:T(8,128)(2,1)} %get-tuple-element.202), channel_id=1, source_target_pairs={{0,1},{1,0},{2,3},{3,2},{4,5},{5,4},{6,7},{7,6},{8,9},{9,8},{10,11... | collective-permute-start | bytes 2377736 | tf_op jit(solution)/shard_map/ppermute | solution.py:55
  26.7 65.2 %collective-permute-start.4 = (bf16[258,1536]{1,0:T(8,128)(2,1)}, bf16[258,1536]{1,0:T(8,128)(2,1)}, u32[]{:S(2)}, u32[]{:S(2)}) collective-permute-start(bf16[258,1536]{1,0:T(8,128)(2,1)} %get-tuple-element.201), channel_id=1, source_target_pairs={{0,2},{1,3},{2,0},{3,1},{4,6},{5,7},{6,4},{7,5},{8,10},{9,11},{10,... | collective-permute-start | bytes 2377736 | tf_op jit(solution)/shard_map/ppermute | solution.py:55
  34.6 57.2 %collective-permute-start.5 = (bf16[258,1536]{1,0:T(8,128)(2,1)}, bf16[258,1536]{1,0:T(8,128)(2,1)S(1)}, u32[]{:S(2)}, u32[]{:S(2)}) collective-permute-start(bf16[258,1536]{1,0:T(8,128)(2,1)} %get-tuple-element.200), channel_id=1, source_target_pairs={{0,3},{1,2},{2,1},{3,0},{4,7},{5,6},{6,5},{7,4},{8,11},{9,10},{10,... | collective-permute-start | bytes 2377736 | tf_op jit(solution)/shard_map/ppermute | solution.py:55
  98.4 34.1 %collective-permute-start.7 = (bf16[128,2048]{1,0:T(8,128)(2,1)}, bf16[128,2048]{1,0:T(8,128)(2,1)}, u32[]{:S(2)}, u32[]{:S(2)}) collective-permute-start(bf16[128,2048]{1,0:T(8,128)(2,1)} %fusion.41), channel_id=1, source_target_pairs={{0,1},{1,0},{2,3},{3,2},{4,5},{5,4},{6,7},{7,6},{8,9},{9,8},{10,11... | collective-permute-start | bytes 1572872 | tf_op jit(solution)/shard_map/ppermute | solution.py:55
  100.0 32.5 %collective-permute-start.8 = (bf16[128,2048]{1,0:T(8,128)(2,1)}, bf16[128,2048]{1,0:T(8,128)(2,1)}, u32[]{:S(2)}, u32[]{:S(2)}) collective-permute-start(bf16[128,2048]{1,0:T(8,128)(2,1)} %fusion.41), channel_id=1, source_target_pairs={{0,2},{1,3},{2,0},{3,1},{4,6},{5,7},{6,4},{7,5},{8,10},{9,11},{10,... | collective-permute-start | bytes 1572872 | tf_op jit(solution)/shard_map/ppermute | solution.py:55
  100.5 42.4 %collective-permute-start.9 = (bf16[128,2048]{1,0:T(8,128)(2,1)}, bf16[128,2048]{1,0:T(8,128)(2,1)}, u32[]{:S(2)}, u32[]{:S(2)}) collective-permute-start(bf16[128,2048]{1,0:T(8,128)(2,1)} %fusion.41), channel_id=1, source_target_pairs={{0,3},{1,2},{2,1},{3,0},{4,7},{5,6},{6,5},{7,4},{8,11},{9,10},{10,... | collective-permute-start | bytes 1572872 | tf_op jit(solution)/shard_map/ppermute | solution.py:55
  144.4 21.4 %collective-permute-start.12 = (bf16[128,2048]{1,0:T(8,128)(2,1)S(1)}, bf16[128,2048]{1,0:T(8,128)(2,1)S(1)}, u32[]{:S(2)}, u32[]{:S(2)}) collective-permute-start(bf16[128,2048]{1,0:T(8,128)(2,1)S(1)} %get-tuple-element.161), channel_id=1, source_target_pairs={{0,3},{1,2},{2,1},{3,0},{4,7},{5,6},{6,5},{7,4},{8,11},{9,10},{10,... | collective-permute-start | bytes 1572872 | tf_op jit(solution)/shard_map/ppermute | solution.py:55
  147.8 30.0 %collective-permute-start.11 = (bf16[128,2048]{1,0:T(8,128)(2,1)S(1)}, bf16[128,2048]{1,0:T(8,128)(2,1)S(1)}, u32[]{:S(2)}, u32[]{:S(2)}) collective-permute-start(bf16[128,2048]{1,0:T(8,128)(2,1)S(1)} %get-tuple-element.162), channel_id=1, source_target_pairs={{0,2},{1,3},{2,0},{3,1},{4,6},{5,7},{6,4},{7,5},{8,10},{9,11},{10,... | collective-permute-start | bytes 1572872 | tf_op jit(solution)/shard_map/ppermute | solution.py:55
  147.8 30.0 %collective-permute-start.10 = (bf16[128,2048]{1,0:T(8,128)(2,1)S(1)}, bf16[128,2048]{1,0:T(8,128)(2,1)S(1)}, u32[]{:S(2)}, u32[]{:S(2)}) collective-permute-start(bf16[128,2048]{1,0:T(8,128)(2,1)S(1)} %get-tuple-element.160), channel_id=1, source_target_pairs={{0,1},{1,0},{2,3},{3,2},{4,5},{5,4},{6,7},{7,6},{8,9},{9,8},{10,11... | collective-permute-start | bytes 1572872 | tf_op jit(solution)/shard_map/ppermute | solution.py:55
  181.6 254.6 %reduce-scatter.2.cloned.1.call-start = ((), (), s32[]{:S(2)}) async-start(), calls=%async_computation.3 | async-start | bytes 7077888 | tf_op jit(solution)/shard_map/reduce_scatter | solution.py:292
  184.7 27.0 %collective-permute-start.14 = (bf16[128,2048]{1,0:T(8,128)(2,1)S(1)}, bf16[128,2048]{1,0:T(8,128)(2,1)S(1)}, u32[]{:S(2)}, u32[]{:S(2)}) collective-permute-start(bf16[128,2048]{1,0:T(8,128)(2,1)S(1)} %copy-done.27), channel_id=1, source_target_pairs={{0,2},{1,3},{2,0},{3,1},{4,6},{5,7},{6,4},{7,5},{8,10},{9,11},{10,... | collective-permute-start | bytes 1572872 | tf_op jit(solution)/shard_map/ppermute | solution.py:55
  186.3 26.3 %collective-permute-start.15 = (bf16[128,2048]{1,0:T(8,128)(2,1)S(1)}, bf16[128,2048]{1,0:T(8,128)(2,1)S(1)}, u32[]{:S(2)}, u32[]{:S(2)}) collective-permute-start(bf16[128,2048]{1,0:T(8,128)(2,1)S(1)} %copy-done.27), channel_id=1, source_target_pairs={{0,3},{1,2},{2,1},{3,0},{4,7},{5,6},{6,5},{7,4},{8,11},{9,10},{10,... | collective-permute-start | bytes 1572872 | tf_op jit(solution)/shard_map/ppermute | solution.py:55
  245.0 15.3 %collective-permute-start.16 = (bf16[128,2048]{1,0:T(8,128)(2,1)}, bf16[128,2048]{1,0:T(8,128)(2,1)}, u32[]{:S(2)}, u32[]{:S(2)}) collective-permute-start(bf16[128,2048]{1,0:T(8,128)(2,1)} %get-tuple-element.159), channel_id=1, source_target_pairs={{0,1},{1,0},{2,3},{3,2},{4,5},{5,4},{6,7},{7,6},{8,9},{9,8},{10,11... | collective-permute-start | bytes 1572872 | tf_op jit(solution)/shard_map/ppermute | solution.py:55
  247.2 19.3 %collective-permute-start.17 = (bf16[128,2048]{1,0:T(8,128)(2,1)}, bf16[128,2048]{1,0:T(8,128)(2,1)}, u32[]{:S(2)}, u32[]{:S(2)}) collective-permute-start(bf16[128,2048]{1,0:T(8,128)(2,1)} %get-tuple-element.158), channel_id=1, source_target_pairs={{0,2},{1,3},{2,0},{3,1},{4,6},{5,7},{6,4},{7,5},{8,10},{9,11},{10,... | collective-permute-start | bytes 1572872 | tf_op jit(solution)/shard_map/ppermute | solution.py:55
  247.2 29.7 %collective-permute-start.18 = (bf16[128,2048]{1,0:T(8,128)(2,1)}, bf16[128,2048]{1,0:T(8,128)(2,1)}, u32[]{:S(2)}, u32[]{:S(2)}) collective-permute-start(bf16[128,2048]{1,0:T(8,128)(2,1)} %get-tuple-element.157), channel_id=1, source_target_pairs={{0,3},{1,2},{2,1},{3,0},{4,7},{5,6},{6,5},{7,4},{8,11},{9,10},{10,... | collective-permute-start | bytes 1572872 | tf_op jit(solution)/shard_map/ppermute | solution.py:55
  305.4 16.8 %collective-permute-start.23 = (bf16[128,2048]{1,0:T(8,128)(2,1)S(1)}, bf16[128,2048]{1,0:T(8,128)(2,1)S(1)}, u32[]{:S(2)}, u32[]{:S(2)}) collective-permute-start(bf16[128,2048]{1,0:T(8,128)(2,1)S(1)} %get-tuple-element.55), channel_id=1, source_target_pairs={{0,2},{1,3},{2,0},{3,1},{4,6},{5,7},{6,4},{7,5},{8,10},{9,11},{10,... | collective-permute-start | bytes 1572872 | tf_op jit(solution)/shard_map/ppermute | solution.py:55
  343.6 172.7 %all-reduce.2.cloned.1.call-start = ((), (), s32[]{:S(2)}) async-start(), calls=%async_computation.5 | async-start | bytes 4194304 | tf_op jit(solution)/shard_map/psum | solution.py:297
  357.8 84.1 %collective-permute-start.30 = (f32[4,512]{1,0:T(4,128)S(1)}, f32[4,512]{1,0:T(4,128)S(1)}, u32[]{:S(2)}, u32[]{:S(2)}) collective-permute-start(f32[4,512]{1,0:T(4,128)S(1)} %get-tuple-element.187), channel_id=1, source_target_pairs={{0,3},{1,2},{2,1},{3,0},{4,7},{5,6},{6,5},{7,4},{8,11},{9,10},{10,... | collective-permute-start | bytes 24584 | tf_op jit(solution)/shard_map/ppermute | solution.py:55
  359.3 83.2 %collective-permute-start.29 = (f32[4,512]{1,0:T(4,128)S(1)}, f32[4,512]{1,0:T(4,128)S(1)}, u32[]{:S(2)}, u32[]{:S(2)}) collective-permute-start(f32[4,512]{1,0:T(4,128)S(1)} %get-tuple-element.188), channel_id=1, source_target_pairs={{0,2},{1,3},{2,0},{3,1},{4,6},{5,7},{6,4},{7,5},{8,10},{9,11},{10,... | collective-permute-start | bytes 24584 | tf_op jit(solution)/shard_map/ppermute | solution.py:55
  363.4 79.1 %collective-permute-start.28 = (f32[4,512]{1,0:T(4,128)S(1)}, f32[4,512]{1,0:T(4,128)S(1)}, u32[]{:S(2)}, u32[]{:S(2)}) collective-permute-start(f32[4,512]{1,0:T(4,128)S(1)} %get-tuple-element.186), channel_id=1, source_target_pairs={{0,1},{1,0},{2,3},{3,2},{4,5},{5,4},{6,7},{7,6},{8,9},{9,8},{10,11... | collective-permute-start | bytes 24584 | tf_op jit(solution)/shard_map/ppermute | solution.py:55
  442.5 137.9 %all-gather.8.cloned.1.call-start = ((), (), s32[]{:S(2)}) async-start(), calls=%async_computation.4 | async-start | bytes 7077888 | tf_op jit(solution)/shard_map/all_gather | solution.py:339
  453.3 38.7 %collective-permute-start.21 = (bf16[128,2048]{1,0:T(8,128)(2,1)S(1)}, bf16[128,2048]{1,0:T(8,128)(2,1)S(1)}, u32[]{:S(2)}, u32[]{:S(2)}) collective-permute-start(bf16[128,2048]{1,0:T(8,128)(2,1)S(1)} %get-tuple-element.155), channel_id=1, source_target_pairs={{0,3},{1,2},{2,1},{3,0},{4,7},{5,6},{6,5},{7,4},{8,11},{9,10},{10,... | collective-permute-start | bytes 1572872 | tf_op jit(solution)/shard_map/ppermute | solution.py:55
  455.5 39.5 %collective-permute-start.20 = (bf16[128,2048]{1,0:T(8,128)(2,1)S(1)}, bf16[128,2048]{1,0:T(8,128)(2,1)S(1)}, u32[]{:S(2)}, u32[]{:S(2)}) collective-permute-start(bf16[128,2048]{1,0:T(8,128)(2,1)S(1)} %get-tuple-element.156), channel_id=1, source_target_pairs={{0,2},{1,3},{2,0},{3,1},{4,6},{5,7},{6,4},{7,5},{8,10},{9,11},{10,... | collective-permute-start | bytes 1572872 | tf_op jit(solution)/shard_map/ppermute | solution.py:55
  456.9 38.1 %collective-permute-start.19 = (bf16[128,2048]{1,0:T(8,128)(2,1)S(1)}, bf16[128,2048]{1,0:T(8,128)(2,1)S(1)}, u32[]{:S(2)}, u32[]{:S(2)}) collective-permute-start(bf16[128,2048]{1,0:T(8,128)(2,1)S(1)} %get-tuple-element.154), channel_id=1, source_target_pairs={{0,1},{1,0},{2,3},{3,2},{4,5},{5,4},{6,7},{7,6},{8,9},{9,8},{10,11... | collective-permute-start | bytes 1572872 | tf_op jit(solution)/shard_map/ppermute | solution.py:55
  456.9 26.7 %collective-permute-start.32 = (f32[3584]{0:T(1024)S(1)}, f32[3584]{0:T(1024)S(1)}, u32[]{:S(2)}, u32[]{:S(2)}) collective-permute-start(f32[3584]{0:T(1024)S(1)} %fusion.54), channel_id=1, source_target_pairs={{0,8},{4,12},{8,0},{12,4},{16,24},{20,28},{24,16},{28,20},{1,9},{5... | collective-permute-start | bytes 43016 | tf_op jit(solution)/shard_map/ppermute | solution.py:146
  458.8 41.7 %collective-permute-start.39 = (bf16[1024,2048]{1,0:T(8,128)(2,1)}, bf16[1024,2048]{1,0:T(8,128)(2,1)S(1)}, u32[]{:S(2)}, u32[]{:S(2)}) collective-permute-start(bf16[1024,2048]{1,0:T(8,128)(2,1)} %convolution_convert_fusion.2), channel_id=1, source_target_pairs={{0,4},{4,0},{8,12},{12,8},{16,20},{20,16},{24,28},{28,24},{1,5},{5... | collective-permute-start | bytes 12582920 | tf_op jit(solution)/shard_map/ppermute | solution.py:119
  483.6 36.9 %collective-permute-start.37 = (bf16[2048,1024]{0,1:T(8,128)(2,1)}, bf16[2048,1024]{0,1:T(8,128)(2,1)}, u32[]{:S(2)}, u32[]{:S(2)}) collective-permute-start(bf16[2048,1024]{0,1:T(8,128)(2,1)} %convolution_convert_fusion.1), channel_id=1, source_target_pairs={{0,4},{4,0},{8,12},{12,8},{16,20},{20,16},{24,28},{28,24},{1,5},{5... | collective-permute-start | bytes 12582920 | tf_op jit(solution)/shard_map/ppermute | solution.py:119
  (62 other events, 1304.4 us)
Sparse Core Ops, SparseCore 0:
  10.9 183.8 all-gather.3
  198.3 122.1 all-gather.5
  343.7 71.6 reduce-scatter.1
  442.7 71.7 all-reduce.1
  515.9 64.4 all-gather.7

commit v2 on v1

--- a/solution.py
+++ b/solution.py
@@ -1,10 +1,15 @@
+import functools
+
 import jax
 import jax.numpy as jnp
 from jax import lax
+from jax.experimental import pallas as pl
+from jax.experimental.pallas import tpu as pltpu
 from jax.sharding import PartitionSpec as P
 
 HD = 64
 LAYER = 12
+QB = 128
 
 bf16 = jnp.bfloat16
 f32 = jnp.float32
@@ -25,25 +30,149 @@
     )
 
 
-def gelu_both(values):
-    inner = 0.7978845608 * (values + 0.044715 * values * values * values)
-    tangent = jnp.tanh(inner)
-    slope = 0.5 * (1.0 + tangent) + 0.5 * values * (1.0 - tangent * tangent) * 0.7978845608 * (
-        1.0 + 3.0 * 0.044715 * values * values
-    )
-    return 0.5 * values * (1.0 + tangent), slope
+def params(mb=56):
+    return pltpu.CompilerParams(vmem_limit_bytes=mb << 20)
+
+def nt(left, right):
+    return lax.dot_general(left, right, (((1,), (1,)), ((), ())), preferred_element_type=f32)
+def tn(left, right):
+    return lax.dot_general(left, right, (((0,), (0,)), ((), ())), preferred_element_type=f32)
+
+def later(keys, first):
+    key = lax.broadcasted_iota(jnp.int32, (keys, QB), 0)
+    query = lax.broadcasted_iota(jnp.int32, (keys, QB), 1) + first
+    return key <= query
+
+def attend_body(q_ref, k_ref, v_ref, out_ref):
+    rows = q_ref.shape[0]
+    for first in range(0, rows, QB):
+        keys = first + QB
+        parts = []
+        for lane in range(0, q_ref.shape[1], HD):
+            at = slice(lane, lane + HD)
+            query = q_ref[first:keys, at] * 0.125
+            scores = jnp.where(later(keys, first), nt(k_ref[:keys, at], query), -1e30)
+            grown = jnp.exp(scores - jnp.max(scores, 0, keepdims=True))
+            probs = grown * (1.0 / jnp.sum(grown, 0, keepdims=True))
+            parts.append(tn(probs.astype(bf16), v_ref[:keys, at]))
+        out_ref[first:keys, :] = jnp.concatenate(parts, 1).astype(bf16)
+
+def attend_back_body(q_ref, k_ref, v_ref, g_ref, dq_ref, dk_ref, dv_ref, key_acc, value_acc):
+    rows = q_ref.shape[0]
+    key_acc[...] = jnp.zeros_like(key_acc)
+    value_acc[...] = jnp.zeros_like(value_acc)
+    for first in range(0, rows, QB):
+        keys = first + QB
+        q_parts, k_parts, v_parts = [], [], []
+        for lane in range(0, q_ref.shape[1], HD):
+            at = slice(lane, lane + HD)
+            query = q_ref[first:keys, at] * 0.125
+            grad = g_ref[first:keys, at]
+            key = k_ref[:keys, at]
+            scores = jnp.where(later(keys, first), nt(key, query), -1e30)
+            grown = jnp.exp(scores - jnp.max(scores, 0, keepdims=True))
+            probs = grown * (1.0 / jnp.sum(grown, 0, keepdims=True))
+            probs_grad = nt(v_ref[:keys, at], grad)
+            delta = jnp.sum(probs * probs_grad, 0, keepdims=True)
+            score_grad = (probs * (probs_grad - delta)).astype(bf16)
+            v_parts.append(jnp.dot(probs.astype(bf16), grad, preferred_element_type=f32))
+            k_parts.append(jnp.dot(score_grad, query, preferred_element_type=f32))
+            q_parts.append(tn(score_grad, key) * 0.125)
+        dq_ref[first:keys, :] = jnp.concatenate(q_parts, 1).astype(bf16)
+        key_acc[:keys, :] += jnp.concatenate(k_parts, 1)
+        value_acc[:keys, :] += jnp.concatenate(v_parts, 1)
+    dk_ref[...] = key_acc[...].astype(bf16)
+    dv_ref[...] = value_acc[...].astype(bf16)
+
+def attention(qkv):
+    rows, cols = qkv.shape[0], qkv.shape[1] // 3
+    lanes = 2 * HD
+    pairs = cols // lanes
+    spec = lambda part: pl.BlockSpec((rows, lanes), lambda h: (0, part * pairs + h))
+    work = 2 * rows * rows * cols
+    return pl.pallas_call(
+        attend_body, grid=(pairs,), in_specs=[spec(0), spec(1), spec(2)], out_specs=spec(0),
+        out_shape=jax.ShapeDtypeStruct((rows, cols), bf16), compiler_params=params(),
+        cost_estimate=pl.CostEstimate(flops=2 * work, bytes_accessed=8 * rows * cols, transcendentals=rows * rows * cols // HD),
+    )(qkv, qkv, qkv)
+
+def attention_back(qkv, grad):
+    rows, cols = grad.shape
+    lanes = 2 * HD
+    pairs = cols // lanes
+    spec = lambda part: pl.BlockSpec((rows, lanes), lambda h: (0, part * pairs + h))
+    work = 2 * rows * rows * cols
+    one = jax.ShapeDtypeStruct((rows, cols), bf16)
+    return pl.pallas_call(
+        attend_back_body, grid=(pairs,), in_specs=[spec(0), spec(1), spec(2), spec(0)], out_specs=[spec(0)] * 3,
+        out_shape=[one] * 3, scratch_shapes=[pltpu.VMEM((rows, lanes), f32)] * 2, compiler_params=params(),
+        cost_estimate=pl.CostEstimate(flops=5 * work, bytes_accessed=14 * rows * cols, transcendentals=rows * rows * cols // HD),
+    )(qkv, qkv, qkv, grad)
+
+def gelu_body(tile, place_ref, x_ref, w_ref, b_ref, g_ref, act_ref, grad_ref, sum_ref):
+    first = pl.program_id(1) == 0
+    for start in range(0, w_ref.shape[1], tile):
+        at = slice(start, start + tile)
+        value = jnp.dot(x_ref[...], w_ref[:, at], preferred_element_type=f32) + b_ref[:, at].astype(f32)
+        square = value * value
+        tangent = jnp.tanh(value * (0.7978845608 + (0.7978845608 * 0.044715) * square))
+        share = 0.5 * value
+        act_ref[:, at] = (share + share * tangent).astype(bf16)
+        bend = share * (0.7978845608 + (3.0 * 0.7978845608 * 0.044715) * square)
+        slope = (0.5 + 0.5 * tangent) + bend * (1.0 - tangent * tangent)
+        grad = g_ref[:, at].astype(f32) * slope
+        grad_ref[:, at] = grad.astype(bf16)
+        total = jnp.sum(grad, 0, keepdims=True)
+        sum_ref[:, at] = jnp.where(first, total, sum_ref[:, at] + total)
+
+def gelu_product(x, weight, bias, grad, place, width, row_tile, col_tile):
+    rows, depth = x.shape
+    steps = width // col_tile
+    grid = pltpu.PrefetchScalarGridSpec(
+        num_scalar_prefetch=1, grid=(steps, rows // row_tile),
+        in_specs=[
+            pl.BlockSpec((row_tile, depth), lambda j, i, s: (i, 0)),
+            pl.BlockSpec((depth, col_tile), lambda j, i, s: (0, s[0] * steps + j)),
+            pl.BlockSpec((1, col_tile), lambda j, i, s: (0, s[0] * steps + j)),
+            pl.BlockSpec((row_tile, col_tile), lambda j, i, s: (i, j)),
+        ],
+        out_specs=[
+            pl.BlockSpec((row_tile, col_tile), lambda j, i, s: (i, j)),
+            pl.BlockSpec((row_tile, col_tile), lambda j, i, s: (i, j)),
+            pl.BlockSpec((1, col_tile), lambda j, i, s: (0, j)),
+        ])
+    return pl.pallas_call(
+        functools.partial(gelu_body, min(256, col_tile)), grid_spec=grid,
+        out_shape=[jax.ShapeDtypeStruct((rows, width), bf16)] * 2 + [jax.ShapeDtypeStruct((1, width), f32)],
+        compiler_params=params(),
+        cost_estimate=pl.CostEstimate(flops=2 * rows * depth * width, bytes_accessed=2 * (rows * depth + depth * width + 3 * rows * width), transcendentals=rows * width),
+    )(place, x, weight, bias[None], grad)
+
+def put_body(place_ref, part_ref, *refs):
+    refs[-1][...] = part_ref[...].astype(f32)
+
+def put_half(part, place, axis, whole=None):
+    rows, width = part.shape
+    tile = min(256, rows)
+    steps = rows // tile
+    shape = (2 * rows, width) if axis == 0 else (rows, 2 * width)
+    at = (lambda i, s: (s[0] * steps + i, 0)) if axis == 0 else (lambda i, s: (i, s[0]))
+    in_specs = [pl.BlockSpec((tile, width), lambda i, s: (i, 0))]
+    args = [place, part]
+    alias = {}
+    if whole is not None:
+        in_specs.append(pl.BlockSpec(memory_space=pl.ANY))
+        args.append(whole)
+        alias = {2: 0}
+    return pl.pallas_call(
+        put_body, grid_spec=pltpu.PrefetchScalarGridSpec(num_scalar_prefetch=1, grid=(steps,), in_specs=in_specs, out_specs=pl.BlockSpec((tile, width), at)),
+        out_shape=jax.ShapeDtypeStruct(shape, f32), input_output_aliases=alias, compiler_params=params(),
+        cost_estimate=pl.CostEstimate(flops=0, bytes_accessed=6 * rows * width, transcendentals=0),
+    )(*args)
 
 
 def matmul(left, right):
     return jnp.dot(left, right, preferred_element_type=f32)
-
-
-def matmul_nt(left, right):
-    return lax.dot_general(left, right, (((1,), (1,)), ((), ())), preferred_element_type=f32)
-
-
-def matmul_tn(left, right):
-    return lax.dot_general(left, right, (((0,), (0,)), ((), ())), preferred_element_type=f32)
 
 
 def column_sums(matrix):
@@ -80,12 +209,16 @@
     terms = [lax.dynamic_slice_in_dim(partial, me * rows, rows, 0)]
     for step in range(1, count):
         sent = lax.dynamic_slice_in_dim(partial, (me ^ step) * rows, rows, 0)
-        terms.append(swap(sent.astype(bf16), step).astype(f32))
+        terms.append(swap(sent.astype(bf16), step))
     return terms
 
 
+def add_terms(terms):
+    return sum(term.astype(f32) for term in terms)
+
+
 def scatter_sum(partial):
-    return sum(scatter_terms(partial))
+    return add_terms(scatter_terms(partial))
 
 
 def gather_rows(block):
@@ -173,7 +306,61 @@
     count = lax.axis_size("group")
     me = lax.axis_index("group")
     cols = width // count
-    heads = cols // HD
+    local = me * rows + jnp.arange(rows, dtype=jnp.int32)
+    active = ((local < lengths[0]) & (exit_layers > LAYER)).astype(f32)[:, None]
+    core = lax.axis_index("replica") % 2
+    other = core_swap(mine)
+    first = jnp.where(core == 0, mine, other)
+    second = jnp.where(core == 0, other, mine)
+    return jnp.concatenate([first, second], axis)
+
+
+class Order:
+    def __init__(self):
+        self.last = ()
+
+    def __call__(self, *values):
+        values = lax.optimization_barrier(values + self.last)[: len(values)]
+        return values[0] if len(values) == 1 else values
+
+    def mark(self, *values):
+        self.last = values
+
+
+def replica_sum_small(values):
+    count = lax.axis_size("replica")
+    step = 1
+    while step < count:
+        values = values + lax.ppermute(values, "replica", [(i, i ^ step) for i in range(count)])
+        step *= 2
+    return values
+
+
+def shards(
+    tokens,
+    lengths,
+    exit_layers,
+    pre_gain,
+    pre_shift,
+    query_weight,
+    query_bias,
+    key_weight,
+    value_weight,
+    value_bias,
+    out_weight,
+    out_bias,
+    mid_gain,
+    mid_shift,
+    up_weight,
+    up_bias,
+    down_weight,
+    down_bias,
+    cotangent,
+):
+    rows, width = tokens.shape
+    count = lax.axis_size("group")
+    me = lax.axis_index("group")
+    cols = width // count
     local = me * rows + jnp.arange(rows, dtype=jnp.int32)
     active = ((local < lengths[0]) & (exit_layers > LAYER)).astype(f32)[:, None]
     position = jnp.arange(count * rows, dtype=jnp.int32)
@@ -183,7 +370,7 @@
 
     grad_out = cotangent.astype(f32)
     branch_grad = (active * grad_out).astype(bf16)
-    tokens_all = in_order(gather_blocks(tokens))
+    tokens_all = in_order(gather_blocks(after(tokens, branch_grad)))
 
     vectors = jnp.concatenate([pre_gain, pre_shift, out_bias, mid_gain, mid_shift, down_bias])
     vectors = vectors.reshape(2, 3 * cols)
@@ -214,92 +401,63 @@
     own = column_block(0, 0, cols).reshape(1, 2, half, 3 * cols)
     qkv_weight = lax.dynamic_update_slice(qkv_weight, own, (me, 0, 0, 0))
     qkv_weight = qkv_weight.reshape(width, 3 * cols)
-    branch_blocks = gather_blocks(after(branch_grad, arrived))
-    branch_all = in_order(branch_blocks)
     everyone = ("replica", "group")
     branch_wide = lax.all_gather(branch_grad, everyone, axis=0, tiled=True)
+    seq = count * rows
+    branch_all = lax.dynamic_slice_in_dim(branch_wide, lax.axis_index("replica") * seq, seq, 0)
 
     normed_all, _ = layer_norm(tokens_all.astype(f32))
     attn_in = (normed_all * gain_one + shift_one).astype(bf16)
     qkv_bias = jnp.concatenate([query_bias, jnp.zeros_like(query_bias), value_bias]).astype(f32)
     qkv = (matmul(attn_in, qkv_weight) + qkv_bias).astype(bf16)
-    queries, keys, values = (
-        qkv[:, k * cols : (k + 1) * cols].reshape(-1, heads, HD) for k in range(3)
-    )
-
-    def scores_of(query, key):
-        scores = jnp.einsum("qhd,khd->hqk", query, key, preferred_element_type=f32) * 0.125
-        return jnp.where(allowed[None], scores, -1e30)
-
-    scores = scores_of(queries, keys)
-    top = jnp.max(scores, -1, keepdims=True)
-    logsum = top + jnp.log(jnp.sum(jnp.exp(scores - top), -1, keepdims=True))
-    weights = jnp.exp(scores - logsum).astype(bf16)
-    context = (
-        jnp.einsum("hqk,khd->qhd", weights, values, preferred_element_type=f32)
-        .astype(bf16)
-        .reshape(-1, cols)
-    )
-    context = after(context, *branch_blocks)
+    context = attention(qkv)
     attn_out = scatter_sum(matmul(context, out_weight)) + obias
     hidden = tokens.astype(f32) + active * attn_out
     normed_two, factor_two = layer_norm(hidden)
     ffn_in = (normed_two * gain_two + shift_two).astype(bf16)
-    act_grad = matmul_nt(branch_all, down_weight)
+    act_grad = nt(branch_all, down_weight).astype(bf16)
     ffn_all = in_order(gather_blocks(ffn_in))
     ffn_wide = lax.all_gather(ffn_in, everyone, axis=0, tiled=True)
-    pre_act = matmul(ffn_all, up_weight) + up_bias.astype(f32)
-    act, slope = gelu_both(pre_act)
-    act_low, pre_grad = lax.optimization_barrier(
-        (act.astype(bf16), (act_grad * slope).astype(bf16))
+    here = jnp.full((1,), core, jnp.int32)
+    ff = up_weight.shape[1]
+    act_low, pre_grad, _ = gelu_product(
+        ffn_all, up_weight, up_bias, act_grad, jnp.zeros((1,), jnp.int32), ff, ffn_all.shape[0], 256
     )
     order = Order()
-    split = up_weight.shape[1] // 2
-    up_half = lax.dynamic_slice(up_weight, (0, core * split), (width, split))
+    order.mark(act_low, pre_grad)
+    split = ff // 2
     down_half = lax.dynamic_slice(down_weight, (core * split, 0), (split, width))
-    bias_half = lax.dynamic_slice(up_bias, (core * split,), (split,)).astype(f32)
-
-    partial = matmul_nt(pre_grad, up_weight)
+
+    partial = nt(pre_grad, up_weight).astype(bf16)
     order.mark(partial)
     ffn_in_grad = scatter_terms(partial)
-    wide_grad = matmul_nt(order(branch_wide), down_half)
+    wide_grad = nt(order(branch_wide), down_half).astype(bf16)
     order.mark(wide_grad)
 
-    ffn_in_grad = sum(order(*ffn_in_grad))
+    ffn_in_grad = add_terms(order(*ffn_in_grad))
     hidden_grad = grad_out + norm_back(ffn_in_grad * gain_two, normed_two, factor_two)
     attn_grad = (active * hidden_grad).astype(bf16)
     order.mark(attn_grad)
     attn_blocks = gather_blocks(attn_grad)
     branch = matmul(order(act_low), down_weight)
-    order.mark(branch)
+    branch_sums = column_sums(branch_wide)
+    order.mark(branch, branch_sums)
 
     attn_all = in_order(list(order(*attn_blocks)))
-    context_grad = matmul_nt(attn_all, out_weight).astype(bf16).reshape(-1, heads, HD)
-    probs = jnp.exp(scores_of(queries, keys) - logsum)
-    probs_grad = jnp.einsum("qhd,khd->hqk", context_grad, values, preferred_element_type=f32)
-    delta = jnp.sum(probs * probs_grad, -1, keepdims=True)
-    score_grad = (probs * (probs_grad - delta)).astype(bf16)
-    query_grad = jnp.einsum("hqk,khd->qhd", score_grad, keys, preferred_element_type=f32) * 0.125
-    key_grad = jnp.einsum("hqk,qhd->khd", score_grad, queries, preferred_element_type=f32) * 0.125
-    value_grad = jnp.einsum(
-        "hqk,qhd->khd", probs.astype(bf16), context_grad, preferred_element_type=f32
-    )
-    qkv_grad = jnp.concatenate(
-        [part.astype(bf16).reshape(-1, cols) for part in (query_grad, key_grad, value_grad)], 1
-    )
-
-    qkv_part = matmul_tn(attn_in, qkv_grad).astype(bf16).reshape(count, cols, 3 * cols)
-    piece = lax.psum_scatter(qkv_part, "replica", scatter_dimension=1, tiled=True)
-    in_part = matmul_nt(after(qkv_grad, qkv_part), qkv_weight)
+    context_grad = nt(attn_all, out_weight).astype(bf16)
+    qkv_grad = jnp.concatenate(attention_back(qkv, context_grad), 1)
+
+    qkv_part = tn(attn_in, qkv_grad).astype(bf16).reshape(count, cols, 3 * cols)
+    out_part = tn(context, attn_all).astype(bf16)
+    out_blocks = [out_part[:, k * cols : (k + 1) * cols] for k in range(count)]
+    parts = jnp.concatenate([qkv_part, jnp.stack(out_blocks)], 2)
+    piece = lax.psum_scatter(parts, "replica", scatter_dimension=1, tiled=True)
+    in_part = nt(after(qkv_grad, parts), qkv_weight)
     order.mark(in_part)
     in_grad = scatter_terms(in_part)
-    out_part = matmul_tn(order(context), attn_all).astype(bf16)
-    out_grad = lax.psum(out_part, "replica")
-    order.mark(out_part)
-
-    wide_act, wide_slope = gelu_both(matmul(order(ffn_wide), up_half) + bias_half)
-    wide_act, wide_grad = lax.optimization_barrier(
-        (wide_act.astype(bf16), (wide_grad * wide_slope).astype(bf16))
+
+    wide_act, wide_grad, wide_sums = gelu_product(
+        order(ffn_wide), up_weight, up_bias, wide_grad, here, split, min(512, rows * count), split
     )
     order.mark(wide_act, wide_grad)
 
@@ -326,39 +484,46 @@
     small_parts = [small[k * cols : (k + 1) * cols] for k in range(7)]
 
     normed_one, factor_one = layer_norm(tokens.astype(f32))
-    in_grad = sum(order(*in_grad))
+    in_grad = add_terms(order(*in_grad))
     token_grad = (hidden_grad + norm_back(in_grad * gain_one, normed_one, factor_one)).astype(bf16)
     order.mark(token_grad)
 
-    down_grad = matmul_tn(order(wide_act), branch_wide).astype(bf16)
+    down_grad = tn(order(wide_act), branch_wide).astype(bf16)
     order.mark(down_grad)
-    piece = reorder(order(piece))
-    piece = reorder(jnp.stack(exchange([piece[k] for k in range(count)])))
-    piece = piece.reshape(count, -1, 3, cols).transpose(1, 2, 0, 3).reshape(-1, 3 * width)
+    piece = order(piece)
+    mixed = reorder(piece[:, :, : 3 * cols])
+    mixed = reorder(jnp.stack(exchange([mixed[k] for k in range(count)])))
+    mixed = mixed.reshape(count, -1, 3, cols).transpose(1, 2, 0, 3).reshape(-1, 3 * width)
+    piece = jnp.concatenate([mixed] + [piece[k, :, 3 * cols :] for k in range(count)], 1)
     order.mark(piece)
-    qkv_wgrad = lax.all_gather(piece, "replica", axis=0, tiled=True)
-    up_grad = matmul_tn(order(ffn_wide), wide_grad).astype(bf16)
+    attn_wgrad = lax.all_gather(piece, "replica", axis=0, tiled=True)
+    up_grad = tn(order(ffn_wide), wide_grad).astype(bf16)
     order.mark(up_grad)
-    down_grad = core_join(down_grad, 0).astype(f32)
-    up_grad = core_join(up_grad, 1).astype(f32)
-    up_bias_grad = core_join(column_sums(wide_grad), 0)
-    down_bias_grad = lax.dynamic_slice(column_sums(branch_wide), (me * cols,), (cols,))
+    down_other, up_other = core_swap(down_grad), core_swap(up_grad)
+    down_grad = put_half(down_grad, here, 0)
+    up_grad = put_half(up_grad, here, 1)
+    down_grad = put_half(down_other, 1 - here, 0, down_grad)
+    up_grad = put_half(up_other, 1 - here, 1, up_grad)
+    up_bias_grad = core_join(wide_sums.reshape(-1), 0)
+    down_bias_grad = lax.dynamic_slice(branch_sums, (me * cols,), (cols,))
 
     branch = scatter_sum(branch) + dbias
     output = (hidden + active * branch).astype(bf16)
-    qkv_wgrad = order(qkv_wgrad)
-    out_grad = order(out_grad).astype(f32)
+    attn_wgrad = order(attn_wgrad)
+    query_wgrad, key_wgrad, value_wgrad, out_wgrad = (
+        attn_wgrad[:, k * width : (k + 1) * width].astype(f32) for k in range(4)
+    )
     return (
         output,
         token_grad,
         small_parts[0],
         small_parts[1],
-        qkv_wgrad[:, :width].astype(f32),
+        query_wgrad,
         small_parts[5],
-        qkv_wgrad[:, width : 2 * width].astype(f32),
-        qkv_wgrad[:, 2 * width :].astype(f32),
+        key_wgrad,
+        value_wgrad,
         small_parts[6],
-        out_grad,
+        out_wgrad,
         small_parts[4],
         small_parts[2],
         small_parts[3],

time: 607 us -> 563 us (0.928)
  Pallas kernels: 0 us -> 96.5 us
  matrix products: 189 us -> 134 us
  other arithmetic: 95.2 us -> 44 us
  local copies, waits for them, and re-layouts: 80.3 us -> 62.9 us
  waiting for transfers between devices: 167 us -> 156 us
  starting transfers between devices: 48.6 us -> 42.5 us
    pallas_call x0 -> x8, Pallas kernels: none -> 96.5 us  [the longest x2 46.7 us: gelu_product(): pl.pallas_call(functools.partial(gelu_body, min(256, col_tile)), grid_spe...]
    convert_element_type x13 -> x1, other arithmetic: 50.3 us -> 10.2 us  [shards(): attn_wgrad[:, k * width:(k + 1) * width].astype(f32)]
    dot_general x5 -> x3, matrix products: 66.8 us -> 27.2 us  [matmul(): return jnp.dot(left, right, preferred_element_type=f32)]
    all_gather x1, waiting for transfers between devices: 24 us -> 0.01 us  [shards(): attn_wgrad = lax.all_gather(piece, 'replica', axis=0, tiled=True)]
    reduce_scatter x1, waiting for transfers between devices: 0.01 us -> 16.3 us  [shards(): piece = lax.psum_scatter(parts, 'replica', scatter_dimension=1, tiled=True)]
    dot_general x15 -> x9, matrix products: 122 us -> 107 us  [the longest x4 55.1 us: tn(): lax.dot_general(left, right, (((0,), (0,)), ((), ())), preferred_element_...]
    unnamed x105 -> x98, local copies, waits for them, and re-layouts: 27.7 us -> 15.7 us
    select_n x3 -> x1, other arithmetic: 10.7 us -> 0.01 us  [core_join(): first = jnp.where(core == 0, mine, other)]
  transfers between devices with their start and end apart: 45 -> 41, of which waited for: 16 -> 22; matrix products, arithmetic and copies ran while one was open for 58% -> 39% of each run, Pallas kernels for 0% -> 17%
where the time goes in v2:
time: 563 us; the launch traced here: 552 us
  waiting for transfers between devices  156 us (28%)
  matrix products  134 us (24%)
  Pallas kernels  96.5 us (17%)
  local copies, waits for them, and re-layouts  62.9 us (11%)
  other arithmetic  44 us (8%)
  starting transfers between devices  42.5 us (8%)
  between operations  15.9 us (3%)
    ppermute x30, waiting for transfers between devices, swap(): return lax.ppermute(block, 'group', [(i, i ^ step) for i in range(count)])  139 us
    dot_general x4, matrix products, tn(): lax.dot_general(left, right, (((0,), (0,)), ((), ())), preferred_element_...  55.1 us
    dot_general x5, matrix products, nt(): lax.dot_general(left, right, (((1,), (1,)), ((), ())), preferred_element_...  51.7 us
    pallas_call x2, Pallas kernels, gelu_product(): pl.pallas_call(functools.partial(gelu_body, min(256, col_tile)), grid_spe...  46.7 us
    ppermute x30, starting transfers between devices, swap(): return lax.ppermute(block, 'group', [(i, i ^ step) for i in range(count)])  37.9 us
    dot_general x3, matrix products, matmul(): return jnp.dot(left, right, preferred_element_type=f32)  27.2 us
    pallas_call x4, Pallas kernels, put_half(): pl.pallas_call(put_body, grid_spec=pltpu.PrefetchScalarGridSpec(num_scala...  26.4 us
    reduce_scatter x1, waiting for transfers between devices, shards(): piece = lax.psum_scatter(parts, 'replica', scatter_dimension=1, tiled=True)  16.3 us
  transfers between devices with their start and end apart: 41, of which 22 were waited for; matrix products, arithmetic and copies ran while one was open for 39% of the time, Pallas kernels for 17%

profile of v2, /device:TPU:0, one launch (start us, length us, event | category | flops | bytes accessed | tf_op | source)
XLA Modules:
  0.0 552.1 jit_solution(13758906416335616286)
XLA Ops:
  34.4 9.0 %collective-permute-done = bf16[128,2048]{1,0:T(8,128)(2,1)} collective-permute-done((bf16[128,2048]{1,0:T(8,128)(2,1)}, bf16[128,2048]{1,0:T(8,128)(2,1)}, u32[]{:S(2)}, u32[]{:S(2)}) %collective-permute-start) | collective-permute-done | bytes 524320 | tf_op jit(solution)/shard_map/ppermute | solution.py:184
  52.6 17.7 %collective-permute-done.5 = bf16[258,1536]{1,0:T(8,128)(2,1)} collective-permute-done((bf16[258,1536]{1,0:T(8,128)(2,1)}, bf16[258,1536]{1,0:T(8,128)(2,1)}, u32[]{:S(2)}, u32[]{:S(2)}) %collective-permute-start.5) | collective-permute-done | bytes 792608 | tf_op jit(solution)/shard_map/ppermute | solution.py:184
  71.5 12.7 %collective-permute-done.4 = bf16[258,1536]{1,0:T(8,128)(2,1)} collective-permute-done((bf16[258,1536]{1,0:T(8,128)(2,1)}, bf16[258,1536]{1,0:T(8,128)(2,1)}, u32[]{:S(2)}, u32[]{:S(2)}) %collective-permute-start.4) | collective-permute-done | bytes 792608 | tf_op jit(solution)/shard_map/ppermute | solution.py:184
  85.4 6.5 %collective-permute-done.3 = bf16[258,1536]{1,0:T(8,128)(2,1)S(1)} collective-permute-done((bf16[258,1536]{1,0:T(8,128)(2,1)}, bf16[258,1536]{1,0:T(8,128)(2,1)S(1)}, u32[]{:S(2)}, u32[]{:S(2)}) %collective-permute-start.3) | collective-permute-done | bytes 792608 | tf_op jit(solution)/shard_map/ppermute | solution.py:184
  108.3 6.7 %fusion.9.q_ref.k_ref.v_ref = bf16[512,1536]{1,0:T(8,128)(2,1)} fusion(bf16[2048,1536]{1,0:T(8,128)(2,1)S(1)} %bitcast.136, f32[1536]{0:T(1024)S(1)} %maximum_convert_fusion, bf16[512,2048]{1,0:T(8,128)(2,1)} %constant_dynamic-update-slice_fusion.17, f32[2048]{0:T(1024)S(1)} %bitcast.164, f32[2048]{0:T(1024)S(1)} %bitcast.157, f32[512]{0:T(512)S(1)} %add_rsqrt_fusion, ...), kind=kOutput, calls=%fused_computation.23 | convolution fusion | flops 3229089792 | bytes 9988096 | tf_op jit(solution)/shard_map/dot_general | solution.py:175
  115.0 8.7 %shard_map.314 = bf16[512,512]{1,0:T(8,128)(2,1)} custom-call(bf16[512,1536]{1,0:T(8,128)(2,1)} %fusion.9.q_ref.k_ref.v_ref, bf16[512,1536]{1,0:T(8,128)(2,1)} %fusion.9.q_ref.k_ref.v_ref, bf16[512,1536]{1,0:T(8,128)(2,1)} %fusion.9.q_ref.k_ref.v_ref), custom_call_target="tpu_custom_call" | custom-call | flops 536870912 | bytes 2097152 | tf_op jit(solution)/shard_map/pallas_call | solution.py:93
  129.9 11.1 %collective-permute-done.7 = bf16[128,2048]{1,0:T(8,128)(2,1)S(1)} collective-permute-done((bf16[128,2048]{1,0:T(8,128)(2,1)S(1)}, bf16[128,2048]{1,0:T(8,128)(2,1)S(1)}, u32[]{:S(2)}, u32[]{:S(2)}) %collective-permute-start.7) | collective-permute-done | bytes 524320 | tf_op jit(solution)/shard_map/ppermute | solution.py:184
  141.0 11.2 %collective-permute-done.9 = bf16[128,2048]{1,0:T(8,128)(2,1)S(1)} collective-permute-done((bf16[128,2048]{1,0:T(8,128)(2,1)S(1)}, bf16[128,2048]{1,0:T(8,128)(2,1)S(1)}, u32[]{:S(2)}, u32[]{:S(2)}) %collective-permute-start.9) | collective-permute-done | bytes 524320 | tf_op jit(solution)/shard_map/ppermute | solution.py:184
  162.0 14.0 %collective-permute-done.10 = bf16[128,2048]{1,0:T(8,128)(2,1)} collective-permute-done((bf16[128,2048]{1,0:T(8,128)(2,1)}, bf16[128,2048]{1,0:T(8,128)(2,1)}, u32[]{:S(2)}, u32[]{:S(2)}) %collective-permute-start.10) | collective-permute-done | bytes 524320 | tf_op jit(solution)/shard_map/ppermute | solution.py:184
  177.9 9.5 %collective-permute-done.11 = bf16[128,2048]{1,0:T(8,128)(2,1)} collective-permute-done((bf16[128,2048]{1,0:T(8,128)(2,1)}, bf16[128,2048]{1,0:T(8,128)(2,1)}, u32[]{:S(2)}, u32[]{:S(2)}) %collective-permute-start.11) | collective-permute-done | bytes 524320 | tf_op jit(solution)/shard_map/ppermute | solution.py:184
  191.2 9.9 %convolution_convert_fusion.6.g_ref = bf16[512,2048]{1,0:T(8,128)(2,1)} fusion(bf16[2048,2048]{1,0:T(8,128)(2,1)} %param.35, bf16[4096,2048]{1,0:T(8,128)(2,1)} %all-gather.4.cloned.1.call-done, s32[]{:T(128)S(6)} %select_n.181), kind=kOutput, calls=%fused_computation.22 | convolution fusion | flops 4296015872 | bytes 12582916 | tf_op jit(solution)/shard_map/dot_general | solution.py:37
  201.1 12.6 %shard_map.315 = (bf16[512,2048]{1,0:T(8,128)(2,1)}, bf16[512,2048]{1,0:T(8,128)(2,1)}, f32[1,2048]{1,0:T(1,128)}) custom-call(s32[1]{0:T(128)} %constant.68.clone.1.place_ref, bf16[512,2048]{1,0:T(8,128)(2,1)} %constant_dynamic-update-slice_fusion.8.x_ref, bf16[2048,2048]{1,0:T(8,128)(2,1)} %w_ref.3, bf16[1,2048]{1,0:T(2,128)(2,1)} %broadcast_in_dim.43.b_ref, ...), custom_call_target="tpu_custom_call" | custom-call | flops 4294967296 | bytes 16777216 | tf_op jit(solution)/shard_map/pallas_call | solution.py:144
  213.6 8.6 %convolution_convert_fusion.5 = bf16[512,2048]{1,0:T(8,128)(2,1)S(1)} fusion(bf16[512,2048]{1,0:T(8,128)(2,1)} %get-tuple-element.48, bf16[2048,2048]{1,0:T(8,128)(2,1)} %w_ref.3), kind=kOutput, calls=%fused_computation.21 | convolution fusion | flops 4296015872 | bytes 12582912 | tf_op jit(solution)/shard_map/dot_general | solution.py:37
  226.9 24.3 %convolution_convert_fusion.1.g_ref = bf16[4096,1024]{1,0:T(8,128)(2,1)} fusion(bf16[4096,2048]{1,0:T(8,128)(2,1)} %all-gather.4.cloned.1.call-done, bf16[2048,2048]{1,0:T(8,128)(2,1)} %param.35, s32[]{:T(128)S(6)} %select_n.182), kind=kOutput, calls=%fused_computation.3 | convolution fusion | flops 17184063488 | bytes 29360132 | tf_op jit(solution)/shard_map/dot_general | solution.py:37
  251.2 4.5 convert_reduce_fusion
  255.8 5.1 collective-permute-done.13
  268.4 18.1 %fusion.47 = f32[512,2048]{1,0:T(8,128)} fusion(bf16[512,2048]{1,0:T(8,128)(2,1)S(1)} %copy-done.38, bf16[2048,2048]{1,0:T(8,128)(2,1)} %param.35), kind=kOutput, calls=%fused_computation.173 | convolution fusion | flops 4294967296 | bytes 14680064 | tf_op jit(solution)/shard_map/dot_general | solution.py:175
  289.4 8.5 %collective-permute-done.20 = bf16[128,2048]{1,0:T(8,128)(2,1)S(1)} collective-permute-done((bf16[128,2048]{1,0:T(8,128)(2,1)S(1)}, bf16[128,2048]{1,0:T(8,128)(2,1)S(1)}, u32[]{:S(2)}, u32[]{:S(2)}) %collective-permute-start.20) | collective-permute-done | bytes 524320 | tf_op jit(solution)/shard_map/ppermute | solution.py:184
  300.5 14.7 %shard_map.316 = (bf16[512,512]{1,0:T(8,128)(2,1)}, bf16[512,512]{1,0:T(8,128)(2,1)}, bf16[512,512]{1,0:T(8,128)(2,1)}) custom-call(bf16[512,1536]{1,0:T(8,128)(2,1)} %fusion.9.q_ref.k_ref.v_ref, bf16[512,1536]{1,0:T(8,128)(2,1)} %fusion.9.q_ref.k_ref.v_ref, bf16[512,1536]{1,0:T(8,128)(2,1)} %fusion.9.q_ref.k_ref.v_ref, ...), custom_call_target="tpu_custom_call" | custom-call | flops 1342177280 | bytes 3670016 | tf_op jit(solution)/shard_map/pallas_call | solution.py:106
  320.4 5.8 %convolution_convert_fusion = bf16[2048,1536]{1,0:T(8,128)(2,1)S(1)} fusion(bf16[512,1536]{1,0:T(8,128)(2,1)S(1)} %constant_dynamic-update-slice_fusion, bf16[512,2048]{1,0:T(8,128)(2,1)} %constant_dynamic-update-slice_fusion.17, f32[2048]{0:T(1024)S(1)} %bitcast.165, f32[2048]{0:T(1024)S(1)} %bitcast.158, f32[512]{0:T(512)S(1)} %copy-done.34, ...), kind=kOutput, calls=%fused_computation.2 | convolution fusion | flops 3230662656 | bytes 9981952 | tf_op jit(solution)/shard_map/dot_general | solution.py:39
  330.8 6.9 %fusion.6 = (f32[2048]{0:T(1024)S(1)}, f32[2048]{0:T(1024)S(1)}, f32[512,2048]{1,0:T(8,128)S(1)}) fusion(bf16[512,2048]{1,0:T(8,128)(2,1)} %constant_dynamic-update-slice_fusion.17, f32[512]{0:T(512)S(1)} %copy-done.34, f32[512]{0:T(512)S(1)} %copy-done.24, bf16[512,1536]{1,0:T(8,128)(2,1)S(1)} %constant_dynamic-update-slice_fusion, ...), kind=kOutput, calls=%fused_computation.12 | convolution fusion | flops 3227512832 | bytes 14176256 | tf_op jit(solution)/shard_map/dot_general | solution.py:37
  342.5 34.1 %shard_map.317 = (bf16[4096,1024]{1,0:T(8,128)(2,1)}, bf16[4096,1024]{1,0:T(8,128)(2,1)}, f32[1,1024]{1,0:T(1,128)}) custom-call(s32[1]{0:T(128)} %bitcast.27.place_ref, bf16[4096,2048]{1,0:T(8,128)(2,1)} %all-gather.6.cloned.1.call-done.x_ref, bf16[2048,2048]{1,0:T(8,128)(2,1)} %w_ref.3, bf16[1,2048]{1,0:T(2,128)(2,1)} %broadcast_in_dim.43.b_ref, ...), custom_call_target="tpu_custom_call" | custom-call | flops 17179869184 | bytes 46137344 | tf_op jit(solution)/shard_map/pallas_call | solution.py:144
  380.0 24.0 %convolution_convert_fusion.3.part_ref = bf16[1024,2048]{1,0:T(8,128)(2,1)} fusion(bf16[4096,1024]{1,0:T(8,128)(2,1)} %get-tuple-element.70, bf16[4096,2048]{1,0:T(8,128)(2,1)} %all-gather.4.cloned.1.call-done), kind=kOutput, calls=%fused_computation.17 | convolution fusion | flops 17181966336 | bytes 29360128 | tf_op jit(solution)/shard_map/dot_general | solution.py:39
  403.9 16.3 %reduce-scatter.2.cloned.1.call-done = bf16[4,64,2048]{2,1,0:T(8,128)(2,1)} async-done(((bf16[4,512,2048]{2,1,0:T(8,128)(2,1)}), bf16[4,64,2048]{2,1,0:T(8,128)(2,1)}) %reduce-scatter.2.cloned.1.call-update) | async-done | bytes 1048592 | tf_op jit(solution)/shard_map/reduce_scatter | solution.py:454
  440.7 24.1 %convolution_convert_fusion.2.part_ref = bf16[2048,1024]{1,0:T(8,128)(2,1)} fusion(bf16[4096,2048]{1,0:T(8,128)(2,1)} %all-gather.6.cloned.1.call-done.x_ref, bf16[4096,1024]{1,0:T(8,128)(2,1)} %get-tuple-element.65), kind=kOutput, calls=%fused_computation.16 | convolution fusion | flops 17181966336 | bytes 29360128 | tf_op jit(solution)/shard_map/dot_general | solution.py:39
  482.2 10.9 %collective-permute-done.16 = bf16[128,2048]{1,0:T(8,128)(2,1)S(1)} collective-permute-done((bf16[128,2048]{1,0:T(8,128)(2,1)}, bf16[128,2048]{1,0:T(8,128)(2,1)S(1)}, u32[]{:S(2)}, u32[]{:S(2)}) %collective-permute-start.16) | collective-permute-done | bytes 524320 | tf_op jit(solution)/shard_map/ppermute | solution.py:184
  494.6 8.7 %collective-permute-done.18 = bf16[128,2048]{1,0:T(8,128)(2,1)S(1)} collective-permute-done((bf16[128,2048]{1,0:T(8,128)(2,1)S(1)}, bf16[128,2048]{1,0:T(8,128)(2,1)S(1)}, u32[]{:S(2)}, u32[]{:S(2)}) %collective-permute-start.18) | collective-permute-done | bytes 524320 | tf_op jit(solution)/shard_map/ppermute | solution.py:184
  507.8 5.9 %shard_map.320.refs_0_ = f32[2048,2048]{1,0:T(8,128)} custom-call(s32[1]{0:T(128)} %bitcast.27.place_ref, bf16[1024,2048]{1,0:T(8,128)(2,1)} %convolution_convert_fusion.3.part_ref), custom_call_target="tpu_custom_call" | custom-call | bytes 12582912 | tf_op jit(solution)/shard_map/pallas_call | solution.py:167
  514.4 6.0 %shard_map.321 = f32[2048,2048]{1,0:T(8,128)} custom-call(s32[1]{0:T(128)S(6)} %sub.68.place_ref, bf16[1024,2048]{1,0:T(8,128)(2,1)} %collective-permute-done.36.part_ref, f32[2048,2048]{1,0:T(8,128)} %shard_map.320.refs_0_), custom_call_target="tpu_custom_call", output_to_operand_aliasing={{}: (2, {})} | custom-call | bytes 12582912 | tf_op jit(solution)/shard_map/pallas_call | solution.py:167
  520.3 7.3 %shard_map.318.refs_0_ = f32[2048,2048]{1,0:T(8,128)} custom-call(s32[1]{0:T(128)} %bitcast.27.place_ref, bf16[2048,1024]{1,0:T(8,128)(2,1)} %convolution_convert_fusion.2.part_ref), custom_call_target="tpu_custom_call" | custom-call | bytes 12582912 | tf_op jit(solution)/shard_map/pallas_call | solution.py:167
  527.6 7.3 %shard_map.319 = f32[2048,2048]{1,0:T(8,128)} custom-call(s32[1]{0:T(128)S(6)} %sub.68.place_ref, bf16[2048,1024]{1,0:T(8,128)(2,1)} %collective-permute-done.34.part_ref, f32[2048,2048]{1,0:T(8,128)} %shard_map.318.refs_0_), custom_call_target="tpu_custom_call", output_to_operand_aliasing={{}: (2, {})} | custom-call | bytes 12582912 | tf_op jit(solution)/shard_map/pallas_call | solution.py:167
  534.9 10.2 %slice_convert_fusion = (f32[512,2048]{1,0:T(8,128)}, f32[512,2048]{1,0:T(8,128)}, f32[512,2048]{1,0:T(8,128)}, f32[512,2048]{1,0:T(8,128)}) fusion(bf16[512,8192]{1,0:T(8,128)(2,1)} %all-gather.8.cloned.1.call-done), kind=kLoop, calls=%fused_computation.25 | loop fusion | flops 4194304 | bytes 25165824 | tf_op jit(solution)/shard_map/convert_element_type | solution.py:514
  (280 shorter events, 155.4 us)
Async XLA Ops:
  7.2 184.0 %all-gather.4.cloned.1.call-start = ((), (), s32[]{:S(2)}) async-start(), calls=%async_computation.1 | async-start | bytes 17301504 | tf_op jit(solution)/shard_map/all_gather | solution.py:405
  10.7 331.7 %all-gather.6.cloned.1.call-start = ((), (), s32[]{:S(2)}) async-start(), calls=%async_computation.2 | async-start | bytes 17301504 | tf_op jit(solution)/shard_map/all_gather | solution.py:420
  10.8 37.8 %collective-permute-start.2 = (bf16[128,2048]{1,0:T(8,128)(2,1)}, bf16[128,2048]{1,0:T(8,128)(2,1)}, u32[]{:S(2)}, u32[]{:S(2)}) collective-permute-start(bf16[128,2048]{1,0:T(8,128)(2,1)} %param.19), channel_id=1, source_target_pairs={{0,3},{1,2},{2,1},{3,0},{4,7},{5,6},{6,5},{7,4},{8,11},{9,10},{10,... | collective-permute-start | bytes 1572872 | tf_op jit(solution)/shard_map/ppermute | solution.py:184
  14.7 32.0 %collective-permute-start.1 = (bf16[128,2048]{1,0:T(8,128)(2,1)}, bf16[128,2048]{1,0:T(8,128)(2,1)}, u32[]{:S(2)}, u32[]{:S(2)}) collective-permute-start(bf16[128,2048]{1,0:T(8,128)(2,1)} %param.19), channel_id=1, source_target_pairs={{0,2},{1,3},{2,0},{3,1},{4,6},{5,7},{6,4},{7,5},{8,10},{9,11},{10,... | collective-permute-start | bytes 1572872 | tf_op jit(solution)/shard_map/ppermute | solution.py:184
  15.2 28.2 %collective-permute-start = (bf16[128,2048]{1,0:T(8,128)(2,1)}, bf16[128,2048]{1,0:T(8,128)(2,1)}, u32[]{:S(2)}, u32[]{:S(2)}) collective-permute-start(bf16[128,2048]{1,0:T(8,128)(2,1)} %param.19), channel_id=1, source_target_pairs={{0,1},{1,0},{2,3},{3,2},{4,5},{5,4},{6,7},{7,6},{8,9},{9,8},{10,11... | collective-permute-start | bytes 1572872 | tf_op jit(solution)/shard_map/ppermute | solution.py:184
  24.8 45.5 %collective-permute-start.5 = (bf16[258,1536]{1,0:T(8,128)(2,1)}, bf16[258,1536]{1,0:T(8,128)(2,1)}, u32[]{:S(2)}, u32[]{:S(2)}) collective-permute-start(bf16[258,1536]{1,0:T(8,128)(2,1)} %get-tuple-element.146), channel_id=1, source_target_pairs={{0,3},{1,2},{2,1},{3,0},{4,7},{5,6},{6,5},{7,4},{8,11},{9,10},{10,... | collective-permute-start | bytes 2377736 | tf_op jit(solution)/shard_map/ppermute | solution.py:184
  27.7 56.5 %collective-permute-start.4 = (bf16[258,1536]{1,0:T(8,128)(2,1)}, bf16[258,1536]{1,0:T(8,128)(2,1)}, u32[]{:S(2)}, u32[]{:S(2)}) collective-permute-start(bf16[258,1536]{1,0:T(8,128)(2,1)} %get-tuple-element.147), channel_id=1, source_target_pairs={{0,2},{1,3},{2,0},{3,1},{4,6},{5,7},{6,4},{7,5},{8,10},{9,11},{10,... | collective-permute-start | bytes 2377736 | tf_op jit(solution)/shard_map/ppermute | solution.py:184
  43.4 48.5 %collective-permute-start.3 = (bf16[258,1536]{1,0:T(8,128)(2,1)}, bf16[258,1536]{1,0:T(8,128)(2,1)S(1)}, u32[]{:S(2)}, u32[]{:S(2)}) collective-permute-start(bf16[258,1536]{1,0:T(8,128)(2,1)} %get-tuple-element.148), channel_id=1, source_target_pairs={{0,1},{1,0},{2,3},{3,2},{4,5},{5,4},{6,7},{7,6},{8,9},{9,8},{10,11... | collective-permute-start | bytes 2377736 | tf_op jit(solution)/shard_map/ppermute | solution.py:184
  126.2 14.8 %collective-permute-start.7 = (bf16[128,2048]{1,0:T(8,128)(2,1)S(1)}, bf16[128,2048]{1,0:T(8,128)(2,1)S(1)}, u32[]{:S(2)}, u32[]{:S(2)}) collective-permute-start(bf16[128,2048]{1,0:T(8,128)(2,1)S(1)} %get-tuple-element.101), channel_id=1, source_target_pairs={{0,1},{1,0},{2,3},{3,2},{4,5},{5,4},{6,7},{7,6},{8,9},{9,8},{10,11... | collective-permute-start | bytes 1572872 | tf_op jit(solution)/shard_map/ppermute | solution.py:184
  128.0 24.1 %collective-permute-start.9 = (bf16[128,2048]{1,0:T(8,128)(2,1)S(1)}, bf16[128,2048]{1,0:T(8,128)(2,1)S(1)}, u32[]{:S(2)}, u32[]{:S(2)}) collective-permute-start(bf16[128,2048]{1,0:T(8,128)(2,1)S(1)} %get-tuple-element.102), channel_id=1, source_target_pairs={{0,3},{1,2},{2,1},{3,0},{4,7},{5,6},{6,5},{7,4},{8,11},{9,10},{10,... | collective-permute-start | bytes 1572872 | tf_op jit(solution)/shard_map/ppermute | solution.py:184
  128.5 24.8 %collective-permute-start.8 = (bf16[128,2048]{1,0:T(8,128)(2,1)S(1)}, bf16[128,2048]{1,0:T(8,128)(2,1)S(1)}, u32[]{:S(2)}, u32[]{:S(2)}) collective-permute-start(bf16[128,2048]{1,0:T(8,128)(2,1)S(1)} %get-tuple-element.103), channel_id=1, source_target_pairs={{0,2},{1,3},{2,0},{3,1},{4,6},{5,7},{6,4},{7,5},{8,10},{9,11},{10,... | collective-permute-start | bytes 1572872 | tf_op jit(solution)/shard_map/ppermute | solution.py:184
  157.5 262.7 %reduce-scatter.2.cloned.1.call-start = ((), (), s32[]{:S(2)}) async-start(), calls=%async_computation.3 | async-start | bytes 9437184 | tf_op jit(solution)/shard_map/reduce_scatter | solution.py:454
  157.8 18.2 %collective-permute-start.10 = (bf16[128,2048]{1,0:T(8,128)(2,1)}, bf16[128,2048]{1,0:T(8,128)(2,1)}, u32[]{:S(2)}, u32[]{:S(2)}) collective-permute-start(bf16[128,2048]{1,0:T(8,128)(2,1)} %get-tuple-element.88), channel_id=1, source_target_pairs={{0,1},{1,0},{2,3},{3,2},{4,5},{5,4},{6,7},{7,6},{8,9},{9,8},{10,11... | collective-permute-start | bytes 1572872 | tf_op jit(solution)/shard_map/ppermute | solution.py:184
  159.5 27.9 %collective-permute-start.11 = (bf16[128,2048]{1,0:T(8,128)(2,1)}, bf16[128,2048]{1,0:T(8,128)(2,1)}, u32[]{:S(2)}, u32[]{:S(2)}) collective-permute-start(bf16[128,2048]{1,0:T(8,128)(2,1)} %get-tuple-element.88), channel_id=1, source_target_pairs={{0,2},{1,3},{2,0},{3,1},{4,6},{5,7},{6,4},{7,5},{8,10},{9,11},{10,... | collective-permute-start | bytes 1572872 | tf_op jit(solution)/shard_map/ppermute | solution.py:184
  160.8 28.5 %collective-permute-start.12 = (bf16[128,2048]{1,0:T(8,128)(2,1)}, bf16[128,2048]{1,0:T(8,128)(2,1)}, u32[]{:S(2)}, u32[]{:S(2)}) collective-permute-start(bf16[128,2048]{1,0:T(8,128)(2,1)} %get-tuple-element.88), channel_id=1, source_target_pairs={{0,3},{1,2},{2,1},{3,0},{4,7},{5,6},{6,5},{7,4},{8,11},{9,10},{10,... | collective-permute-start | bytes 1572872 | tf_op jit(solution)/shard_map/ppermute | solution.py:184
  223.4 32.4 %collective-permute-start.15 = (bf16[128,2048]{1,0:T(8,128)(2,1)}, bf16[128,2048]{1,0:T(8,128)(2,1)S(1)}, u32[]{:S(2)}, u32[]{:S(2)}) collective-permute-start(bf16[128,2048]{1,0:T(8,128)(2,1)} %get-tuple-element.108), channel_id=1, source_target_pairs={{0,3},{1,2},{2,1},{3,0},{4,7},{5,6},{6,5},{7,4},{8,11},{9,10},{10,... | collective-permute-start | bytes 1572872 | tf_op jit(solution)/shard_map/ppermute | solution.py:184
  224.8 31.0 %collective-permute-start.14 = (bf16[128,2048]{1,0:T(8,128)(2,1)}, bf16[128,2048]{1,0:T(8,128)(2,1)}, u32[]{:S(2)}, u32[]{:S(2)}) collective-permute-start(bf16[128,2048]{1,0:T(8,128)(2,1)} %get-tuple-element.109), channel_id=1, source_target_pairs={{0,2},{1,3},{2,0},{3,1},{4,6},{5,7},{6,4},{7,5},{8,10},{9,11},{10,... | collective-permute-start | bytes 1572872 | tf_op jit(solution)/shard_map/ppermute | solution.py:184
  224.8 36.1 %collective-permute-start.13 = (bf16[128,2048]{1,0:T(8,128)(2,1)}, bf16[128,2048]{1,0:T(8,128)(2,1)}, u32[]{:S(2)}, u32[]{:S(2)}) collective-permute-start(bf16[128,2048]{1,0:T(8,128)(2,1)} %get-tuple-element.110), channel_id=1, source_target_pairs={{0,1},{1,0},{2,3},{3,2},{4,5},{5,4},{6,7},{7,6},{8,9},{9,8},{10,11... | collective-permute-start | bytes 1572872 | tf_op jit(solution)/shard_map/ppermute | solution.py:184
  264.6 24.9 %collective-permute-start.21 = (bf16[128,2048]{1,0:T(8,128)(2,1)S(1)}, bf16[128,2048]{1,0:T(8,128)(2,1)S(1)}, u32[]{:S(2)}, u32[]{:S(2)}) collective-permute-start(bf16[128,2048]{1,0:T(8,128)(2,1)S(1)} %get-tuple-element.55), channel_id=1, source_target_pairs={{0,3},{1,2},{2,1},{3,0},{4,7},{5,6},{6,5},{7,4},{8,11},{9,10},{10,... | collective-permute-start | bytes 1572872 | tf_op jit(solution)/shard_map/ppermute | solution.py:184
  265.0 32.9 %collective-permute-start.20 = (bf16[128,2048]{1,0:T(8,128)(2,1)S(1)}, bf16[128,2048]{1,0:T(8,128)(2,1)S(1)}, u32[]{:S(2)}, u32[]{:S(2)}) collective-permute-start(bf16[128,2048]{1,0:T(8,128)(2,1)S(1)} %get-tuple-element.55), channel_id=1, source_target_pairs={{0,2},{1,3},{2,0},{3,1},{4,6},{5,7},{6,4},{7,5},{8,10},{9,11},{10,... | collective-permute-start | bytes 1572872 | tf_op jit(solution)/shard_map/ppermute | solution.py:184
  268.4 29.5 %collective-permute-start.19 = (bf16[128,2048]{1,0:T(8,128)(2,1)S(1)}, bf16[128,2048]{1,0:T(8,128)(2,1)S(1)}, u32[]{:S(2)}, u32[]{:S(2)}) collective-permute-start(bf16[128,2048]{1,0:T(8,128)(2,1)S(1)} %get-tuple-element.55), channel_id=1, source_target_pairs={{0,1},{1,0},{2,3},{3,2},{4,5},{5,4},{6,7},{7,6},{8,9},{9,8},{10,11... | collective-permute-start | bytes 1572872 | tf_op jit(solution)/shard_map/ppermute | solution.py:184
  330.1 204.7 %all-gather.8.cloned.1.call-start = ((), (), s32[]{:S(2)}) async-start(), calls=%async_computation.4 | async-start | bytes 9437184 | tf_op jit(solution)/shard_map/all_gather | solution.py:499
  338.9 37.8 %collective-permute-start.24 = (bf16[128,2048]{1,0:T(8,128)(2,1)}, bf16[128,2048]{1,0:T(8,128)(2,1)}, u32[]{:S(2)}, u32[]{:S(2)}) collective-permute-start(bf16[128,2048]{1,0:T(8,128)(2,1)} %get-tuple-element.95), channel_id=1, source_target_pairs={{0,3},{1,2},{2,1},{3,0},{4,7},{5,6},{6,5},{7,4},{8,11},{9,10},{10,... | collective-permute-start | bytes 1572872 | tf_op jit(solution)/shard_map/ppermute | solution.py:184
  340.6 36.1 %collective-permute-start.23 = (bf16[128,2048]{1,0:T(8,128)(2,1)}, bf16[128,2048]{1,0:T(8,128)(2,1)}, u32[]{:S(2)}, u32[]{:S(2)}) collective-permute-start(bf16[128,2048]{1,0:T(8,128)(2,1)} %get-tuple-element.96), channel_id=1, source_target_pairs={{0,2},{1,3},{2,0},{3,1},{4,6},{5,7},{6,4},{7,5},{8,10},{9,11},{10,... | collective-permute-start | bytes 1572872 | tf_op jit(solution)/shard_map/ppermute | solution.py:184
  341.5 35.2 %collective-permute-start.22 = (bf16[128,2048]{1,0:T(8,128)(2,1)S(1)}, bf16[128,2048]{1,0:T(8,128)(2,1)}, u32[]{:S(2)}, u32[]{:S(2)}) collective-permute-start(bf16[128,2048]{1,0:T(8,128)(2,1)S(1)} %get-tuple-element.97), channel_id=1, source_target_pairs={{0,1},{1,0},{2,3},{3,2},{4,5},{5,4},{6,7},{7,6},{8,9},{9,8},{10,11... | collective-permute-start | bytes 1572872 | tf_op jit(solution)/shard_map/ppermute | solution.py:184
  421.8 7.9 %collective-permute-start.33 = (bf16[64,1536]{1,0:T(8,128)(2,1)S(1)}, bf16[64,1536]{1,0:T(8,128)(2,1)S(1)}, u32[]{:S(2)}, u32[]{:S(2)}) collective-permute-start(bf16[64,1536]{1,0:T(8,128)(2,1)S(1)} %get-tuple-element.122), channel_id=1, source_target_pairs={{0,3},{1,2},{2,1},{3,0},{4,7},{5,6},{6,5},{7,4},{8,11},{9,10},{10,... | collective-permute-start | bytes 589832 | tf_op jit(solution)/shard_map/ppermute | solution.py:184
  440.6 73.8 %collective-permute-start.36 = (bf16[1024,2048]{1,0:T(8,128)(2,1)}, bf16[1024,2048]{1,0:T(8,128)(2,1)}, u32[]{:S(2)}, u32[]{:S(2)}) collective-permute-start(bf16[1024,2048]{1,0:T(8,128)(2,1)} %convolution_convert_fusion.3.part_ref), channel_id=1, source_target_pairs={{0,4},{4,0},{8,12},{12,8},{16,20},{20,16},{24,28},{28,24},{1,5},{5... | collective-permute-start | bytes 12582920 | tf_op jit(solution)/shard_map/ppermute | solution.py:252
  464.8 62.8 %collective-permute-start.34 = (bf16[2048,1024]{1,0:T(8,128)(2,1)}, bf16[2048,1024]{1,0:T(8,128)(2,1)}, u32[]{:S(2)}, u32[]{:S(2)}) collective-permute-start(bf16[2048,1024]{1,0:T(8,128)(2,1)} %convolution_convert_fusion.2.part_ref), channel_id=1, source_target_pairs={{0,4},{4,0},{8,12},{12,8},{16,20},{20,16},{24,28},{28,24},{1,5},{5... | collective-permute-start | bytes 12582920 | tf_op jit(solution)/shard_map/ppermute | solution.py:252
  478.1 15.0 %collective-permute-start.16 = (bf16[128,2048]{1,0:T(8,128)(2,1)}, bf16[128,2048]{1,0:T(8,128)(2,1)S(1)}, u32[]{:S(2)}, u32[]{:S(2)}) collective-permute-start(bf16[128,2048]{1,0:T(8,128)(2,1)} %get-tuple-element.98), channel_id=1, source_target_pairs={{0,1},{1,0},{2,3},{3,2},{4,5},{5,4},{6,7},{7,6},{8,9},{9,8},{10,11... | collective-permute-start | bytes 1572872 | tf_op jit(solution)/shard_map/ppermute | solution.py:184
  479.0 24.2 %collective-permute-start.18 = (bf16[128,2048]{1,0:T(8,128)(2,1)S(1)}, bf16[128,2048]{1,0:T(8,128)(2,1)S(1)}, u32[]{:S(2)}, u32[]{:S(2)}) collective-permute-start(bf16[128,2048]{1,0:T(8,128)(2,1)S(1)} %get-tuple-element.99), channel_id=1, source_target_pairs={{0,3},{1,2},{2,1},{3,0},{4,7},{5,6},{6,5},{7,4},{8,11},{9,10},{10,... | collective-permute-start | bytes 1572872 | tf_op jit(solution)/shard_map/ppermute | solution.py:184
  480.1 24.5 %collective-permute-start.17 = (bf16[128,2048]{1,0:T(8,128)(2,1)S(1)}, bf16[128,2048]{1,0:T(8,128)(2,1)}, u32[]{:S(2)}, u32[]{:S(2)}) collective-permute-start(bf16[128,2048]{1,0:T(8,128)(2,1)S(1)} %get-tuple-element.100), channel_id=1, source_target_pairs={{0,2},{1,3},{2,0},{3,1},{4,6},{5,7},{6,4},{7,5},{8,10},{9,11},{10,... | collective-permute-start | bytes 1572872 | tf_op jit(solution)/shard_map/ppermute | solution.py:184
  493.1 14.0 %collective-permute-start.30 = (f32[3584]{0:T(1024)S(1)}, f32[3584]{0:T(1024)S(1)}, u32[]{:S(2)}, u32[]{:S(2)}) collective-permute-start(f32[3584]{0:T(1024)S(1)} %add.317), channel_id=1, source_target_pairs={{0,16},{4,20},{8,24},{12,28},{16,0},{20,4},{24,8},{28,12},{1,17},{... | collective-permute-start | bytes 43016 | tf_op jit(solution)/shard_map/ppermute | solution.py:334
  (52 other events, 913.6 us)
Sparse Core Ops, SparseCore 0:
  11.5 138.4 all-gather.3
  157.6 161.3 all-gather.5
  330.2 89.9 reduce-scatter.1
  440.7 82.4 all-gather.7

commit v3 on v2

--- a/solution.py
+++ b/solution.py
@@ -109,8 +109,7 @@
         cost_estimate=pl.CostEstimate(flops=5 * work, bytes_accessed=14 * rows * cols, transcendentals=rows * rows * cols // HD),
     )(qkv, qkv, qkv, grad)
 
-def gelu_body(tile, place_ref, x_ref, w_ref, b_ref, g_ref, act_ref, grad_ref, sum_ref):
-    first = pl.program_id(1) == 0
+def gelu_tiles(tile, first, x_ref, w_ref, b_ref, g_ref, act_ref, grad_ref, sum_ref):
     for start in range(0, w_ref.shape[1], tile):
         at = slice(start, start + tile)
         value = jnp.dot(x_ref[...], w_ref[:, at], preferred_element_type=f32) + b_ref[:, at].astype(f32)
@@ -123,7 +122,14 @@
         grad = g_ref[:, at].astype(f32) * slope
         grad_ref[:, at] = grad.astype(bf16)
         total = jnp.sum(grad, 0, keepdims=True)
-        sum_ref[:, at] = jnp.where(first, total, sum_ref[:, at] + total)
+        if first is not True:
+            total = jnp.where(first, total, sum_ref[:, at] + total)
+        sum_ref[:, at] = total
+
+
+def gelu_body(tile, place_ref, *refs):
+    gelu_tiles(tile, pl.program_id(1) == 0, *refs)
+
 
 def gelu_product(x, weight, bias, grad, place, width, row_tile, col_tile):
     rows, depth = x.shape
@@ -148,6 +154,90 @@
         cost_estimate=pl.CostEstimate(flops=2 * rows * depth * width, bytes_accessed=2 * (rows * depth + depth * width + 3 * rows * width), transcendentals=rows * width),
     )(place, x, weight, bias[None], grad)
 
+def gelu_blocks_body(tile, member_ref, *refs):
+    count = len(refs) - 7
+    blocks, (w_ref, b_ref, g_ref, act_ref, grad_ref, sum_ref, x_ref) = refs[:count], refs[count:]
+    rows = blocks[0].shape[0]
+
+    @pl.when(pl.program_id(0) == 0)
+    def _():
+        for k, block in enumerate(blocks):
+            start = pl.multiple_of(member_ref[k] * rows, rows)
+            x_ref[pl.ds(start, rows), :] = block[...]
+
+    gelu_tiles(tile, True, x_ref, w_ref, b_ref, g_ref, act_ref, grad_ref, sum_ref)
+
+
+def gelu_product_blocks(blocks, members, weight, bias, grad, col_tile):
+    (rows, depth), count, width = blocks[0].shape, len(blocks), weight.shape[1]
+    tall = count * rows
+    grid = pltpu.PrefetchScalarGridSpec(
+        num_scalar_prefetch=1,
+        grid=(width // col_tile,),
+        in_specs=[pl.BlockSpec((rows, depth), lambda j, s: (0, 0))] * count
+        + [
+            pl.BlockSpec((depth, col_tile), lambda j, s: (0, j)),
+            pl.BlockSpec((1, col_tile), lambda j, s: (0, j)),
+            pl.BlockSpec((tall, col_tile), lambda j, s: (0, j)),
+        ],
+        out_specs=[
+            pl.BlockSpec((tall, col_tile), lambda j, s: (0, j)),
+            pl.BlockSpec((tall, col_tile), lambda j, s: (0, j)),
+            pl.BlockSpec((1, col_tile), lambda j, s: (0, j)),
+        ],
+        scratch_shapes=[pltpu.VMEM((tall, depth), bf16)],
+    )
+    return pl.pallas_call(
+        functools.partial(gelu_blocks_body, col_tile),
+        grid_spec=grid,
+        out_shape=[jax.ShapeDtypeStruct((tall, width), bf16)] * 2
+        + [jax.ShapeDtypeStruct((1, width), f32)],
+        compiler_params=params(),
+        cost_estimate=pl.CostEstimate(
+            flops=2 * tall * depth * width,
+            bytes_accessed=2 * (tall * depth + depth * width + 3 * tall * width),
+            transcendentals=tall * width,
+        ),
+    )(members, *blocks, weight, bias[None], grad)
+
+
+def qkv_body(count, at_ref, x_ref, own_ref, *refs):
+    blocks, b_ref, out_ref = refs[:-2], refs[-2], refs[-1]
+    cols = own_ref.shape[0]
+    half = cols // 2
+    at = pl.multiple_of(at_ref[0], cols)
+    total = jnp.dot(x_ref[:, pl.ds(at, cols)], own_ref[...], preferred_element_type=f32)
+    for k, block in enumerate(blocks):
+        at = pl.multiple_of(at_ref[1 + k], half)
+        total += jnp.dot(x_ref[:, pl.ds(at, half)], block[...], preferred_element_type=f32)
+    out_ref[...] = (total + b_ref[...].astype(f32)).astype(bf16)
+
+
+def qkv_product(x, own, blocks, starts, bias):
+    rows, width = x.shape
+    cols = own.shape[0]
+    half = cols // 2
+    column = lambda size: pl.BlockSpec((size, cols), lambda j, s: (0, j))
+    return pl.pallas_call(
+        functools.partial(qkv_body, len(blocks)),
+        grid_spec=pltpu.PrefetchScalarGridSpec(
+            num_scalar_prefetch=1,
+            grid=(3,),
+            in_specs=[pl.BlockSpec((rows, width), lambda j, s: (0, 0)), column(cols)]
+            + [column(half)] * len(blocks)
+            + [column(1)],
+            out_specs=column(rows),
+        ),
+        out_shape=jax.ShapeDtypeStruct((rows, 3 * cols), bf16),
+        compiler_params=params(),
+        cost_estimate=pl.CostEstimate(
+            flops=6 * rows * width * cols,
+            bytes_accessed=2 * (rows * width + 3 * width * cols + 3 * rows * cols),
+            transcendentals=0,
+        ),
+    )(starts, x, own, *blocks, bias[None])
+
+
 def put_body(place_ref, part_ref, *refs):
     refs[-1][...] = part_ref[...].astype(f32)
 
@@ -171,6 +261,28 @@
     )(*args)
 
 
+def put_blocks_body(block_ref, *out_refs):
+    cols = out_refs[0].shape[1]
+    for w, out_ref in enumerate(out_refs):
+        out_ref[...] = block_ref[0, :, w * cols : (w + 1) * cols].astype(f32)
+
+
+def put_blocks(stack):
+    count, rows, width = stack.shape
+    cols = width // 4
+    return pl.pallas_call(
+        put_blocks_body,
+        grid=(count,),
+        in_specs=[pl.BlockSpec((1, rows, width), lambda i: (i, 0, 0))],
+        out_specs=[pl.BlockSpec((rows, cols), lambda i: (0, i))] * 4,
+        out_shape=[jax.ShapeDtypeStruct((rows, count * cols), f32)] * 4,
+        compiler_params=params(),
+        cost_estimate=pl.CostEstimate(
+            flops=0, bytes_accessed=6 * count * rows * width, transcendentals=0
+        ),
+    )(stack)
+
+
 def matmul(left, right):
     return jnp.dot(left, right, preferred_element_type=f32)
 
@@ -272,13 +384,9 @@
         self.last = values
 
 
-def replica_sum_small(values):
+def replica_swap(values, step):
     count = lax.axis_size("replica")
-    step = 1
-    while step < count:
-        values = values + lax.ppermute(values, "replica", [(i, i ^ step) for i in range(count)])
-        step *= 2
-    return values
+    return lax.ppermute(values, "replica", [(i, i ^ step) for i in range(count)])
 
 
 def shards(
@@ -370,10 +478,15 @@
 
     grad_out = cotangent.astype(f32)
     branch_grad = (active * grad_out).astype(bf16)
-    tokens_all = in_order(gather_blocks(after(tokens, branch_grad)))
-
     vectors = jnp.concatenate([pre_gain, pre_shift, out_bias, mid_gain, mid_shift, down_bias])
-    vectors = vectors.reshape(2, 3 * cols)
+    extra = -(-vectors.size // width)
+    vectors = jnp.pad(vectors, (0, extra * width - vectors.size)).reshape(extra, width)
+    sent = after(jnp.concatenate([tokens, vectors]), branch_grad)
+    got = gather_blocks(sent)
+    tokens_all = in_order([block[:rows] for block in got])
+    vectors = in_order([block[rows:].reshape(1, -1)[:, : 6 * cols] for block in got])
+    vectors = vectors.reshape(count, 6, cols).transpose(1, 0, 2).reshape(6, width).astype(f32)
+    gain_one, shift_one, obias, gain_two, shift_two, dbias = (vectors[i] for i in range(6))
 
     def column_block(step, start, length):
         at = (start, (me ^ step) * cols)
@@ -382,46 +495,36 @@
         ]
         return jnp.concatenate(parts, 1)
 
-    blocks = [vectors] + [
-        jnp.concatenate([column_block(step, core * half, half), vectors])
-        for step in range(1, count)
-    ]
-    blocks = exchange(blocks)
-    arrived = jnp.stack([block[:half] for block in blocks[1:]])
-    vectors = in_order([block[-2:][None] for block in blocks]).reshape(count, 6, cols)
-    vectors = vectors.transpose(1, 0, 2).reshape(6, width).astype(f32)
-    gain_one, shift_one, obias, gain_two, shift_two, dbias = (vectors[i] for i in range(6))
-    others = core_swap(arrived)
-    qkv_weight = jnp.zeros((count, 2, half, 3 * cols), bf16)
-    for step in range(1, count):
-        for place, block in ((core, arrived), (1 - core, others)):
-            qkv_weight = lax.dynamic_update_slice(
-                qkv_weight, block[step - 1][None, None], (me ^ step, place, 0, 0)
-            )
-    own = column_block(0, 0, cols).reshape(1, 2, half, 3 * cols)
-    qkv_weight = lax.dynamic_update_slice(qkv_weight, own, (me, 0, 0, 0))
-    qkv_weight = qkv_weight.reshape(width, 3 * cols)
+    normed_all, _ = layer_norm(tokens_all.astype(f32))
+    attn_in = (normed_all * gain_one + shift_one).astype(bf16)
+    own = column_block(0, 0, cols)
+    blocks = exchange([own] + [column_block(step, core * half, half) for step in range(1, count)])
+    arrived = [after(block, attn_in, own) for block in blocks[1:]]
+    others = [core_swap(block) for block in arrived]
+    starts = [(me ^ k) * cols + core * half for k in range(1, count)]
+    starts += [(me ^ k) * cols + (1 - core) * half for k in range(1, count)]
+    starts = jnp.stack([me * cols] + starts).astype(jnp.int32)
     everyone = ("replica", "group")
     branch_wide = lax.all_gather(branch_grad, everyone, axis=0, tiled=True)
     seq = count * rows
     branch_all = lax.dynamic_slice_in_dim(branch_wide, lax.axis_index("replica") * seq, seq, 0)
 
-    normed_all, _ = layer_norm(tokens_all.astype(f32))
-    attn_in = (normed_all * gain_one + shift_one).astype(bf16)
-    qkv_bias = jnp.concatenate([query_bias, jnp.zeros_like(query_bias), value_bias]).astype(f32)
-    qkv = (matmul(attn_in, qkv_weight) + qkv_bias).astype(bf16)
+    qkv_bias = jnp.concatenate([query_bias, jnp.zeros_like(query_bias), value_bias])
+    qkv = qkv_product(attn_in, own, arrived + others, starts, qkv_bias)
     context = attention(qkv)
     attn_out = scatter_sum(matmul(context, out_weight)) + obias
     hidden = tokens.astype(f32) + active * attn_out
     normed_two, factor_two = layer_norm(hidden)
     ffn_in = (normed_two * gain_two + shift_two).astype(bf16)
     act_grad = nt(branch_all, down_weight).astype(bf16)
-    ffn_all = in_order(gather_blocks(ffn_in))
+    ffn_blocks = gather_blocks(ffn_in)
+    ffn_blocks = ffn_blocks[:1] + [after(block, act_grad) for block in ffn_blocks[1:]]
     ffn_wide = lax.all_gather(ffn_in, everyone, axis=0, tiled=True)
     here = jnp.full((1,), core, jnp.int32)
     ff = up_weight.shape[1]
-    act_low, pre_grad, _ = gelu_product(
-        ffn_all, up_weight, up_bias, act_grad, jnp.zeros((1,), jnp.int32), ff, ffn_all.shape[0], 256
+    members = (me ^ jnp.arange(count, dtype=jnp.int32)).astype(jnp.int32)
+    act_low, pre_grad, _ = gelu_product_blocks(
+        ffn_blocks, members, up_weight, up_bias, act_grad, 256
     )
     order = Order()
     order.mark(act_low, pre_grad)
@@ -440,18 +543,23 @@
     order.mark(attn_grad)
     attn_blocks = gather_blocks(attn_grad)
     branch = matmul(order(act_low), down_weight)
-    branch_sums = column_sums(branch_wide)
-    order.mark(branch, branch_sums)
+    order.mark(branch)
+    branch_sums = column_sums(order(branch_wide))
+    order.mark(branch_sums)
 
     attn_all = in_order(list(order(*attn_blocks)))
     context_grad = nt(attn_all, out_weight).astype(bf16)
-    qkv_grad = jnp.concatenate(attention_back(qkv, context_grad), 1)
+    out_part = tn(context, attn_all).astype(bf16)
+    qkv_grad = jnp.concatenate(attention_back(qkv, after(context_grad, out_part)), 1)
 
     qkv_part = tn(attn_in, qkv_grad).astype(bf16).reshape(count, cols, 3 * cols)
-    out_part = tn(context, attn_all).astype(bf16)
     out_blocks = [out_part[:, k * cols : (k + 1) * cols] for k in range(count)]
     parts = jnp.concatenate([qkv_part, jnp.stack(out_blocks)], 2)
     piece = lax.psum_scatter(parts, "replica", scatter_dimension=1, tiled=True)
+    qkv_weight = jnp.zeros((width, 3 * cols), bf16)
+    for start, block in zip([me * cols] + [starts[1 + k] for k in range(2 * count - 2)], [own] + arrived + others):
+        block = after(block, hidden)
+        qkv_weight = lax.dynamic_update_slice(qkv_weight, block, (start, 0))
     in_part = nt(after(qkv_grad, parts), qkv_weight)
     order.mark(in_part)
     in_grad = scatter_terms(in_part)
@@ -469,19 +577,37 @@
             jnp.sum(ffn_in_grad, 0),
         ]
     )
+    qkv_bias_part = column_sums(qkv_grad)
     shared = reorder(shared.reshape(4, count, cols).transpose(1, 0, 2))
-    shared = sum(exchange([shared[k] for k in range(count)]))
-    qkv_bias_part = column_sums(qkv_grad)
-    small = jnp.concatenate(
-        [
-            shared.reshape(-1),
-            lax.dynamic_slice(column_sums(attn_all), (me * cols,), (cols,)),
-            qkv_bias_part[:cols],
-            qkv_bias_part[2 * cols :],
-        ]
-    )
-    small = replica_sum_small(small)
-    small_parts = [small[k * cols : (k + 1) * cols] for k in range(7)]
+    shared, qkv_bias_part = order(shared, qkv_bias_part)
+    shared = exchange([shared[k] for k in range(count)])
+
+    def join_shared():
+        values = jnp.concatenate(
+            [
+                sum(order(*shared)).reshape(-1),
+                lax.dynamic_slice(column_sums(attn_all), (me * cols,), (cols,)),
+                qkv_bias_part[:cols],
+                qkv_bias_part[2 * cols :],
+            ]
+        )
+        order.mark(values)
+        return values, replica_swap(values, 1)
+
+    def small_step(step):
+        def run(pair):
+            values, arrived = pair
+            values = values + order(arrived)
+            order.mark(values)
+            return values if 2 * step >= replicas else (values, replica_swap(values, 2 * step))
+
+        return run
+
+    replicas = lax.axis_size("replica")
+    small_steps, step = [lambda _: join_shared()], 1
+    while step < replicas:
+        small_steps.append(small_step(step))
+        step *= 2
 
     normed_one, factor_one = layer_norm(tokens.astype(f32))
     in_grad = add_terms(order(*in_grad))
@@ -490,29 +616,38 @@
 
     down_grad = tn(order(wide_act), branch_wide).astype(bf16)
     order.mark(down_grad)
+    small = small_steps[0](None)
     piece = order(piece)
-    mixed = reorder(piece[:, :, : 3 * cols])
-    mixed = reorder(jnp.stack(exchange([mixed[k] for k in range(count)])))
-    mixed = mixed.reshape(count, -1, 3, cols).transpose(1, 2, 0, 3).reshape(-1, 3 * width)
-    piece = jnp.concatenate([mixed] + [piece[k, :, 3 * cols :] for k in range(count)], 1)
+    size = (1,) + piece.shape[1:2] + (3 * cols,)
+    sent = [lax.dynamic_slice(piece, (me ^ step, 0, 0), size) for step in range(1, count)]
+    sent = lax.optimization_barrier(tuple(sent))
+    owned = lax.optimization_barrier(tuple(swap(s, k + 1) for k, s in enumerate(sent)))
+    for step in range(1, count):
+        piece = lax.dynamic_update_slice(piece, owned[step - 1], (me ^ step, 0, 0))
     order.mark(piece)
-    attn_wgrad = lax.all_gather(piece, "replica", axis=0, tiled=True)
+    attn_wgrad = lax.all_gather(piece, "replica", axis=1, tiled=True)
+    small = small_steps[1](small)
     up_grad = tn(order(ffn_wide), wide_grad).astype(bf16)
     order.mark(up_grad)
+    branch = scatter_terms(order(branch))
     down_other, up_other = core_swap(down_grad), core_swap(up_grad)
-    down_grad = put_half(down_grad, here, 0)
-    up_grad = put_half(up_grad, here, 1)
-    down_grad = put_half(down_other, 1 - here, 0, down_grad)
+    down_grad = put_half(order(down_grad), here, 0)
+    order.mark(down_grad)
+    small = small_steps[2](small)
+    up_grad = put_half(order(up_grad), here, 1)
+    order.mark(up_grad)
+    for run in small_steps[3:]:
+        small = run(small)
+    down_grad = put_half(order(down_other), 1 - here, 0, down_grad)
     up_grad = put_half(up_other, 1 - here, 1, up_grad)
+    order.mark(down_grad, up_grad)
+    output = (hidden + active * (add_terms(order(*branch)) + dbias)).astype(bf16)
+    order.mark(output)
     up_bias_grad = core_join(wide_sums.reshape(-1), 0)
     down_bias_grad = lax.dynamic_slice(branch_sums, (me * cols,), (cols,))
 
-    branch = scatter_sum(branch) + dbias
-    output = (hidden + active * branch).astype(bf16)
-    attn_wgrad = order(attn_wgrad)
-    query_wgrad, key_wgrad, value_wgrad, out_wgrad = (
-        attn_wgrad[:, k * width : (k + 1) * width].astype(f32) for k in range(4)
-    )
+    query_wgrad, key_wgrad, value_wgrad, out_wgrad = put_blocks(order(attn_wgrad))
+    small_parts = [small[k * cols : (k + 1) * cols] for k in range(7)]
     return (
         output,
         token_grad,

time: 563 us -> 534 us (0.948)
  Pallas kernels: 96.5 us -> 117 us
  local copies, waits for them, and re-layouts: 62.9 us -> 46.5 us
  matrix products: 134 us -> 119 us
  other arithmetic: 44 us -> 34.9 us
  waiting for transfers between devices: 156 us -> 147 us
    pallas_call x0 -> x3, Pallas kernels: none -> 32.9 us  [the longest x1 13.9 us: gelu_product_blocks(): pl.pallas_call(functools.partial(gelu_blocks_body, col_tile), grid_spec=g...]
    ppermute x30, waiting for transfers between devices: 139 us -> 122 us  [swap(): return lax.ppermute(block, 'group', [(i, i ^ step) for i in range(count)])]
    all_gather x1, waiting for transfers between devices: 0.01 us -> 14 us  [shards(): attn_wgrad = lax.all_gather(piece, 'replica', axis=1, tiled=True)]
    pallas_call x2 -> x1, Pallas kernels: 46.7 us -> 34.1 us  [gelu_product(): pl.pallas_call(functools.partial(gelu_body, min(256, col_tile)), grid_spe...]
    reduce_scatter x1, waiting for transfers between devices: 16.3 us -> 5.83 us  [shards(): piece = lax.psum_scatter(parts, 'replica', scatter_dimension=1, tiled=True)]
    dot_general x3 -> x2, matrix products: 27.2 us -> 18.6 us  [matmul(): return jnp.dot(left, right, preferred_element_type=f32)]
    dynamic_update_slice x15 -> x12, local copies, waits for them, and re-layouts: 14.1 us -> 7.21 us  [in_order(): whole = lax.dynamic_update_slice(whole, block, start)]
    convert_element_type x3, other arithmetic: 12.8 us -> 5.98 us  [the longest x1 3.76 us: shards(): attn_in = (normed_all * gain_one + shift_one).astype(bf16)]
  transfers between devices with their start and end apart: 41 -> 43, of which waited for: 22 -> 20; matrix products, arithmetic and copies ran while one was open for 39% -> 37% of each run, Pallas kernels for 17% -> 20%
where the time goes in v3:
time: 534 us; the launch traced here: 525 us
  waiting for transfers between devices  147 us (28%)
  matrix products  119 us (22%)
  Pallas kernels  117 us (22%)
  local copies, waits for them, and re-layouts  46.5 us (9%)
  starting transfers between devices  43.9 us (8%)
  other arithmetic  34.9 us (7%)
  between operations  15.8 us (3%)
    ppermute x30, waiting for transfers between devices, swap(): return lax.ppermute(block, 'group', [(i, i ^ step) for i in range(count)])  122 us
    dot_general x4, matrix products, tn(): lax.dot_general(left, right, (((0,), (0,)), ((), ())), preferred_element_...  52.6 us
    dot_general x5, matrix products, nt(): lax.dot_general(left, right, (((1,), (1,)), ((), ())), preferred_element_...  48.1 us
    ppermute x30, starting transfers between devices, swap(): return lax.ppermute(block, 'group', [(i, i ^ step) for i in range(count)])  37.6 us
    pallas_call x1, Pallas kernels, gelu_product(): pl.pallas_call(functools.partial(gelu_body, min(256, col_tile)), grid_spe...  34.1 us
    pallas_call x4, Pallas kernels, put_half(): pl.pallas_call(put_body, grid_spec=pltpu.PrefetchScalarGridSpec(num_scala...  26.6 us
    dot_general x2, matrix products, matmul(): return jnp.dot(left, right, preferred_element_type=f32)  18.6 us
    pallas_call x1, Pallas kernels, attention_back(): pl.pallas_call(attend_back_body, grid=(pairs,), in_specs=[spec(0), spec(1...  14.6 us
  transfers between devices with their start and end apart: 43, of which 20 were waited for; matrix products, arithmetic and copies ran while one was open for 37% of the time, Pallas kernels for 20%

profile of v3, /device:TPU:0, one launch (start us, length us, event | category | flops | bytes accessed | tf_op | source)
XLA Modules:
  0.0 524.6 jit_solution(5086144708762918311)
XLA Ops:
  17.0 4.0 collective-permute-start.2
  37.6 13.3 %collective-permute-done = bf16[130,2048]{1,0:T(8,128)(2,1)} collective-permute-done((bf16[130,2048]{1,0:T(8,128)(2,1)S(1)}, bf16[130,2048]{1,0:T(8,128)(2,1)}, u32[]{:S(2)}, u32[]{:S(2)}) %collective-permute-start) | collective-permute-done | bytes 532512 | tf_op jit(solution)/shard_map/ppermute | solution.py:296
  65.7 3.8 fusion.5.x_ref
  69.5 28.6 %collective-permute-done.5.refs_2_ = bf16[256,1536]{1,0:T(8,128)(2,1)} collective-permute-done((bf16[256,1536]{1,0:T(8,128)(2,1)}, bf16[256,1536]{1,0:T(8,128)(2,1)}, u32[]{:S(2)}, u32[]{:S(2)}) %collective-permute-start.5) | collective-permute-done | bytes 786464 | tf_op jit(solution)/shard_map/ppermute | solution.py:296
  103.0 9.6 %shard_map.314.q_ref.k_ref.v_ref = bf16[512,1536]{1,0:T(8,128)(2,1)} custom-call(s32[7]{0:T(128)} %stack.61.at_ref, bf16[512,2048]{1,0:T(8,128)(2,1)} %fusion.5.x_ref, bf16[512,1536]{1,0:T(8,128)(2,1)} %pad_maximum_fusion.own_ref, bf16[256,1536]{1,0:T(8,128)(2,1)} %collective-permute-done.3.refs_0_, bf16[256,1536]{1,0:T(8,128)(2,1)} %collective-permute-done.4.refs_1_, ...), custom_call_target="tpu_custom_call" | custom-call | flops 3221225472 | bytes 9961472 | tf_op jit(solution)/shard_map/pallas_call | solution.py:221
  112.6 8.6 %shard_map.315 = bf16[512,512]{1,0:T(8,128)(2,1)} custom-call(bf16[512,1536]{1,0:T(8,128)(2,1)} %shard_map.314.q_ref.k_ref.v_ref, bf16[512,1536]{1,0:T(8,128)(2,1)} %shard_map.314.q_ref.k_ref.v_ref, bf16[512,1536]{1,0:T(8,128)(2,1)} %shard_map.314.q_ref.k_ref.v_ref), custom_call_target="tpu_custom_call" | custom-call | flops 536870912 | bytes 2097152 | tf_op jit(solution)/shard_map/pallas_call | solution.py:93
  127.6 19.3 %collective-permute-done.9 = bf16[128,2048]{1,0:T(8,128)(2,1)S(1)} collective-permute-done((bf16[128,2048]{1,0:T(8,128)(2,1)S(1)}, bf16[128,2048]{1,0:T(8,128)(2,1)S(1)}, u32[]{:S(2)}, u32[]{:S(2)}) %collective-permute-start.9) | collective-permute-done | bytes 524320 | tf_op jit(solution)/shard_map/ppermute | solution.py:296
  146.9 11.9 %collective-permute-done.11 = bf16[128,2048]{1,0:T(8,128)(2,1)S(1)} collective-permute-done((bf16[128,2048]{1,0:T(8,128)(2,1)S(1)}, bf16[128,2048]{1,0:T(8,128)(2,1)S(1)}, u32[]{:S(2)}, u32[]{:S(2)}) %collective-permute-start.11) | collective-permute-done | bytes 524320 | tf_op jit(solution)/shard_map/ppermute | solution.py:296
  165.7 9.9 %convolution_convert_fusion.6.refs_6_ = bf16[512,2048]{1,0:T(8,128)(2,1)} fusion(bf16[2048,2048]{1,0:T(8,128)(2,1)} %param.35, bf16[4096,2048]{1,0:T(8,128)(2,1)} %all-gather.4.cloned.1.call-done, s32[]{:T(128)S(6)} %select_n.159), kind=kOutput, calls=%fused_computation.21 | convolution fusion | flops 4296015872 | bytes 12582916 | tf_op jit(solution)/shard_map/dot_general | solution.py:37
  178.2 13.2 %collective-permute-done.13.refs_2_ = bf16[128,2048]{1,0:T(8,128)(2,1)} collective-permute-done((bf16[128,2048]{1,0:T(8,128)(2,1)}, bf16[128,2048]{1,0:T(8,128)(2,1)}, u32[]{:S(2)}, u32[]{:S(2)}) %collective-permute-start.13) | collective-permute-done | bytes 524320 | tf_op jit(solution)/shard_map/ppermute | solution.py:296
  191.4 13.9 %shard_map.316 = (bf16[512,2048]{1,0:T(8,128)(2,1)}, bf16[512,2048]{1,0:T(8,128)(2,1)}, f32[1,2048]{1,0:T(1,128)}) custom-call(s32[4]{0:T(128)} %iota_xor_fusion.member_ref, bf16[128,2048]{1,0:T(8,128)(2,1)} %add_convert_fusion.1.refs_0_, bf16[128,2048]{1,0:T(8,128)(2,1)} %collective-permute-done.12.refs_1_, ...), custom_call_target="tpu_custom_call" | custom-call | flops 4294967296 | bytes 16777216 | tf_op jit(solution)/shard_map/pallas_call | solution.py:190
  205.3 8.7 %convolution_convert_fusion.5 = bf16[512,2048]{1,0:T(8,128)(2,1)S(1)} fusion(bf16[512,2048]{1,0:T(8,128)(2,1)} %get-tuple-element.96, bf16[2048,2048]{1,0:T(8,128)(2,1)} %refs_1_.1), kind=kOutput, calls=%fused_computation.20 | convolution fusion | flops 4296015872 | bytes 12582912 | tf_op jit(solution)/shard_map/dot_general | solution.py:37
  217.8 22.3 %convolution_convert_fusion.1.refs_3_ = bf16[4096,1024]{1,0:T(8,128)(2,1)} fusion(bf16[4096,2048]{1,0:T(8,128)(2,1)} %all-gather.4.cloned.1.call-done, bf16[2048,2048]{1,0:T(8,128)(2,1)S(1)} %bitcast.112, s32[]{:T(128)S(6)} %select_n.160), kind=kOutput, calls=%fused_computation.3 | convolution fusion | flops 17184063488 | bytes 29360132 | tf_op jit(solution)/shard_map/dot_general | solution.py:37
  240.1 8.2 %collective-permute-done.16 = bf16[128,2048]{1,0:T(8,128)(2,1)S(1)} collective-permute-done((bf16[128,2048]{1,0:T(8,128)(2,1)S(1)}, bf16[128,2048]{1,0:T(8,128)(2,1)S(1)}, u32[]{:S(2)}, u32[]{:S(2)}) %collective-permute-start.16) | collective-permute-done | bytes 524320 | tf_op jit(solution)/shard_map/ppermute | solution.py:296
  254.8 16.2 %fusion.34 = f32[512,2048]{1,0:T(8,128)} fusion(bf16[512,2048]{1,0:T(8,128)(2,1)S(1)} %copy-done.21, bf16[2048,2048]{1,0:T(8,128)(2,1)S(1)} %bitcast.112), kind=kOutput, calls=%fused_computation.143 | convolution fusion | flops 4294967296 | bytes 14680064 | tf_op jit(solution)/shard_map/dot_general | solution.py:287
  271.0 4.5 convert_reduce_fusion
  278.2 10.3 %collective-permute-done.19 = bf16[128,2048]{1,0:T(8,128)(2,1)S(1)} collective-permute-done((bf16[128,2048]{1,0:T(8,128)(2,1)S(1)}, bf16[128,2048]{1,0:T(8,128)(2,1)S(1)}, u32[]{:S(2)}, u32[]{:S(2)}) %collective-permute-start.19) | collective-permute-done | bytes 524320 | tf_op jit(solution)/shard_map/ppermute | solution.py:296
  288.5 4.4 collective-permute-done.18
  296.9 14.6 %shard_map.317 = (bf16[512,512]{1,0:T(8,128)(2,1)}, bf16[512,512]{1,0:T(8,128)(2,1)}, bf16[512,512]{1,0:T(8,128)(2,1)}) custom-call(bf16[512,1536]{1,0:T(8,128)(2,1)} %shard_map.314.q_ref.k_ref.v_ref, bf16[512,1536]{1,0:T(8,128)(2,1)} %shard_map.314.q_ref.k_ref.v_ref, bf16[512,1536]{1,0:T(8,128)(2,1)} %shard_map.314.q_ref.k_ref.v_ref, ...), custom_call_target="tpu_custom_call" | custom-call | flops 1342177280 | bytes 3670016 | tf_op jit(solution)/shard_map/pallas_call | solution.py:106
  315.2 3.7 convolution_convert_fusion
  319.0 4.0 maximum_maximum_fusion
  331.5 5.2 fusion.6
  341.9 34.1 %shard_map.318 = (bf16[4096,1024]{1,0:T(8,128)(2,1)}, bf16[4096,1024]{1,0:T(8,128)(2,1)}, f32[1,1024]{1,0:T(1,128)}) custom-call(s32[1]{0:T(128)} %bitcast.27.place_ref, bf16[4096,2048]{1,0:T(8,128)(2,1)} %all-gather.6.cloned.1.call-done.refs_0_, bf16[2048,2048]{1,0:T(8,128)(2,1)} %refs_1_.1, bf16[1,2048]{1,0:T(2,128)(2,1)} %broadcast_in_dim.15.refs_5_.refs_2_, ...), custom_call_target="tpu_custom_call" | custom-call | flops 17179869184 | bytes 46137344 | tf_op jit(solution)/shard_map/pallas_call | solution.py:150
  382.8 23.9 %convolution_convert_fusion.3.part_ref = bf16[1024,2048]{1,0:T(8,128)(2,1)} fusion(bf16[4096,1024]{1,0:T(8,128)(2,1)} %get-tuple-element.128, bf16[4096,2048]{1,0:T(8,128)(2,1)} %all-gather.4.cloned.1.call-done), kind=kOutput, calls=%fused_computation.17 | convolution fusion | flops 17181966336 | bytes 29360128 | tf_op jit(solution)/shard_map/dot_general | solution.py:39
  406.7 5.8 %reduce-scatter.2.cloned.1.call-done = bf16[4,64,2048]{2,1,0:T(8,128)(2,1)} async-done(((bf16[4,512,2048]{2,1,0:T(8,128)(2,1)}), bf16[4,64,2048]{2,1,0:T(8,128)(2,1)}) %reduce-scatter.2.cloned.1.call-update) | async-done | bytes 1048592 | tf_op jit(solution)/shard_map/reduce_scatter | solution.py:558
  427.4 23.7 %convolution_convert_fusion.2.part_ref = bf16[2048,1024]{1,0:T(8,128)(2,1)} fusion(bf16[4096,2048]{1,0:T(8,128)(2,1)} %all-gather.6.cloned.1.call-done.refs_0_, bf16[4096,1024]{1,0:T(8,128)(2,1)} %get-tuple-element.122), kind=kOutput, calls=%fused_computation.16 | convolution fusion | flops 17181966336 | bytes 29360128 | tf_op jit(solution)/shard_map/dot_general | solution.py:39
  455.9 6.0 %shard_map.319.refs_0_ = f32[2048,2048]{1,0:T(8,128)} custom-call(s32[1]{0:T(128)} %bitcast.27.place_ref, bf16[1024,2048]{1,0:T(8,128)(2,1)} %convolution_convert_fusion.3.part_ref), custom_call_target="tpu_custom_call" | custom-call | bytes 12582912 | tf_op jit(solution)/shard_map/pallas_call | solution.py:257
  471.8 7.3 %shard_map.320.refs_0_ = f32[2048,2048]{1,0:T(8,128)} custom-call(s32[1]{0:T(128)} %bitcast.27.place_ref, bf16[2048,1024]{1,0:T(8,128)(2,1)} %convolution_convert_fusion.2.part_ref), custom_call_target="tpu_custom_call" | custom-call | bytes 12582912 | tf_op jit(solution)/shard_map/pallas_call | solution.py:257
  479.1 6.0 %shard_map.321 = f32[2048,2048]{1,0:T(8,128)} custom-call(s32[1]{0:T(128)S(6)} %sub.68.place_ref, bf16[1024,2048]{1,0:T(8,128)(2,1)} %collective-permute-done.34.part_ref, f32[2048,2048]{1,0:T(8,128)} %shard_map.319.refs_0_), custom_call_target="tpu_custom_call", output_to_operand_aliasing={{}: (2, {})} | custom-call | bytes 12582912 | tf_op jit(solution)/shard_map/pallas_call | solution.py:257
  485.8 7.3 %shard_map.322 = f32[2048,2048]{1,0:T(8,128)} custom-call(s32[1]{0:T(128)S(6)} %sub.68.place_ref, bf16[2048,1024]{1,0:T(8,128)(2,1)} %collective-permute-done.37.part_ref, f32[2048,2048]{1,0:T(8,128)} %shard_map.320.refs_0_), custom_call_target="tpu_custom_call", output_to_operand_aliasing={{}: (2, {})} | custom-call | bytes 12582912 | tf_op jit(solution)/shard_map/pallas_call | solution.py:257
  494.3 14.0 %all-gather.8.cloned.1.call-done.block_ref = bf16[4,512,2048]{2,1,0:T(8,128)(2,1)} async-done(((bf16[4,64,2048]{2,1,0:T(8,128)(2,1)}), bf16[4,512,2048]{2,1,0:T(8,128)(2,1)}) %all-gather.8.cloned.1.call-update) | async-done | bytes 8388624 | tf_op jit(solution)/shard_map/all_gather | solution.py:628
  508.3 9.4 %shard_map.323 = (f32[512,2048]{1,0:T(8,128)}, f32[512,2048]{1,0:T(8,128)}, f32[512,2048]{1,0:T(8,128)}, f32[512,2048]{1,0:T(8,128)}) custom-call(bf16[4,512,2048]{2,1,0:T(8,128)(2,1)} %all-gather.8.cloned.1.call-done.block_ref), custom_call_target="tpu_custom_call" | custom-call | bytes 25165824 | tf_op jit(solution)/shard_map/pallas_call | solution.py:273
  (256 shorter events, 133.2 us)
Async XLA Ops:
  7.2 158.5 %all-gather.4.cloned.1.call-start = ((), (), s32[]{:S(2)}) async-start(), calls=%async_computation.1 | async-start | bytes 17301504 | tf_op jit(solution)/shard_map/all_gather | solution.py:508
  10.7 331.1 %all-gather.6.cloned.1.call-start = ((), (), s32[]{:S(2)}) async-start(), calls=%async_computation.2 | async-start | bytes 17301504 | tf_op jit(solution)/shard_map/all_gather | solution.py:522
  17.0 39.0 %collective-permute-start.2 = (bf16[130,2048]{1,0:T(8,128)(2,1)S(1)}, bf16[130,2048]{1,0:T(8,128)(2,1)}, u32[]{:S(2)}, u32[]{:S(2)}) collective-permute-start(bf16[130,2048]{1,0:T(8,128)(2,1)S(1)} %pad_maximum_fusion.4), channel_id=1, source_target_pairs={{0,3},{1,2},{2,1},{3,0},{4,7},{5,6},{6,5},{7,4},{8,11},{9,10},{10,... | collective-permute-start | bytes 1597448 | tf_op jit(solution)/shard_map/ppermute | solution.py:296
  21.0 33.2 %collective-permute-start.1 = (bf16[130,2048]{1,0:T(8,128)(2,1)S(1)}, bf16[130,2048]{1,0:T(8,128)(2,1)}, u32[]{:S(2)}, u32[]{:S(2)}) collective-permute-start(bf16[130,2048]{1,0:T(8,128)(2,1)S(1)} %pad_maximum_fusion.4), channel_id=1, source_target_pairs={{0,2},{1,3},{2,0},{3,1},{4,6},{5,7},{6,4},{7,5},{8,10},{9,11},{10,... | collective-permute-start | bytes 1597448 | tf_op jit(solution)/shard_map/ppermute | solution.py:296
  21.5 29.4 %collective-permute-start = (bf16[130,2048]{1,0:T(8,128)(2,1)S(1)}, bf16[130,2048]{1,0:T(8,128)(2,1)}, u32[]{:S(2)}, u32[]{:S(2)}) collective-permute-start(bf16[130,2048]{1,0:T(8,128)(2,1)S(1)} %pad_maximum_fusion.4), channel_id=1, source_target_pairs={{0,1},{1,0},{2,3},{3,2},{4,5},{5,4},{6,7},{7,6},{8,9},{9,8},{10,11... | collective-permute-start | bytes 1597448 | tf_op jit(solution)/shard_map/ppermute | solution.py:296
  26.1 72.0 %collective-permute-start.4 = (bf16[256,1536]{1,0:T(8,128)(2,1)}, bf16[256,1536]{1,0:T(8,128)(2,1)}, u32[]{:S(2)}, u32[]{:S(2)}) collective-permute-start(bf16[256,1536]{1,0:T(8,128)(2,1)} %pad_maximum_fusion.2), channel_id=1, source_target_pairs={{0,2},{1,3},{2,0},{3,1},{4,6},{5,7},{6,4},{7,5},{8,10},{9,11},{10,... | collective-permute-start | bytes 2359304 | tf_op jit(solution)/shard_map/ppermute | solution.py:296
  28.9 69.2 %collective-permute-start.3 = (bf16[256,1536]{1,0:T(8,128)(2,1)}, bf16[256,1536]{1,0:T(8,128)(2,1)}, u32[]{:S(2)}, u32[]{:S(2)}) collective-permute-start(bf16[256,1536]{1,0:T(8,128)(2,1)} %pad_maximum_fusion.1), channel_id=1, source_target_pairs={{0,1},{1,0},{2,3},{3,2},{4,5},{5,4},{6,7},{7,6},{8,9},{9,8},{10,11... | collective-permute-start | bytes 2359304 | tf_op jit(solution)/shard_map/ppermute | solution.py:296
  50.9 47.2 %collective-permute-start.5 = (bf16[256,1536]{1,0:T(8,128)(2,1)}, bf16[256,1536]{1,0:T(8,128)(2,1)}, u32[]{:S(2)}, u32[]{:S(2)}) collective-permute-start(bf16[256,1536]{1,0:T(8,128)(2,1)} %pad_maximum_fusion.3), channel_id=1, source_target_pairs={{0,3},{1,2},{2,1},{3,0},{4,7},{5,6},{6,5},{7,4},{8,11},{9,10},{10,... | collective-permute-start | bytes 2359304 | tf_op jit(solution)/shard_map/ppermute | solution.py:296
  123.9 23.0 %collective-permute-start.9 = (bf16[128,2048]{1,0:T(8,128)(2,1)S(1)}, bf16[128,2048]{1,0:T(8,128)(2,1)S(1)}, u32[]{:S(2)}, u32[]{:S(2)}) collective-permute-start(bf16[128,2048]{1,0:T(8,128)(2,1)S(1)} %get-tuple-element.179), channel_id=1, source_target_pairs={{0,1},{1,0},{2,3},{3,2},{4,5},{5,4},{6,7},{7,6},{8,9},{9,8},{10,11... | collective-permute-start | bytes 1572872 | tf_op jit(solution)/shard_map/ppermute | solution.py:296
  125.7 33.1 %collective-permute-start.11 = (bf16[128,2048]{1,0:T(8,128)(2,1)S(1)}, bf16[128,2048]{1,0:T(8,128)(2,1)S(1)}, u32[]{:S(2)}, u32[]{:S(2)}) collective-permute-start(bf16[128,2048]{1,0:T(8,128)(2,1)S(1)} %get-tuple-element.180), channel_id=1, source_target_pairs={{0,3},{1,2},{2,1},{3,0},{4,7},{5,6},{6,5},{7,4},{8,11},{9,10},{10,... | collective-permute-start | bytes 1572872 | tf_op jit(solution)/shard_map/ppermute | solution.py:296
  127.2 31.6 %collective-permute-start.10 = (bf16[128,2048]{1,0:T(8,128)(2,1)S(1)}, bf16[128,2048]{1,0:T(8,128)(2,1)S(1)}, u32[]{:S(2)}, u32[]{:S(2)}) collective-permute-start(bf16[128,2048]{1,0:T(8,128)(2,1)S(1)} %get-tuple-element.181), channel_id=1, source_target_pairs={{0,2},{1,3},{2,0},{3,1},{4,6},{5,7},{6,4},{7,5},{8,10},{9,11},{10,... | collective-permute-start | bytes 1572872 | tf_op jit(solution)/shard_map/ppermute | solution.py:296
  160.8 251.8 %reduce-scatter.2.cloned.1.call-start = ((), (), s32[]{:S(2)}) async-start(), calls=%async_computation.3 | async-start | bytes 9437184 | tf_op jit(solution)/shard_map/reduce_scatter | solution.py:558
  162.6 28.8 %collective-permute-start.13 = (bf16[128,2048]{1,0:T(8,128)(2,1)}, bf16[128,2048]{1,0:T(8,128)(2,1)}, u32[]{:S(2)}, u32[]{:S(2)}) collective-permute-start(bf16[128,2048]{1,0:T(8,128)(2,1)} %add_convert_fusion.1.refs_0_), channel_id=1, source_target_pairs={{0,2},{1,3},{2,0},{3,1},{4,6},{5,7},{6,4},{7,5},{8,10},{9,11},{10,... | collective-permute-start | bytes 1572872 | tf_op jit(solution)/shard_map/ppermute | solution.py:296
  164.2 27.2 %collective-permute-start.12 = (bf16[128,2048]{1,0:T(8,128)(2,1)}, bf16[128,2048]{1,0:T(8,128)(2,1)}, u32[]{:S(2)}, u32[]{:S(2)}) collective-permute-start(bf16[128,2048]{1,0:T(8,128)(2,1)} %add_convert_fusion.1.refs_0_), channel_id=1, source_target_pairs={{0,1},{1,0},{2,3},{3,2},{4,5},{5,4},{6,7},{7,6},{8,9},{9,8},{10,11... | collective-permute-start | bytes 1572872 | tf_op jit(solution)/shard_map/ppermute | solution.py:296
  214.2 25.8 %collective-permute-start.17 = (bf16[128,2048]{1,0:T(8,128)(2,1)S(1)}, bf16[128,2048]{1,0:T(8,128)(2,1)S(1)}, u32[]{:S(2)}, u32[]{:S(2)}) collective-permute-start(bf16[128,2048]{1,0:T(8,128)(2,1)S(1)} %get-tuple-element.186), channel_id=1, source_target_pairs={{0,3},{1,2},{2,1},{3,0},{4,7},{5,6},{6,5},{7,4},{8,11},{9,10},{10,... | collective-permute-start | bytes 1572872 | tf_op jit(solution)/shard_map/ppermute | solution.py:296
  215.8 32.4 %collective-permute-start.16 = (bf16[128,2048]{1,0:T(8,128)(2,1)S(1)}, bf16[128,2048]{1,0:T(8,128)(2,1)S(1)}, u32[]{:S(2)}, u32[]{:S(2)}) collective-permute-start(bf16[128,2048]{1,0:T(8,128)(2,1)S(1)} %get-tuple-element.187), channel_id=1, source_target_pairs={{0,2},{1,3},{2,0},{3,1},{4,6},{5,7},{6,4},{7,5},{8,10},{9,11},{10,... | collective-permute-start | bytes 1572872 | tf_op jit(solution)/shard_map/ppermute | solution.py:296
  217.3 31.7 %collective-permute-start.15 = (bf16[128,2048]{1,0:T(8,128)(2,1)S(1)}, bf16[128,2048]{1,0:T(8,128)(2,1)S(1)}, u32[]{:S(2)}, u32[]{:S(2)}) collective-permute-start(bf16[128,2048]{1,0:T(8,128)(2,1)S(1)} %get-tuple-element.188), channel_id=1, source_target_pairs={{0,1},{1,0},{2,3},{3,2},{4,5},{5,4},{6,7},{7,6},{8,9},{9,8},{10,11... | collective-permute-start | bytes 1572872 | tf_op jit(solution)/shard_map/ppermute | solution.py:296
  251.3 26.9 %collective-permute-start.20 = (bf16[128,2048]{1,0:T(8,128)(2,1)S(1)}, bf16[128,2048]{1,0:T(8,128)(2,1)S(1)}, u32[]{:S(2)}, u32[]{:S(2)}) collective-permute-start(bf16[128,2048]{1,0:T(8,128)(2,1)S(1)} %get-tuple-element.104), channel_id=1, source_target_pairs={{0,3},{1,2},{2,1},{3,0},{4,7},{5,6},{6,5},{7,4},{8,11},{9,10},{10,... | collective-permute-start | bytes 1572872 | tf_op jit(solution)/shard_map/ppermute | solution.py:296
  252.7 35.8 %collective-permute-start.19 = (bf16[128,2048]{1,0:T(8,128)(2,1)S(1)}, bf16[128,2048]{1,0:T(8,128)(2,1)S(1)}, u32[]{:S(2)}, u32[]{:S(2)}) collective-permute-start(bf16[128,2048]{1,0:T(8,128)(2,1)S(1)} %get-tuple-element.104), channel_id=1, source_target_pairs={{0,2},{1,3},{2,0},{3,1},{4,6},{5,7},{6,4},{7,5},{8,10},{9,11},{10,... | collective-permute-start | bytes 1572872 | tf_op jit(solution)/shard_map/ppermute | solution.py:296
  253.4 39.6 %collective-permute-start.18 = (bf16[128,2048]{1,0:T(8,128)(2,1)S(1)}, bf16[128,2048]{1,0:T(8,128)(2,1)S(1)}, u32[]{:S(2)}, u32[]{:S(2)}) collective-permute-start(bf16[128,2048]{1,0:T(8,128)(2,1)S(1)} %get-tuple-element.104), channel_id=1, source_target_pairs={{0,1},{1,0},{2,3},{3,2},{4,5},{5,4},{6,7},{7,6},{8,9},{9,8},{10,11... | collective-permute-start | bytes 1572872 | tf_op jit(solution)/shard_map/ppermute | solution.py:296
  322.9 185.3 %all-gather.8.cloned.1.call-start = ((), (), s32[]{:S(2)}) async-start(), calls=%async_computation.4 | async-start | bytes 9437184 | tf_op jit(solution)/shard_map/all_gather | solution.py:628
  337.9 38.1 %collective-permute-start.26 = (bf16[128,2048]{1,0:T(8,128)(2,1)}, bf16[128,2048]{1,0:T(8,128)(2,1)}, u32[]{:S(2)}, u32[]{:S(2)}) collective-permute-start(bf16[128,2048]{1,0:T(8,128)(2,1)} %get-tuple-element.176), channel_id=1, source_target_pairs={{0,3},{1,2},{2,1},{3,0},{4,7},{5,6},{6,5},{7,4},{8,11},{9,10},{10,... | collective-permute-start | bytes 1572872 | tf_op jit(solution)/shard_map/ppermute | solution.py:296
  339.3 36.7 %collective-permute-start.25 = (bf16[128,2048]{1,0:T(8,128)(2,1)}, bf16[128,2048]{1,0:T(8,128)(2,1)}, u32[]{:S(2)}, u32[]{:S(2)}) collective-permute-start(bf16[128,2048]{1,0:T(8,128)(2,1)} %get-tuple-element.177), channel_id=1, source_target_pairs={{0,2},{1,3},{2,0},{3,1},{4,6},{5,7},{6,4},{7,5},{8,10},{9,11},{10,... | collective-permute-start | bytes 1572872 | tf_op jit(solution)/shard_map/ppermute | solution.py:296
  339.7 36.3 %collective-permute-start.24 = (bf16[128,2048]{1,0:T(8,128)(2,1)S(1)}, bf16[128,2048]{1,0:T(8,128)(2,1)}, u32[]{:S(2)}, u32[]{:S(2)}) collective-permute-start(bf16[128,2048]{1,0:T(8,128)(2,1)S(1)} %get-tuple-element.178), channel_id=1, source_target_pairs={{0,1},{1,0},{2,3},{3,2},{4,5},{5,4},{6,7},{7,6},{8,9},{9,8},{10,11... | collective-permute-start | bytes 1572872 | tf_op jit(solution)/shard_map/ppermute | solution.py:296
  379.3 27.4 %collective-permute-start.23 = (f32[4,512]{1,0:T(4,128)S(1)}, f32[4,512]{1,0:T(4,128)S(1)}, u32[]{:S(2)}, u32[]{:S(2)}) collective-permute-start(f32[4,512]{1,0:T(4,128)S(1)} %get-tuple-element.209), channel_id=1, source_target_pairs={{0,3},{1,2},{2,1},{3,0},{4,7},{5,6},{6,5},{7,4},{8,11},{9,10},{10,... | collective-permute-start | bytes 24584 | tf_op jit(solution)/shard_map/ppermute | solution.py:296
  380.7 25.9 %collective-permute-start.22 = (f32[4,512]{1,0:T(4,128)S(1)}, f32[4,512]{1,0:T(4,128)S(1)}, u32[]{:S(2)}, u32[]{:S(2)}) collective-permute-start(f32[4,512]{1,0:T(4,128)S(1)} %get-tuple-element.210), channel_id=1, source_target_pairs={{0,2},{1,3},{2,0},{3,1},{4,6},{5,7},{6,4},{7,5},{8,10},{9,11},{10,... | collective-permute-start | bytes 24584 | tf_op jit(solution)/shard_map/ppermute | solution.py:296
  381.2 25.5 %collective-permute-start.21 = (f32[4,512]{1,0:T(4,128)S(1)}, f32[4,512]{1,0:T(4,128)S(1)}, u32[]{:S(2)}, u32[]{:S(2)}) collective-permute-start(f32[4,512]{1,0:T(4,128)S(1)} %get-tuple-element.211), channel_id=1, source_target_pairs={{0,1},{1,0},{2,3},{3,2},{4,5},{5,4},{6,7},{7,6},{8,9},{9,8},{10,11... | collective-permute-start | bytes 24584 | tf_op jit(solution)/shard_map/ppermute | solution.py:296
  426.2 52.9 %collective-permute-start.34 = (bf16[1024,2048]{1,0:T(8,128)(2,1)}, bf16[1024,2048]{1,0:T(8,128)(2,1)}, u32[]{:S(2)}, u32[]{:S(2)}) collective-permute-start(bf16[1024,2048]{1,0:T(8,128)(2,1)} %convolution_convert_fusion.3.part_ref), channel_id=1, source_target_pairs={{0,4},{4,0},{8,12},{12,8},{16,20},{20,16},{24,28},{28,24},{1,5},{5... | collective-permute-start | bytes 12582920 | tf_op jit(solution)/shard_map/ppermute | solution.py:364
  451.1 34.6 %collective-permute-start.37 = (bf16[2048,1024]{1,0:T(8,128)(2,1)}, bf16[2048,1024]{1,0:T(8,128)(2,1)}, u32[]{:S(2)}, u32[]{:S(2)}) collective-permute-start(bf16[2048,1024]{1,0:T(8,128)(2,1)} %convolution_convert_fusion.2.part_ref), channel_id=1, source_target_pairs={{0,4},{4,0},{8,12},{12,8},{16,20},{20,16},{24,28},{28,24},{1,5},{5... | collective-permute-start | bytes 12582920 | tf_op jit(solution)/shard_map/ppermute | solution.py:364
  466.4 26.7 %collective-permute-start.33 = (bf16[128,2048]{1,0:T(8,128)(2,1)S(1)}, bf16[128,2048]{1,0:T(8,128)(2,1)S(1)}, u32[]{:S(2)}, u32[]{:S(2)}) collective-permute-start(bf16[128,2048]{1,0:T(8,128)(2,1)S(1)} %get-tuple-element.173), channel_id=1, source_target_pairs={{0,3},{1,2},{2,1},{3,0},{4,7},{5,6},{6,5},{7,4},{8,11},{9,10},{10,... | collective-permute-start | bytes 1572872 | tf_op jit(solution)/shard_map/ppermute | solution.py:296
  467.9 25.1 %collective-permute-start.32 = (bf16[128,2048]{1,0:T(8,128)(2,1)S(1)}, bf16[128,2048]{1,0:T(8,128)(2,1)S(1)}, u32[]{:S(2)}, u32[]{:S(2)}) collective-permute-start(bf16[128,2048]{1,0:T(8,128)(2,1)S(1)} %get-tuple-element.174), channel_id=1, source_target_pairs={{0,2},{1,3},{2,0},{3,1},{4,6},{5,7},{6,4},{7,5},{8,10},{9,11},{10,... | collective-permute-start | bytes 1572872 | tf_op jit(solution)/shard_map/ppermute | solution.py:296
  469.1 24.0 %collective-permute-start.31 = (bf16[128,2048]{1,0:T(8,128)(2,1)S(1)}, bf16[128,2048]{1,0:T(8,128)(2,1)S(1)}, u32[]{:S(2)}, u32[]{:S(2)}) collective-permute-start(bf16[128,2048]{1,0:T(8,128)(2,1)S(1)} %get-tuple-element.175), channel_id=1, source_target_pairs={{0,1},{1,0},{2,3},{3,2},{4,5},{5,4},{6,7},{7,6},{8,9},{9,8},{10,11... | collective-permute-start | bytes 1572872 | tf_op jit(solution)/shard_map/ppermute | solution.py:296
  (39 other events, 576.8 us)
Sparse Core Ops, SparseCore 0:
  11.5 152.7 all-gather.3
  167.7 145.9 all-gather.5
  323.1 89.4 reduce-scatter.1
  426.2 82.0 all-gather.7

commit v4 on v3

--- a/solution.py
+++ b/solution.py
@@ -153,6 +153,33 @@
         compiler_params=params(),
         cost_estimate=pl.CostEstimate(flops=2 * rows * depth * width, bytes_accessed=2 * (rows * depth + depth * width + 3 * rows * width), transcendentals=rows * width),
     )(place, x, weight, bias[None], grad)
+
+def parts_body(x_ref, q_ref, k_ref, v_ref, context_ref, grad_ref, out_ref):
+    cols = q_ref.shape[1]
+    for w, ref in enumerate((q_ref, k_ref, v_ref)):
+        out_ref[0, :, w * cols : (w + 1) * cols] = tn(x_ref[...], ref[...]).astype(bf16)
+    out_ref[0, :, 3 * cols :] = tn(context_ref[...], grad_ref[...]).astype(bf16)
+
+
+def weight_parts(x, query_grad, key_grad, value_grad, context, grad):
+    rows, cols = context.shape
+    count = x.shape[1] // cols
+    whole = pl.BlockSpec((rows, cols), lambda i: (0, 0))
+    block = pl.BlockSpec((rows, cols), lambda i: (0, i))
+    return pl.pallas_call(
+        parts_body,
+        grid=(count,),
+        in_specs=[block, whole, whole, whole, whole, block],
+        out_specs=pl.BlockSpec((1, cols, 4 * cols), lambda i: (i, 0, 0)),
+        out_shape=jax.ShapeDtypeStruct((count, cols, 4 * cols), bf16),
+        compiler_params=params(),
+        cost_estimate=pl.CostEstimate(
+            flops=8 * count * rows * cols * cols,
+            bytes_accessed=2 * (2 * rows * count * cols + 4 * rows * cols + 4 * count * cols * cols),
+            transcendentals=0,
+        ),
+    )(x, query_grad, key_grad, value_grad, context, grad)
+
 
 def gelu_blocks_body(tile, member_ref, *refs):
     count = len(refs) - 7
@@ -272,9 +299,9 @@
     cols = width // 4
     return pl.pallas_call(
         put_blocks_body,
-        grid=(count,),
-        in_specs=[pl.BlockSpec((1, rows, width), lambda i: (i, 0, 0))],
-        out_specs=[pl.BlockSpec((rows, cols), lambda i: (0, i))] * 4,
+        grid=(count, 2),
+        in_specs=[pl.BlockSpec((1, rows // 2, width), lambda i, h: (i, h, 0))],
+        out_specs=[pl.BlockSpec((rows // 2, cols), lambda i, h: (h, i))] * 4,
         out_shape=[jax.ShapeDtypeStruct((rows, count * cols), f32)] * 4,
         compiler_params=params(),
         cost_estimate=pl.CostEstimate(
@@ -302,6 +329,26 @@
 
 def gather_blocks(block):
     return exchange([block] * lax.axis_size("group"))
+
+
+def gather_halves(block):
+    count, width = lax.axis_size("group"), block.shape[1] // 2
+    bits = [1 << b for b in range(count.bit_length() - 1)]
+    held = []
+    for side, path in enumerate((bits, bits[::-1])):
+        held.append((block[:, side * width : (side + 1) * width], [0], path))
+    for turn in range(len(bits)):
+        moved = []
+        for value, members, path in held:
+            bit = path[turn]
+            arrived = swap(value, bit)
+            moved.append((jnp.concatenate([value, arrived]), members + [m ^ bit for m in members], path))
+        held = moved
+    rows, sides = block.shape[0], []
+    for value, members, _ in held:
+        at = {m: value[i * rows : (i + 1) * rows] for i, m in enumerate(members)}
+        sides.append([at[k] for k in range(count)])
+    return sides
 
 
 def in_order(blocks):
@@ -541,20 +588,19 @@
     hidden_grad = grad_out + norm_back(ffn_in_grad * gain_two, normed_two, factor_two)
     attn_grad = (active * hidden_grad).astype(bf16)
     order.mark(attn_grad)
-    attn_blocks = gather_blocks(attn_grad)
+    attn_sides = gather_halves(attn_grad)
     branch = matmul(order(act_low), down_weight)
     order.mark(branch)
     branch_sums = column_sums(order(branch_wide))
     order.mark(branch_sums)
 
-    attn_all = in_order(list(order(*attn_blocks)))
+    attn_sides = order(*(attn_sides[0] + attn_sides[1]))
+    attn_all = in_order([jnp.concatenate(pair, 1) for pair in zip(attn_sides[:count], attn_sides[count:])])
     context_grad = nt(attn_all, out_weight).astype(bf16)
-    out_part = tn(context, attn_all).astype(bf16)
-    qkv_grad = jnp.concatenate(attention_back(qkv, after(context_grad, out_part)), 1)
-
-    qkv_part = tn(attn_in, qkv_grad).astype(bf16).reshape(count, cols, 3 * cols)
-    out_blocks = [out_part[:, k * cols : (k + 1) * cols] for k in range(count)]
-    parts = jnp.concatenate([qkv_part, jnp.stack(out_blocks)], 2)
+    qkv_grads = attention_back(qkv, context_grad)
+
+    parts = weight_parts(attn_in, *qkv_grads, context, attn_all)
+    qkv_grad = jnp.concatenate(qkv_grads, 1)
     piece = lax.psum_scatter(parts, "replica", scatter_dimension=1, tiled=True)
     qkv_weight = jnp.zeros((width, 3 * cols), bf16)
     for start, block in zip([me * cols] + [starts[1 + k] for k in range(2 * count - 2)], [own] + arrived + others):

time: 534 us -> 526 us (0.985)
  Pallas kernels: 117 us -> 127 us
  matrix products: 119 us -> 113 us
    pallas_call x1 -> x2, Pallas kernels: 9.42 us -> 19.3 us  [the longest x1 10.2 us: put_blocks(): pl.pallas_call(put_blocks_body, grid=(count, 2), in_specs=[pl.BlockSpec((...]
    ppermute x30 -> x31, waiting for transfers between devices: 122 us -> 117 us  [swap(): return lax.ppermute(block, 'group', [(i, i ^ step) for i in range(count)])]
    dot_general x4 -> x2, matrix products: 52.6 us -> 47.7 us  [tn(): lax.dot_general(left, right, (((0,), (0,)), ((), ())), preferred_element_...]
    ppermute x30 -> x31, starting transfers between devices: 37.6 us -> 38.5 us  [swap(): return lax.ppermute(block, 'group', [(i, i ^ step) for i in range(count)])]
  transfers between devices with their start and end apart: 43 -> 44, of which waited for: 20 -> 18; matrix products, arithmetic and copies ran while one was open for 37% -> 35% of each run, Pallas kernels for 20% -> 23%
where the time goes in v4:
time: 526 us; the launch traced here: 516 us
  waiting for transfers between devices  142 us (27%)
  Pallas kernels  127 us (24%)
  matrix products  113 us (21%)
  starting transfers between devices  44.8 us (9%)
  local copies, waits for them, and re-layouts  42.8 us (8%)
  other arithmetic  31.2 us (6%)
  between operations  15.8 us (3%)
    ppermute x31, waiting for transfers between devices, swap(): return lax.ppermute(block, 'group', [(i, i ^ step) for i in range(count)])  117 us
    dot_general x5, matrix products, nt(): lax.dot_general(left, right, (((1,), (1,)), ((), ())), preferred_element_...  48.1 us
    dot_general x2, matrix products, tn(): lax.dot_general(left, right, (((0,), (0,)), ((), ())), preferred_element_...  47.7 us
    ppermute x31, starting transfers between devices, swap(): return lax.ppermute(block, 'group', [(i, i ^ step) for i in range(count)])  38.5 us
    pallas_call x1, Pallas kernels, gelu_product(): pl.pallas_call(functools.partial(gelu_body, min(256, col_tile)), grid_spe...  34.1 us
    pallas_call x4, Pallas kernels, put_half(): pl.pallas_call(put_body, grid_spec=pltpu.PrefetchScalarGridSpec(num_scala...  26.6 us
    dot_general x2, matrix products, matmul(): return jnp.dot(left, right, preferred_element_type=f32)  17.4 us
    pallas_call x1, Pallas kernels, attention_back(): pl.pallas_call(attend_back_body, grid=(pairs,), in_specs=[spec(0), spec(1...  14.8 us
  transfers between devices with their start and end apart: 44, of which 18 were waited for; matrix products, arithmetic and copies ran while one was open for 35% of the time, Pallas kernels for 23%

profile of v4, /device:TPU:0, one launch (start us, length us, event | category | flops | bytes accessed | tf_op | source)
XLA Modules:
  0.0 516.3 jit_solution(8580259723479119468)
XLA Ops:
  17.0 4.0 collective-permute-start.2
  37.6 13.2 %collective-permute-done = bf16[130,2048]{1,0:T(8,128)(2,1)} collective-permute-done((bf16[130,2048]{1,0:T(8,128)(2,1)S(1)}, bf16[130,2048]{1,0:T(8,128)(2,1)}, u32[]{:S(2)}, u32[]{:S(2)}) %collective-permute-start) | collective-permute-done | bytes 532512 | tf_op jit(solution)/shard_map/ppermute | solution.py:323
  65.7 3.8 fusion.5.x_ref
  69.4 28.7 %collective-permute-done.5.refs_2_ = bf16[256,1536]{1,0:T(8,128)(2,1)} collective-permute-done((bf16[256,1536]{1,0:T(8,128)(2,1)}, bf16[256,1536]{1,0:T(8,128)(2,1)}, u32[]{:S(2)}, u32[]{:S(2)}) %collective-permute-start.5) | collective-permute-done | bytes 786464 | tf_op jit(solution)/shard_map/ppermute | solution.py:323
  103.0 9.6 %shard_map.314.q_ref.k_ref.v_ref = bf16[512,1536]{1,0:T(8,128)(2,1)} custom-call(s32[7]{0:T(128)} %stack.46.at_ref, bf16[512,2048]{1,0:T(8,128)(2,1)} %fusion.5.x_ref, bf16[512,1536]{1,0:T(8,128)(2,1)} %pad_maximum_fusion.own_ref, bf16[256,1536]{1,0:T(8,128)(2,1)} %collective-permute-done.3.refs_0_, bf16[256,1536]{1,0:T(8,128)(2,1)} %collective-permute-done.4.refs_1_, ...), custom_call_target="tpu_custom_call" | custom-call | flops 3221225472 | bytes 9961472 | tf_op jit(solution)/shard_map/pallas_call | solution.py:248
  112.6 8.6 %shard_map.315.context_ref = bf16[512,512]{1,0:T(8,128)(2,1)} custom-call(bf16[512,1536]{1,0:T(8,128)(2,1)} %shard_map.314.q_ref.k_ref.v_ref, bf16[512,1536]{1,0:T(8,128)(2,1)} %shard_map.314.q_ref.k_ref.v_ref, bf16[512,1536]{1,0:T(8,128)(2,1)} %shard_map.314.q_ref.k_ref.v_ref), custom_call_target="tpu_custom_call" | custom-call | flops 536870912 | bytes 2097152 | tf_op jit(solution)/shard_map/pallas_call | solution.py:93
  127.6 19.3 %collective-permute-done.9 = bf16[128,2048]{1,0:T(8,128)(2,1)S(1)} collective-permute-done((bf16[128,2048]{1,0:T(8,128)(2,1)S(1)}, bf16[128,2048]{1,0:T(8,128)(2,1)S(1)}, u32[]{:S(2)}, u32[]{:S(2)}) %collective-permute-start.9) | collective-permute-done | bytes 524320 | tf_op jit(solution)/shard_map/ppermute | solution.py:323
  146.9 11.9 %collective-permute-done.11 = bf16[128,2048]{1,0:T(8,128)(2,1)S(1)} collective-permute-done((bf16[128,2048]{1,0:T(8,128)(2,1)S(1)}, bf16[128,2048]{1,0:T(8,128)(2,1)S(1)}, u32[]{:S(2)}, u32[]{:S(2)}) %collective-permute-start.11) | collective-permute-done | bytes 524320 | tf_op jit(solution)/shard_map/ppermute | solution.py:323
  165.7 9.9 %convolution_convert_fusion.4.refs_6_ = bf16[512,2048]{1,0:T(8,128)(2,1)} fusion(bf16[2048,2048]{1,0:T(8,128)(2,1)} %param.35, bf16[4096,2048]{1,0:T(8,128)(2,1)} %all-gather.4.cloned.1.call-done, s32[]{:T(128)S(6)} %select_n.159), kind=kOutput, calls=%fused_computation.18 | convolution fusion | flops 4296015872 | bytes 12582916 | tf_op jit(solution)/shard_map/dot_general | solution.py:37
  178.2 13.2 %collective-permute-done.13.refs_2_ = bf16[128,2048]{1,0:T(8,128)(2,1)} collective-permute-done((bf16[128,2048]{1,0:T(8,128)(2,1)}, bf16[128,2048]{1,0:T(8,128)(2,1)}, u32[]{:S(2)}, u32[]{:S(2)}) %collective-permute-start.13) | collective-permute-done | bytes 524320 | tf_op jit(solution)/shard_map/ppermute | solution.py:323
  191.4 13.9 %shard_map.316 = (bf16[512,2048]{1,0:T(8,128)(2,1)}, bf16[512,2048]{1,0:T(8,128)(2,1)}, f32[1,2048]{1,0:T(1,128)}) custom-call(s32[4]{0:T(128)} %iota_xor_fusion.member_ref, bf16[128,2048]{1,0:T(8,128)(2,1)} %add_convert_fusion.1.refs_0_, bf16[128,2048]{1,0:T(8,128)(2,1)} %collective-permute-done.12.refs_1_, ...), custom_call_target="tpu_custom_call" | custom-call | flops 4294967296 | bytes 16777216 | tf_op jit(solution)/shard_map/pallas_call | solution.py:217
  205.3 8.7 %convolution_convert_fusion.3 = bf16[512,2048]{1,0:T(8,128)(2,1)S(1)} fusion(bf16[512,2048]{1,0:T(8,128)(2,1)} %get-tuple-element.99, bf16[2048,2048]{1,0:T(8,128)(2,1)} %refs_1_.1), kind=kOutput, calls=%fused_computation.17 | convolution fusion | flops 4296015872 | bytes 12582912 | tf_op jit(solution)/shard_map/dot_general | solution.py:37
  217.8 22.3 %convolution_convert_fusion.refs_3_ = bf16[4096,1024]{1,0:T(8,128)(2,1)} fusion(bf16[4096,2048]{1,0:T(8,128)(2,1)} %all-gather.4.cloned.1.call-done, bf16[2048,2048]{1,0:T(8,128)(2,1)S(1)} %bitcast.98, s32[]{:T(128)S(6)} %select_n.160), kind=kOutput, calls=%fused_computation.1 | convolution fusion | flops 17184063488 | bytes 29360132 | tf_op jit(solution)/shard_map/dot_general | solution.py:37
  240.1 8.2 %collective-permute-done.16 = bf16[128,2048]{1,0:T(8,128)(2,1)S(1)} collective-permute-done((bf16[128,2048]{1,0:T(8,128)(2,1)S(1)}, bf16[128,2048]{1,0:T(8,128)(2,1)S(1)}, u32[]{:S(2)}, u32[]{:S(2)}) %collective-permute-start.16) | collective-permute-done | bytes 524320 | tf_op jit(solution)/shard_map/ppermute | solution.py:323
  253.5 14.9 %fusion.37 = f32[512,2048]{1,0:T(8,128)} fusion(bf16[512,2048]{1,0:T(8,128)(2,1)S(1)} %copy-done.20, bf16[2048,2048]{1,0:T(8,128)(2,1)S(1)} %bitcast.98), kind=kOutput, calls=%fused_computation.141 | convolution fusion | flops 4294967296 | bytes 14680064 | tf_op jit(solution)/shard_map/dot_general | solution.py:314
  270.7 4.5 convert_reduce_fusion
  275.2 12.1 %collective-permute-done.21 = bf16[256,1024]{1,0:T(8,128)(2,1)S(1)} collective-permute-done((bf16[256,1024]{1,0:T(8,128)(2,1)S(1)}, bf16[256,1024]{1,0:T(8,128)(2,1)S(1)}, u32[]{:S(2)}, u32[]{:S(2)}) %collective-permute-start.21) | collective-permute-done | bytes 524320 | tf_op jit(solution)/shard_map/ppermute | solution.py:323
  290.0 14.8 %shard_map.317 = (bf16[512,512]{1,0:T(8,128)(2,1)}, bf16[512,512]{1,0:T(8,128)(2,1)}, bf16[512,512]{1,0:T(8,128)(2,1)}) custom-call(bf16[512,1536]{1,0:T(8,128)(2,1)} %shard_map.314.q_ref.k_ref.v_ref, bf16[512,1536]{1,0:T(8,128)(2,1)} %shard_map.314.q_ref.k_ref.v_ref, bf16[512,1536]{1,0:T(8,128)(2,1)} %shard_map.314.q_ref.k_ref.v_ref, ...), custom_call_target="tpu_custom_call" | custom-call | flops 1342177280 | bytes 3670016 | tf_op jit(solution)/shard_map/pallas_call | solution.py:106
  304.8 9.1 %shard_map.318 = bf16[4,512,2048]{2,1,0:T(8,128)(2,1)} custom-call(bf16[512,2048]{1,0:T(8,128)(2,1)} %fusion.5.x_ref, bf16[512,512]{1,0:T(8,128)(2,1)} %get-tuple-element.115.q_ref, bf16[512,512]{1,0:T(8,128)(2,1)} %get-tuple-element.116.k_ref, bf16[512,512]{1,0:T(8,128)(2,1)} %get-tuple-element.117.v_ref, bf16[512,512]{1,0:T(8,128)(2,1)} %shard_map.315.context_ref, ...), custom_call_target="tpu_custom_call" | custom-call | flops 4294967296 | bytes 14680064 | tf_op jit(solution)/shard_map/pallas_call | solution.py:169
  322.7 5.2 %fusion.6 = (f32[2048]{0:T(1024)S(1)}, f32[2048]{0:T(1024)S(1)}, f32[512,2048]{1,0:T(8,128)S(1)}) fusion(bf16[512,2048]{1,0:T(8,128)(2,1)} %slice_dynamic-update-slice_fusion, f32[512]{0:T(512)S(1)} %add_rsqrt_fusion, f32[512]{0:T(512)S(1)} %broadcast_multiply_fusion, bf16[512,1536]{1,0:T(8,128)(2,1)S(1)} %constant_dynamic-update-slice_fusion.10, ...), kind=kOutput, calls=%fused_computation.10 | convolution fusion | flops 3227512832 | bytes 14176256 | tf_op jit(solution)/shard_map/dot_general | solution.py:37
  333.1 34.1 %shard_map.319 = (bf16[4096,1024]{1,0:T(8,128)(2,1)}, bf16[4096,1024]{1,0:T(8,128)(2,1)}, f32[1,1024]{1,0:T(1,128)}) custom-call(s32[1]{0:T(128)} %bitcast.22.place_ref, bf16[4096,2048]{1,0:T(8,128)(2,1)} %all-gather.6.cloned.1.call-done.refs_0_, bf16[2048,2048]{1,0:T(8,128)(2,1)} %refs_1_.1, bf16[1,2048]{1,0:T(2,128)(2,1)} %broadcast_in_dim.15.refs_5_.refs_2_, ...), custom_call_target="tpu_custom_call" | custom-call | flops 17179869184 | bytes 46137344 | tf_op jit(solution)/shard_map/pallas_call | solution.py:150
  374.0 23.9 %convolution_convert_fusion.2.part_ref = bf16[1024,2048]{1,0:T(8,128)(2,1)} fusion(bf16[4096,1024]{1,0:T(8,128)(2,1)} %get-tuple-element.134, bf16[4096,2048]{1,0:T(8,128)(2,1)} %all-gather.4.cloned.1.call-done), kind=kOutput, calls=%fused_computation.15 | convolution fusion | flops 17181966336 | bytes 29360128 | tf_op jit(solution)/shard_map/dot_general | solution.py:39
  397.9 5.6 %reduce-scatter.2.cloned.1.call-done = bf16[4,64,2048]{2,1,0:T(8,128)(2,1)} async-done(((bf16[4,512,2048]{2,1,0:T(8,128)(2,1)}), bf16[4,64,2048]{2,1,0:T(8,128)(2,1)}) %reduce-scatter.2.cloned.1.call-update) | async-done | bytes 1048592 | tf_op jit(solution)/shard_map/reduce_scatter | solution.py:604
  408.2 3.4 collective-permute-done.29
  411.6 3.3 collective-permute-done.30
  418.3 23.7 %convolution_convert_fusion.1.part_ref = bf16[2048,1024]{1,0:T(8,128)(2,1)} fusion(bf16[4096,2048]{1,0:T(8,128)(2,1)} %all-gather.6.cloned.1.call-done.refs_0_, bf16[4096,1024]{1,0:T(8,128)(2,1)} %get-tuple-element.128), kind=kOutput, calls=%fused_computation.14 | convolution fusion | flops 17181966336 | bytes 29360128 | tf_op jit(solution)/shard_map/dot_general | solution.py:39
  446.8 6.0 %shard_map.320.refs_0_ = f32[2048,2048]{1,0:T(8,128)} custom-call(s32[1]{0:T(128)} %bitcast.22.place_ref, bf16[1024,2048]{1,0:T(8,128)(2,1)} %convolution_convert_fusion.2.part_ref), custom_call_target="tpu_custom_call" | custom-call | bytes 12582912 | tf_op jit(solution)/shard_map/pallas_call | solution.py:284
  462.8 7.3 %shard_map.321.refs_0_ = f32[2048,2048]{1,0:T(8,128)} custom-call(s32[1]{0:T(128)} %bitcast.22.place_ref, bf16[2048,1024]{1,0:T(8,128)(2,1)} %convolution_convert_fusion.1.part_ref), custom_call_target="tpu_custom_call" | custom-call | bytes 12582912 | tf_op jit(solution)/shard_map/pallas_call | solution.py:284
  470.1 6.0 %shard_map.322 = f32[2048,2048]{1,0:T(8,128)} custom-call(s32[1]{0:T(128)S(6)} %sub.68.place_ref, bf16[1024,2048]{1,0:T(8,128)(2,1)} %collective-permute-done.35.part_ref, f32[2048,2048]{1,0:T(8,128)} %shard_map.320.refs_0_), custom_call_target="tpu_custom_call", output_to_operand_aliasing={{}: (2, {})} | custom-call | bytes 12582912 | tf_op jit(solution)/shard_map/pallas_call | solution.py:284
  476.7 7.3 %shard_map.323 = f32[2048,2048]{1,0:T(8,128)} custom-call(s32[1]{0:T(128)S(6)} %sub.68.place_ref, bf16[2048,1024]{1,0:T(8,128)(2,1)} %collective-permute-done.38.part_ref, f32[2048,2048]{1,0:T(8,128)} %shard_map.321.refs_0_), custom_call_target="tpu_custom_call", output_to_operand_aliasing={{}: (2, {})} | custom-call | bytes 12582912 | tf_op jit(solution)/shard_map/pallas_call | solution.py:284
  485.2 14.0 %all-gather.8.cloned.1.call-done.block_ref = bf16[4,512,2048]{2,1,0:T(8,128)(2,1)} async-done(((bf16[4,64,2048]{2,1,0:T(8,128)(2,1)}), bf16[4,512,2048]{2,1,0:T(8,128)(2,1)}) %all-gather.8.cloned.1.call-update) | async-done | bytes 8388624 | tf_op jit(solution)/shard_map/all_gather | solution.py:674
  499.2 10.2 %shard_map.324 = (f32[512,2048]{1,0:T(8,128)}, f32[512,2048]{1,0:T(8,128)}, f32[512,2048]{1,0:T(8,128)}, f32[512,2048]{1,0:T(8,128)}) custom-call(bf16[4,512,2048]{2,1,0:T(8,128)(2,1)} %all-gather.8.cloned.1.call-done.block_ref), custom_call_target="tpu_custom_call" | custom-call | bytes 25165824 | tf_op jit(solution)/shard_map/pallas_call | solution.py:300
  (258 shorter events, 120.0 us)
Async XLA Ops:
  7.2 158.5 %all-gather.4.cloned.1.call-start = ((), (), s32[]{:S(2)}) async-start(), calls=%async_computation.1 | async-start | bytes 17301504 | tf_op jit(solution)/shard_map/all_gather | solution.py:555
  10.7 322.3 %all-gather.6.cloned.1.call-start = ((), (), s32[]{:S(2)}) async-start(), calls=%async_computation.2 | async-start | bytes 17301504 | tf_op jit(solution)/shard_map/all_gather | solution.py:569
  17.0 39.0 %collective-permute-start.2 = (bf16[130,2048]{1,0:T(8,128)(2,1)S(1)}, bf16[130,2048]{1,0:T(8,128)(2,1)}, u32[]{:S(2)}, u32[]{:S(2)}) collective-permute-start(bf16[130,2048]{1,0:T(8,128)(2,1)S(1)} %pad_maximum_fusion.4), channel_id=1, source_target_pairs={{0,3},{1,2},{2,1},{3,0},{4,7},{5,6},{6,5},{7,4},{8,11},{9,10},{10,... | collective-permute-start | bytes 1597448 | tf_op jit(solution)/shard_map/ppermute | solution.py:323
  21.0 33.2 %collective-permute-start.1 = (bf16[130,2048]{1,0:T(8,128)(2,1)S(1)}, bf16[130,2048]{1,0:T(8,128)(2,1)}, u32[]{:S(2)}, u32[]{:S(2)}) collective-permute-start(bf16[130,2048]{1,0:T(8,128)(2,1)S(1)} %pad_maximum_fusion.4), channel_id=1, source_target_pairs={{0,2},{1,3},{2,0},{3,1},{4,6},{5,7},{6,4},{7,5},{8,10},{9,11},{10,... | collective-permute-start | bytes 1597448 | tf_op jit(solution)/shard_map/ppermute | solution.py:323
  21.5 29.4 %collective-permute-start = (bf16[130,2048]{1,0:T(8,128)(2,1)S(1)}, bf16[130,2048]{1,0:T(8,128)(2,1)}, u32[]{:S(2)}, u32[]{:S(2)}) collective-permute-start(bf16[130,2048]{1,0:T(8,128)(2,1)S(1)} %pad_maximum_fusion.4), channel_id=1, source_target_pairs={{0,1},{1,0},{2,3},{3,2},{4,5},{5,4},{6,7},{7,6},{8,9},{9,8},{10,11... | collective-permute-start | bytes 1597448 | tf_op jit(solution)/shard_map/ppermute | solution.py:323
  26.1 72.0 %collective-permute-start.4 = (bf16[256,1536]{1,0:T(8,128)(2,1)}, bf16[256,1536]{1,0:T(8,128)(2,1)}, u32[]{:S(2)}, u32[]{:S(2)}) collective-permute-start(bf16[256,1536]{1,0:T(8,128)(2,1)} %pad_maximum_fusion.2), channel_id=1, source_target_pairs={{0,2},{1,3},{2,0},{3,1},{4,6},{5,7},{6,4},{7,5},{8,10},{9,11},{10,... | collective-permute-start | bytes 2359304 | tf_op jit(solution)/shard_map/ppermute | solution.py:323
  28.9 69.2 %collective-permute-start.3 = (bf16[256,1536]{1,0:T(8,128)(2,1)}, bf16[256,1536]{1,0:T(8,128)(2,1)}, u32[]{:S(2)}, u32[]{:S(2)}) collective-permute-start(bf16[256,1536]{1,0:T(8,128)(2,1)} %pad_maximum_fusion.1), channel_id=1, source_target_pairs={{0,1},{1,0},{2,3},{3,2},{4,5},{5,4},{6,7},{7,6},{8,9},{9,8},{10,11... | collective-permute-start | bytes 2359304 | tf_op jit(solution)/shard_map/ppermute | solution.py:323
  50.9 47.2 %collective-permute-start.5 = (bf16[256,1536]{1,0:T(8,128)(2,1)}, bf16[256,1536]{1,0:T(8,128)(2,1)}, u32[]{:S(2)}, u32[]{:S(2)}) collective-permute-start(bf16[256,1536]{1,0:T(8,128)(2,1)} %pad_maximum_fusion.3), channel_id=1, source_target_pairs={{0,3},{1,2},{2,1},{3,0},{4,7},{5,6},{6,5},{7,4},{8,11},{9,10},{10,... | collective-permute-start | bytes 2359304 | tf_op jit(solution)/shard_map/ppermute | solution.py:323
  123.9 23.0 %collective-permute-start.9 = (bf16[128,2048]{1,0:T(8,128)(2,1)S(1)}, bf16[128,2048]{1,0:T(8,128)(2,1)S(1)}, u32[]{:S(2)}, u32[]{:S(2)}) collective-permute-start(bf16[128,2048]{1,0:T(8,128)(2,1)S(1)} %get-tuple-element.185), channel_id=1, source_target_pairs={{0,1},{1,0},{2,3},{3,2},{4,5},{5,4},{6,7},{7,6},{8,9},{9,8},{10,11... | collective-permute-start | bytes 1572872 | tf_op jit(solution)/shard_map/ppermute | solution.py:323
  125.7 33.1 %collective-permute-start.11 = (bf16[128,2048]{1,0:T(8,128)(2,1)S(1)}, bf16[128,2048]{1,0:T(8,128)(2,1)S(1)}, u32[]{:S(2)}, u32[]{:S(2)}) collective-permute-start(bf16[128,2048]{1,0:T(8,128)(2,1)S(1)} %get-tuple-element.186), channel_id=1, source_target_pairs={{0,3},{1,2},{2,1},{3,0},{4,7},{5,6},{6,5},{7,4},{8,11},{9,10},{10,... | collective-permute-start | bytes 1572872 | tf_op jit(solution)/shard_map/ppermute | solution.py:323
  127.2 31.6 %collective-permute-start.10 = (bf16[128,2048]{1,0:T(8,128)(2,1)S(1)}, bf16[128,2048]{1,0:T(8,128)(2,1)S(1)}, u32[]{:S(2)}, u32[]{:S(2)}) collective-permute-start(bf16[128,2048]{1,0:T(8,128)(2,1)S(1)} %get-tuple-element.187), channel_id=1, source_target_pairs={{0,2},{1,3},{2,0},{3,1},{4,6},{5,7},{6,4},{7,5},{8,10},{9,11},{10,... | collective-permute-start | bytes 1572872 | tf_op jit(solution)/shard_map/ppermute | solution.py:323
  160.8 242.8 %reduce-scatter.2.cloned.1.call-start = ((), (), s32[]{:S(2)}) async-start(), calls=%async_computation.3 | async-start | bytes 9437184 | tf_op jit(solution)/shard_map/reduce_scatter | solution.py:604
  162.6 28.8 %collective-permute-start.13 = (bf16[128,2048]{1,0:T(8,128)(2,1)}, bf16[128,2048]{1,0:T(8,128)(2,1)}, u32[]{:S(2)}, u32[]{:S(2)}) collective-permute-start(bf16[128,2048]{1,0:T(8,128)(2,1)} %add_convert_fusion.1.refs_0_), channel_id=1, source_target_pairs={{0,2},{1,3},{2,0},{3,1},{4,6},{5,7},{6,4},{7,5},{8,10},{9,11},{10,... | collective-permute-start | bytes 1572872 | tf_op jit(solution)/shard_map/ppermute | solution.py:323
  164.2 27.2 %collective-permute-start.12 = (bf16[128,2048]{1,0:T(8,128)(2,1)}, bf16[128,2048]{1,0:T(8,128)(2,1)}, u32[]{:S(2)}, u32[]{:S(2)}) collective-permute-start(bf16[128,2048]{1,0:T(8,128)(2,1)} %add_convert_fusion.1.refs_0_), channel_id=1, source_target_pairs={{0,1},{1,0},{2,3},{3,2},{4,5},{5,4},{6,7},{7,6},{8,9},{9,8},{10,11... | collective-permute-start | bytes 1572872 | tf_op jit(solution)/shard_map/ppermute | solution.py:323
  214.2 25.8 %collective-permute-start.17 = (bf16[128,2048]{1,0:T(8,128)(2,1)S(1)}, bf16[128,2048]{1,0:T(8,128)(2,1)S(1)}, u32[]{:S(2)}, u32[]{:S(2)}) collective-permute-start(bf16[128,2048]{1,0:T(8,128)(2,1)S(1)} %get-tuple-element.188), channel_id=1, source_target_pairs={{0,3},{1,2},{2,1},{3,0},{4,7},{5,6},{6,5},{7,4},{8,11},{9,10},{10,... | collective-permute-start | bytes 1572872 | tf_op jit(solution)/shard_map/ppermute | solution.py:323
  215.8 32.4 %collective-permute-start.16 = (bf16[128,2048]{1,0:T(8,128)(2,1)S(1)}, bf16[128,2048]{1,0:T(8,128)(2,1)S(1)}, u32[]{:S(2)}, u32[]{:S(2)}) collective-permute-start(bf16[128,2048]{1,0:T(8,128)(2,1)S(1)} %get-tuple-element.189), channel_id=1, source_target_pairs={{0,2},{1,3},{2,0},{3,1},{4,6},{5,7},{6,4},{7,5},{8,10},{9,11},{10,... | collective-permute-start | bytes 1572872 | tf_op jit(solution)/shard_map/ppermute | solution.py:323
  217.3 31.7 %collective-permute-start.15 = (bf16[128,2048]{1,0:T(8,128)(2,1)S(1)}, bf16[128,2048]{1,0:T(8,128)(2,1)S(1)}, u32[]{:S(2)}, u32[]{:S(2)}) collective-permute-start(bf16[128,2048]{1,0:T(8,128)(2,1)S(1)} %get-tuple-element.190), channel_id=1, source_target_pairs={{0,1},{1,0},{2,3},{3,2},{4,5},{5,4},{6,7},{7,6},{8,9},{9,8},{10,11... | collective-permute-start | bytes 1572872 | tf_op jit(solution)/shard_map/ppermute | solution.py:323
  253.1 17.1 %collective-permute-start.18 = (bf16[128,1024]{1,0:T(8,128)(2,1)S(1)}, bf16[128,1024]{1,0:T(8,128)(2,1)S(1)}, u32[]{:S(2)}, u32[]{:S(2)}) collective-permute-start(bf16[128,1024]{1,0:T(8,128)(2,1)S(1)} %get-tuple-element.107), channel_id=1, source_target_pairs={{0,1},{1,0},{2,3},{3,2},{4,5},{5,4},{6,7},{7,6},{8,9},{9,8},{10,11... | collective-permute-start | bytes 786440 | tf_op jit(solution)/shard_map/ppermute | solution.py:323
  268.4 18.9 %collective-permute-start.21 = (bf16[256,1024]{1,0:T(8,128)(2,1)S(1)}, bf16[256,1024]{1,0:T(8,128)(2,1)S(1)}, u32[]{:S(2)}, u32[]{:S(2)}) collective-permute-start(bf16[256,1024]{1,0:T(8,128)(2,1)S(1)} %pad_maximum_fusion.6), channel_id=1, source_target_pairs={{0,1},{1,0},{2,3},{3,2},{4,5},{5,4},{6,7},{7,6},{8,9},{9,8},{10,11... | collective-permute-start | bytes 1572872 | tf_op jit(solution)/shard_map/ppermute | solution.py:323
  270.3 17.1 %collective-permute-start.19 = (bf16[256,1024]{1,0:T(8,128)(2,1)S(1)}, bf16[256,1024]{1,0:T(8,128)(2,1)S(1)}, u32[]{:S(2)}, u32[]{:S(2)}) collective-permute-start(bf16[256,1024]{1,0:T(8,128)(2,1)S(1)} %pad_maximum_fusion.5), channel_id=1, source_target_pairs={{0,2},{1,3},{2,0},{3,1},{4,6},{5,7},{6,4},{7,5},{8,10},{9,11},{10,... | collective-permute-start | bytes 1572872 | tf_op jit(solution)/shard_map/ppermute | solution.py:323
  313.9 185.3 %all-gather.8.cloned.1.call-start = ((), (), s32[]{:S(2)}) async-start(), calls=%async_computation.4 | async-start | bytes 9437184 | tf_op jit(solution)/shard_map/all_gather | solution.py:674
  329.1 38.0 %collective-permute-start.27 = (bf16[128,2048]{1,0:T(8,128)(2,1)}, bf16[128,2048]{1,0:T(8,128)(2,1)}, u32[]{:S(2)}, u32[]{:S(2)}) collective-permute-start(bf16[128,2048]{1,0:T(8,128)(2,1)} %get-tuple-element.182), channel_id=1, source_target_pairs={{0,3},{1,2},{2,1},{3,0},{4,7},{5,6},{6,5},{7,4},{8,11},{9,10},{10,... | collective-permute-start | bytes 1572872 | tf_op jit(solution)/shard_map/ppermute | solution.py:323
  330.5 36.6 %collective-permute-start.26 = (bf16[128,2048]{1,0:T(8,128)(2,1)}, bf16[128,2048]{1,0:T(8,128)(2,1)}, u32[]{:S(2)}, u32[]{:S(2)}) collective-permute-start(bf16[128,2048]{1,0:T(8,128)(2,1)} %get-tuple-element.183), channel_id=1, source_target_pairs={{0,2},{1,3},{2,0},{3,1},{4,6},{5,7},{6,4},{7,5},{8,10},{9,11},{10,... | collective-permute-start | bytes 1572872 | tf_op jit(solution)/shard_map/ppermute | solution.py:323
  331.6 35.6 %collective-permute-start.25 = (bf16[128,2048]{1,0:T(8,128)(2,1)S(1)}, bf16[128,2048]{1,0:T(8,128)(2,1)}, u32[]{:S(2)}, u32[]{:S(2)}) collective-permute-start(bf16[128,2048]{1,0:T(8,128)(2,1)S(1)} %get-tuple-element.184), channel_id=1, source_target_pairs={{0,1},{1,0},{2,3},{3,2},{4,5},{5,4},{6,7},{7,6},{8,9},{9,8},{10,11... | collective-permute-start | bytes 1572872 | tf_op jit(solution)/shard_map/ppermute | solution.py:323
  370.5 27.4 %collective-permute-start.24 = (f32[4,512]{1,0:T(4,128)S(1)}, f32[4,512]{1,0:T(4,128)S(1)}, u32[]{:S(2)}, u32[]{:S(2)}) collective-permute-start(f32[4,512]{1,0:T(4,128)S(1)} %get-tuple-element.217), channel_id=1, source_target_pairs={{0,3},{1,2},{2,1},{3,0},{4,7},{5,6},{6,5},{7,4},{8,11},{9,10},{10,... | collective-permute-start | bytes 24584 | tf_op jit(solution)/shard_map/ppermute | solution.py:323
  372.0 25.9 %collective-permute-start.23 = (f32[4,512]{1,0:T(4,128)S(1)}, f32[4,512]{1,0:T(4,128)S(1)}, u32[]{:S(2)}, u32[]{:S(2)}) collective-permute-start(f32[4,512]{1,0:T(4,128)S(1)} %get-tuple-element.218), channel_id=1, source_target_pairs={{0,2},{1,3},{2,0},{3,1},{4,6},{5,7},{6,4},{7,5},{8,10},{9,11},{10,... | collective-permute-start | bytes 24584 | tf_op jit(solution)/shard_map/ppermute | solution.py:323
  373.0 24.9 %collective-permute-start.22 = (f32[4,512]{1,0:T(4,128)S(1)}, f32[4,512]{1,0:T(4,128)S(1)}, u32[]{:S(2)}, u32[]{:S(2)}) collective-permute-start(f32[4,512]{1,0:T(4,128)S(1)} %get-tuple-element.219), channel_id=1, source_target_pairs={{0,1},{1,0},{2,3},{3,2},{4,5},{5,4},{6,7},{7,6},{8,9},{9,8},{10,11... | collective-permute-start | bytes 24584 | tf_op jit(solution)/shard_map/ppermute | solution.py:323
  417.1 52.9 %collective-permute-start.35 = (bf16[1024,2048]{1,0:T(8,128)(2,1)}, bf16[1024,2048]{1,0:T(8,128)(2,1)}, u32[]{:S(2)}, u32[]{:S(2)}) collective-permute-start(bf16[1024,2048]{1,0:T(8,128)(2,1)} %convolution_convert_fusion.2.part_ref), channel_id=1, source_target_pairs={{0,4},{4,0},{8,12},{12,8},{16,20},{20,16},{24,28},{28,24},{1,5},{5... | collective-permute-start | bytes 12582920 | tf_op jit(solution)/shard_map/ppermute | solution.py:411
  442.1 34.7 %collective-permute-start.38 = (bf16[2048,1024]{1,0:T(8,128)(2,1)}, bf16[2048,1024]{1,0:T(8,128)(2,1)}, u32[]{:S(2)}, u32[]{:S(2)}) collective-permute-start(bf16[2048,1024]{1,0:T(8,128)(2,1)} %convolution_convert_fusion.1.part_ref), channel_id=1, source_target_pairs={{0,4},{4,0},{8,12},{12,8},{16,20},{20,16},{24,28},{28,24},{1,5},{5... | collective-permute-start | bytes 12582920 | tf_op jit(solution)/shard_map/ppermute | solution.py:411
  457.3 26.7 %collective-permute-start.34 = (bf16[128,2048]{1,0:T(8,128)(2,1)S(1)}, bf16[128,2048]{1,0:T(8,128)(2,1)S(1)}, u32[]{:S(2)}, u32[]{:S(2)}) collective-permute-start(bf16[128,2048]{1,0:T(8,128)(2,1)S(1)} %get-tuple-element.179), channel_id=1, source_target_pairs={{0,3},{1,2},{2,1},{3,0},{4,7},{5,6},{6,5},{7,4},{8,11},{9,10},{10,... | collective-permute-start | bytes 1572872 | tf_op jit(solution)/shard_map/ppermute | solution.py:323
  458.9 25.1 %collective-permute-start.33 = (bf16[128,2048]{1,0:T(8,128)(2,1)S(1)}, bf16[128,2048]{1,0:T(8,128)(2,1)S(1)}, u32[]{:S(2)}, u32[]{:S(2)}) collective-permute-start(bf16[128,2048]{1,0:T(8,128)(2,1)S(1)} %get-tuple-element.180), channel_id=1, source_target_pairs={{0,2},{1,3},{2,0},{3,1},{4,6},{5,7},{6,4},{7,5},{8,10},{9,11},{10,... | collective-permute-start | bytes 1572872 | tf_op jit(solution)/shard_map/ppermute | solution.py:323
  460.0 24.0 %collective-permute-start.32 = (bf16[128,2048]{1,0:T(8,128)(2,1)S(1)}, bf16[128,2048]{1,0:T(8,128)(2,1)S(1)}, u32[]{:S(2)}, u32[]{:S(2)}) collective-permute-start(bf16[128,2048]{1,0:T(8,128)(2,1)S(1)} %get-tuple-element.181), channel_id=1, source_target_pairs={{0,1},{1,0},{2,3},{3,2},{4,5},{5,4},{6,7},{7,6},{8,9},{9,8},{10,11... | collective-permute-start | bytes 1572872 | tf_op jit(solution)/shard_map/ppermute | solution.py:323
  (39 other events, 575.5 us)
Sparse Core Ops, SparseCore 0:
  11.5 152.7 all-gather.3
  167.7 135.1 all-gather.5
  314.0 89.4 reduce-scatter.1
  417.2 82.0 all-gather.7

commit v5 on v4

--- a/solution.py
+++ b/solution.py
@@ -92,7 +92,7 @@
     work = 2 * rows * rows * cols
     return pl.pallas_call(
         attend_body, grid=(pairs,), in_specs=[spec(0), spec(1), spec(2)], out_specs=spec(0),
-        out_shape=jax.ShapeDtypeStruct((rows, cols), bf16), compiler_params=params(),
+        out_shape=jax.ShapeDtypeStruct((rows, cols), bf16), compiler_params=params(12),
         cost_estimate=pl.CostEstimate(flops=2 * work, bytes_accessed=8 * rows * cols, transcendentals=rows * rows * cols // HD),
     )(qkv, qkv, qkv)
 
@@ -105,7 +105,7 @@
     one = jax.ShapeDtypeStruct((rows, cols), bf16)
     return pl.pallas_call(
         attend_back_body, grid=(pairs,), in_specs=[spec(0), spec(1), spec(2), spec(0)], out_specs=[spec(0)] * 3,
-        out_shape=[one] * 3, scratch_shapes=[pltpu.VMEM((rows, lanes), f32)] * 2, compiler_params=params(),
+        out_shape=[one] * 3, scratch_shapes=[pltpu.VMEM((rows, lanes), f32)] * 2, compiler_params=params(12),
         cost_estimate=pl.CostEstimate(flops=5 * work, bytes_accessed=14 * rows * cols, transcendentals=rows * rows * cols // HD),
     )(qkv, qkv, qkv, grad)
 
@@ -150,7 +150,7 @@
     return pl.pallas_call(
         functools.partial(gelu_body, min(256, col_tile)), grid_spec=grid,
         out_shape=[jax.ShapeDtypeStruct((rows, width), bf16)] * 2 + [jax.ShapeDtypeStruct((1, width), f32)],
-        compiler_params=params(),
+        compiler_params=params(30),
         cost_estimate=pl.CostEstimate(flops=2 * rows * depth * width, bytes_accessed=2 * (rows * depth + depth * width + 3 * rows * width), transcendentals=rows * width),
     )(place, x, weight, bias[None], grad)
 
@@ -172,7 +172,7 @@
         in_specs=[block, whole, whole, whole, whole, block],
         out_specs=pl.BlockSpec((1, cols, 4 * cols), lambda i: (i, 0, 0)),
         out_shape=jax.ShapeDtypeStruct((count, cols, 4 * cols), bf16),
-        compiler_params=params(),
+        compiler_params=params(18),
         cost_estimate=pl.CostEstimate(
             flops=8 * count * rows * cols * cols,
             bytes_accessed=2 * (2 * rows * count * cols + 4 * rows * cols + 4 * count * cols * cols),
@@ -219,7 +219,7 @@
         grid_spec=grid,
         out_shape=[jax.ShapeDtypeStruct((tall, width), bf16)] * 2
         + [jax.ShapeDtypeStruct((1, width), f32)],
-        compiler_params=params(),
+        compiler_params=params(24),
         cost_estimate=pl.CostEstimate(
             flops=2 * tall * depth * width,
             bytes_accessed=2 * (tall * depth + depth * width + 3 * tall * width),
@@ -256,7 +256,7 @@
             out_specs=column(rows),
         ),
         out_shape=jax.ShapeDtypeStruct((rows, 3 * cols), bf16),
-        compiler_params=params(),
+        compiler_params=params(20),
         cost_estimate=pl.CostEstimate(
             flops=6 * rows * width * cols,
             bytes_accessed=2 * (rows * width + 3 * width * cols + 3 * rows * cols),
@@ -283,7 +283,7 @@
         alias = {2: 0}
     return pl.pallas_call(
         put_body, grid_spec=pltpu.PrefetchScalarGridSpec(num_scalar_prefetch=1, grid=(steps,), in_specs=in_specs, out_specs=pl.BlockSpec((tile, width), at)),
-        out_shape=jax.ShapeDtypeStruct(shape, f32), input_output_aliases=alias, compiler_params=params(),
+        out_shape=jax.ShapeDtypeStruct(shape, f32), input_output_aliases=alias, compiler_params=params(12),
         cost_estimate=pl.CostEstimate(flops=0, bytes_accessed=6 * rows * width, transcendentals=0),
     )(*args)
 
@@ -303,7 +303,7 @@
         in_specs=[pl.BlockSpec((1, rows // 2, width), lambda i, h: (i, h, 0))],
         out_specs=[pl.BlockSpec((rows // 2, cols), lambda i, h: (h, i))] * 4,
         out_shape=[jax.ShapeDtypeStruct((rows, count * cols), f32)] * 4,
-        compiler_params=params(),
+        compiler_params=params(12),
         cost_estimate=pl.CostEstimate(
             flops=0, bytes_accessed=6 * count * rows * width, transcendentals=0
         ),

time: 526 us -> 531 us (level); the launches traced: 516 us -> 527 us
  Pallas kernels: 127 us -> 108 us
  waiting for transfers between devices: 142 us -> 159 us
  local copies, waits for them, and re-layouts: 42.8 us -> 58.2 us
  matrix products: 113 us -> 99.4 us
  starting transfers between devices: 44.8 us -> 54.4 us
    unnamed x70 -> x102, local copies, waits for them, and re-layouts: 7.73 us -> 27.5 us
    reduce_scatter x1, starting transfers between devices: 0.3 us -> 11.3 us  [shards(): piece = lax.psum_scatter(parts, 'replica', scatter_dimension=1, tiled=True)]
    dot_general x2, matrix products: 17.4 us -> 7.32 us  [matmul(): return jnp.dot(left, right, preferred_element_type=f32)]
    ppermute x31, waiting for transfers between devices: 117 us -> 126 us  [swap(): return lax.ppermute(block, 'group', [(i, i ^ step) for i in range(count)])]
  transfers between devices with their start and end apart: 44 -> 44, of which waited for: 18 -> 21; matrix products, arithmetic and copies ran while one was open for 35% -> 31% of each run, Pallas kernels for 23% -> 19%
where the time goes in v5:
time: 531 us; the launch traced here: 527 us
  waiting for transfers between devices  159 us (30%)
  Pallas kernels  108 us (20%)
  matrix products  99.4 us (19%)
  local copies, waits for them, and re-layouts  58.2 us (11%)
  starting transfers between devices  54.4 us (10%)
  other arithmetic  32.5 us (6%)
  between operations  15.8 us (3%)
    ppermute x31, waiting for transfers between devices, swap(): return lax.ppermute(block, 'group', [(i, i ^ step) for i in range(count)])  126 us
    dot_general x5, matrix products, nt(): lax.dot_general(left, right, (((1,), (1,)), ((), ())), preferred_element_...  47 us
    dot_general x2, matrix products, tn(): lax.dot_general(left, right, (((0,), (0,)), ((), ())), preferred_element_...  45 us
    ppermute x31, starting transfers between devices, swap(): return lax.ppermute(block, 'group', [(i, i ^ step) for i in range(count)])  36.9 us
    pallas_call x1, Pallas kernels, gelu_product(): pl.pallas_call(functools.partial(gelu_body, min(256, col_tile)), grid_spe...  32.7 us
    unnamed x102, local copies, waits for them, and re-layouts  27.5 us
    pallas_call x4, Pallas kernels, put_half(): pl.pallas_call(put_body, grid_spec=pltpu.PrefetchScalarGridSpec(num_scala...  24.9 us
    all_gather x1, waiting for transfers between devices, shards(): attn_wgrad = lax.all_gather(piece, 'replica', axis=1, tiled=True)  14.9 us
  transfers between devices with their start and end apart: 44, of which 21 were waited for; matrix products, arithmetic and copies ran while one was open for 31% of the time, Pallas kernels for 19%

profile of v5, /device:TPU:0, one launch (start us, length us, event | category | flops | bytes accessed | tf_op | source)
XLA Modules:
  0.0 527.0 jit_solution(4573845307940548490)
XLA Ops:
  17.0 4.0 collective-permute-start.2
  38.4 12.5 %collective-permute-done = bf16[130,2048]{1,0:T(8,128)(2,1)} collective-permute-done((bf16[130,2048]{1,0:T(8,128)(2,1)S(1)}, bf16[130,2048]{1,0:T(8,128)(2,1)}, u32[]{:S(2)}, u32[]{:S(2)}) %collective-permute-start) | collective-permute-done | bytes 532512 | tf_op jit(solution)/shard_map/ppermute | solution.py:323
  69.4 28.7 %collective-permute-done.5.refs_2_ = bf16[256,1536]{1,0:T(8,128)(2,1)} collective-permute-done((bf16[256,1536]{1,0:T(8,128)(2,1)}, bf16[256,1536]{1,0:T(8,128)(2,1)}, u32[]{:S(2)}, u32[]{:S(2)}) %collective-permute-start.5) | collective-permute-done | bytes 786464 | tf_op jit(solution)/shard_map/ppermute | solution.py:323
  106.9 5.8 %shard_map.314.q_ref.k_ref.v_ref = bf16[512,1536]{1,0:T(8,128)(2,1)S(1)} custom-call(s32[7]{0:T(128)S(1)} %stack.46.at_ref, bf16[512,2048]{1,0:T(8,128)(2,1)S(1)} %copy-done.11, bf16[512,1536]{1,0:T(8,128)(2,1)S(1)} %copy-done.8, bf16[256,1536]{1,0:T(8,128)(2,1)} %collective-permute-done.3.refs_0_, bf16[256,1536]{1,0:T(8,128)(2,1)S(1)} %collective-permute-done.4.refs_1_, ...), custom_call_target="tpu_custom_call" | custom-call | flops 3221225472 | bytes 9961472 | tf_op jit(solution)/shard_map/pallas_call | solution.py:248
  113.6 7.2 %shard_map.315.context_ref = bf16[512,512]{1,0:T(8,128)(2,1)S(1)} custom-call(bf16[512,1536]{1,0:T(8,128)(2,1)S(1)} %shard_map.314.q_ref.k_ref.v_ref, bf16[512,1536]{1,0:T(8,128)(2,1)S(1)} %shard_map.314.q_ref.k_ref.v_ref, bf16[512,1536]{1,0:T(8,128)(2,1)S(1)} %shard_map.314.q_ref.k_ref.v_ref), custom_call_target="tpu_custom_call" | custom-call | flops 536870912 | bytes 2097152 | tf_op jit(solution)/shard_map/pallas_call | solution.py:93
  126.1 20.7 %collective-permute-done.9 = bf16[128,2048]{1,0:T(8,128)(2,1)S(1)} collective-permute-done((bf16[128,2048]{1,0:T(8,128)(2,1)S(1)}, bf16[128,2048]{1,0:T(8,128)(2,1)S(1)}, u32[]{:S(2)}, u32[]{:S(2)}) %collective-permute-start.9) | collective-permute-done | bytes 524320 | tf_op jit(solution)/shard_map/ppermute | solution.py:323
  146.8 11.9 %collective-permute-done.11 = bf16[128,2048]{1,0:T(8,128)(2,1)S(1)} collective-permute-done((bf16[128,2048]{1,0:T(8,128)(2,1)S(1)}, bf16[128,2048]{1,0:T(8,128)(2,1)S(1)}, u32[]{:S(2)}, u32[]{:S(2)}) %collective-permute-start.11) | collective-permute-done | bytes 524320 | tf_op jit(solution)/shard_map/ppermute | solution.py:323
  161.4 11.3 %reduce-scatter.2.cloned.1.call-start = ((), (), s32[]{:S(2)}) async-start(), calls=%async_computation.3 | async-start | bytes 9437184 | tf_op jit(solution)/shard_map/reduce_scatter | solution.py:604
  176.4 8.7 %convolution_convert_fusion.4.refs_6_ = bf16[512,2048]{1,0:T(8,128)(2,1)S(1)} fusion(bf16[2048,2048]{1,0:T(8,128)(2,1)} %param.35, bf16[4096,2048]{1,0:T(8,128)(2,1)} %all-gather.4.cloned.1.call-done, s32[]{:T(128)S(6)} %select_n.159), kind=kOutput, calls=%fused_computation.18 | convolution fusion | flops 4296015872 | bytes 12582916 | tf_op jit(solution)/shard_map/dot_general | solution.py:37
  185.1 7.6 %collective-permute-done.14.refs_3_ = bf16[128,2048]{1,0:T(8,128)(2,1)} collective-permute-done((bf16[128,2048]{1,0:T(8,128)(2,1)}, bf16[128,2048]{1,0:T(8,128)(2,1)}, u32[]{:S(2)}, u32[]{:S(2)}) %collective-permute-start.14) | collective-permute-done | bytes 524320 | tf_op jit(solution)/shard_map/ppermute | solution.py:323
  192.7 9.4 %collective-permute-done.13.refs_2_ = bf16[128,2048]{1,0:T(8,128)(2,1)} collective-permute-done((bf16[128,2048]{1,0:T(8,128)(2,1)}, bf16[128,2048]{1,0:T(8,128)(2,1)}, u32[]{:S(2)}, u32[]{:S(2)}) %collective-permute-start.13) | collective-permute-done | bytes 524320 | tf_op jit(solution)/shard_map/ppermute | solution.py:323
  205.5 12.5 %shard_map.316 = (bf16[512,2048]{1,0:T(8,128)(2,1)S(1)}, bf16[512,2048]{1,0:T(8,128)(2,1)S(1)}, f32[1,2048]{1,0:T(1,128)}) custom-call(s32[4]{0:T(128)S(1)} %iota_xor_fusion.member_ref, bf16[128,2048]{1,0:T(8,128)(2,1)S(1)} %copy-done.13, bf16[128,2048]{1,0:T(8,128)(2,1)} %collective-permute-done.12.refs_1_, ...), custom_call_target="tpu_custom_call" | custom-call | flops 4294967296 | bytes 16777216 | tf_op jit(solution)/shard_map/pallas_call | solution.py:217
  217.9 8.2 %convolution_convert_fusion.3 = bf16[512,2048]{1,0:T(8,128)(2,1)S(1)} fusion(bf16[512,2048]{1,0:T(8,128)(2,1)S(1)} %get-tuple-element.99, bf16[2048,2048]{1,0:T(8,128)(2,1)} %refs_1_.1), kind=kOutput, calls=%fused_computation.17 | convolution fusion | flops 4296015872 | bytes 12582912 | tf_op jit(solution)/shard_map/dot_general | solution.py:37
  229.9 23.7 %convolution_convert_fusion.refs_3_ = bf16[4096,1024]{1,0:T(8,128)(2,1)} fusion(bf16[4096,2048]{1,0:T(8,128)(2,1)} %all-gather.4.cloned.1.call-done, bf16[2048,2048]{1,0:T(8,128)(2,1)} %param.35, s32[]{:T(128)S(6)} %select_n.160), kind=kOutput, calls=%fused_computation.1 | convolution fusion | flops 17184063488 | bytes 29360132 | tf_op jit(solution)/shard_map/dot_general | solution.py:37
  253.6 8.7 %collective-permute-done.16 = bf16[128,2048]{1,0:T(8,128)(2,1)S(1)} collective-permute-done((bf16[128,2048]{1,0:T(8,128)(2,1)S(1)}, bf16[128,2048]{1,0:T(8,128)(2,1)S(1)}, u32[]{:S(2)}, u32[]{:S(2)}) %collective-permute-start.16) | collective-permute-done | bytes 524320 | tf_op jit(solution)/shard_map/ppermute | solution.py:323
  268.1 6.1 %fusion.37 = f32[512,2048]{1,0:T(8,128)} fusion(bf16[512,2048]{1,0:T(8,128)(2,1)S(1)} %get-tuple-element.105, bf16[2048,2048]{1,0:T(8,128)(2,1)S(1)} %bitcast.98), kind=kOutput, calls=%fused_computation.141 | convolution fusion | flops 4294967296 | bytes 14680064 | tf_op jit(solution)/shard_map/dot_general | solution.py:314
  274.2 6.2 %collective-permute-done.20 = bf16[128,1024]{1,0:T(8,128)(2,1)S(1)} collective-permute-done((bf16[128,1024]{1,0:T(8,128)(2,1)S(1)}, bf16[128,1024]{1,0:T(8,128)(2,1)S(1)}, u32[]{:S(2)}, u32[]{:S(2)}) %collective-permute-start.20) | collective-permute-done | bytes 262176 | tf_op jit(solution)/shard_map/ppermute | solution.py:323
  282.5 4.9 convert_reduce_fusion
  287.4 11.9 %collective-permute-done.21 = bf16[256,1024]{1,0:T(8,128)(2,1)S(1)} collective-permute-done((bf16[256,1024]{1,0:T(8,128)(2,1)S(1)}, bf16[256,1024]{1,0:T(8,128)(2,1)S(1)}, u32[]{:S(2)}, u32[]{:S(2)}) %collective-permute-start.21) | collective-permute-done | bytes 524320 | tf_op jit(solution)/shard_map/ppermute | solution.py:323
  302.0 13.3 %shard_map.317 = (bf16[512,512]{1,0:T(8,128)(2,1)S(1)}, bf16[512,512]{1,0:T(8,128)(2,1)S(1)}, bf16[512,512]{1,0:T(8,128)(2,1)S(1)}) custom-call(bf16[512,1536]{1,0:T(8,128)(2,1)S(1)} %copy-done.3, bf16[512,1536]{1,0:T(8,128)(2,1)S(1)} %copy-done.3, bf16[512,1536]{1,0:T(8,128)(2,1)S(1)} %copy-done.3, bf16[512,512]{1,0:T(8,128)(2,1)S(1)} %convolution_convert_fusion.5.g_ref), custom_call_target="tpu_custom_call" | custom-call | flops 1342177280 | bytes 3670016 | tf_op jit(solution)/shard_map/pallas_call | solution.py:106
  315.4 5.5 %shard_map.318 = bf16[4,512,2048]{2,1,0:T(8,128)(2,1)S(1)} custom-call(bf16[512,2048]{1,0:T(8,128)(2,1)S(1)} %copy-done.12, bf16[512,512]{1,0:T(8,128)(2,1)S(1)} %get-tuple-element.115.q_ref, bf16[512,512]{1,0:T(8,128)(2,1)S(1)} %get-tuple-element.116.k_ref, bf16[512,512]{1,0:T(8,128)(2,1)S(1)} %get-tuple-element.117.v_ref, ...), custom_call_target="tpu_custom_call" | custom-call | flops 4294967296 | bytes 14680064 | tf_op jit(solution)/shard_map/pallas_call | solution.py:169
  333.9 5.2 fusion.6
  344.0 32.7 %shard_map.319 = (bf16[4096,1024]{1,0:T(8,128)(2,1)S(1)}, bf16[4096,1024]{1,0:T(8,128)(2,1)S(1)}, f32[1,1024]{1,0:T(1,128)S(1)}) custom-call(s32[1]{0:T(128)} %bitcast.22.place_ref, bf16[4096,2048]{1,0:T(8,128)(2,1)} %all-gather.6.cloned.1.call-done.refs_0_, bf16[2048,2048]{1,0:T(8,128)(2,1)} %refs_1_.1, ...), custom_call_target="tpu_custom_call" | custom-call | flops 17179869184 | bytes 46137344 | tf_op jit(solution)/shard_map/pallas_call | solution.py:150
  385.1 21.3 %convolution_convert_fusion.2.part_ref = bf16[1024,2048]{1,0:T(8,128)(2,1)} fusion(bf16[4096,1024]{1,0:T(8,128)(2,1)S(1)} %get-tuple-element.134, bf16[4096,2048]{1,0:T(8,128)(2,1)} %all-gather.4.cloned.1.call-done), kind=kOutput, calls=%fused_computation.15 | convolution fusion | flops 17181966336 | bytes 29360128 | tf_op jit(solution)/shard_map/dot_general | solution.py:39
  406.5 8.4 %reduce-scatter.2.cloned.1.call-done = bf16[4,64,2048]{2,1,0:T(8,128)(2,1)} async-done(((bf16[4,512,2048]{2,1,0:T(8,128)(2,1)}), bf16[4,64,2048]{2,1,0:T(8,128)(2,1)}) %reduce-scatter.2.cloned.1.call-update) | async-done | bytes 1048592 | tf_op jit(solution)/shard_map/reduce_scatter | solution.py:604
  429.7 23.7 %convolution_convert_fusion.1.part_ref = bf16[2048,1024]{1,0:T(8,128)(2,1)} fusion(bf16[4096,2048]{1,0:T(8,128)(2,1)} %all-gather.6.cloned.1.call-done.refs_0_, bf16[4096,1024]{1,0:T(8,128)(2,1)} %copy-done.21), kind=kOutput, calls=%fused_computation.14 | convolution fusion | flops 17181966336 | bytes 29360128 | tf_op jit(solution)/shard_map/dot_general | solution.py:39
  460.3 4.2 shard_map.320.refs_0_
  473.2 7.3 %shard_map.321.refs_0_ = f32[2048,2048]{1,0:T(8,128)} custom-call(s32[1]{0:T(128)} %bitcast.22.place_ref, bf16[2048,1024]{1,0:T(8,128)(2,1)} %convolution_convert_fusion.1.part_ref), custom_call_target="tpu_custom_call" | custom-call | bytes 12582912 | tf_op jit(solution)/shard_map/pallas_call | solution.py:284
  480.5 6.0 %shard_map.322 = f32[2048,2048]{1,0:T(8,128)} custom-call(s32[1]{0:T(128)S(6)} %sub.68.place_ref, bf16[1024,2048]{1,0:T(8,128)(2,1)} %collective-permute-done.35.part_ref, f32[2048,2048]{1,0:T(8,128)} %shard_map.320.refs_0_), custom_call_target="tpu_custom_call", output_to_operand_aliasing={{}: (2, {})} | custom-call | bytes 12582912 | tf_op jit(solution)/shard_map/pallas_call | solution.py:284
  487.1 7.4 %shard_map.323 = f32[2048,2048]{1,0:T(8,128)} custom-call(s32[1]{0:T(128)S(6)} %sub.68.place_ref, bf16[2048,1024]{1,0:T(8,128)(2,1)} %collective-permute-done.38.part_ref, f32[2048,2048]{1,0:T(8,128)} %shard_map.321.refs_0_), custom_call_target="tpu_custom_call", output_to_operand_aliasing={{}: (2, {})} | custom-call | bytes 12582912 | tf_op jit(solution)/shard_map/pallas_call | solution.py:284
  495.8 14.9 %all-gather.8.cloned.1.call-done.block_ref = bf16[4,512,2048]{2,1,0:T(8,128)(2,1)} async-done(((bf16[4,64,2048]{2,1,0:T(8,128)(2,1)}), bf16[4,512,2048]{2,1,0:T(8,128)(2,1)}) %all-gather.8.cloned.1.call-update) | async-done | bytes 8388624 | tf_op jit(solution)/shard_map/all_gather | solution.py:674
  514.1 6.2 %shard_map.324 = (f32[512,2048]{1,0:T(8,128)}, f32[512,2048]{1,0:T(8,128)}, f32[512,2048]{1,0:T(8,128)}, f32[512,2048]{1,0:T(8,128)}) custom-call(bf16[4,512,2048]{2,1,0:T(8,128)(2,1)S(1)} %copy-done.5), custom_call_target="tpu_custom_call" | custom-call | bytes 25165824 | tf_op jit(solution)/shard_map/pallas_call | solution.py:300
  (290 shorter events, 145.2 us)
Async XLA Ops:
  7.2 169.2 %all-gather.4.cloned.1.call-start = ((), (), s32[]{:S(2)}) async-start(), calls=%async_computation.1 | async-start | bytes 17301504 | tf_op jit(solution)/shard_map/all_gather | solution.py:555
  10.7 333.3 %all-gather.6.cloned.1.call-start = ((), (), s32[]{:S(2)}) async-start(), calls=%async_computation.2 | async-start | bytes 17301504 | tf_op jit(solution)/shard_map/all_gather | solution.py:569
  17.0 39.0 %collective-permute-start.2 = (bf16[130,2048]{1,0:T(8,128)(2,1)S(1)}, bf16[130,2048]{1,0:T(8,128)(2,1)}, u32[]{:S(2)}, u32[]{:S(2)}) collective-permute-start(bf16[130,2048]{1,0:T(8,128)(2,1)S(1)} %pad_maximum_fusion.4), channel_id=1, source_target_pairs={{0,3},{1,2},{2,1},{3,0},{4,7},{5,6},{6,5},{7,4},{8,11},{9,10},{10,... | collective-permute-start | bytes 1597448 | tf_op jit(solution)/shard_map/ppermute | solution.py:323
  21.0 33.2 %collective-permute-start.1 = (bf16[130,2048]{1,0:T(8,128)(2,1)S(1)}, bf16[130,2048]{1,0:T(8,128)(2,1)}, u32[]{:S(2)}, u32[]{:S(2)}) collective-permute-start(bf16[130,2048]{1,0:T(8,128)(2,1)S(1)} %pad_maximum_fusion.4), channel_id=1, source_target_pairs={{0,2},{1,3},{2,0},{3,1},{4,6},{5,7},{6,4},{7,5},{8,10},{9,11},{10,... | collective-permute-start | bytes 1597448 | tf_op jit(solution)/shard_map/ppermute | solution.py:323
  21.5 29.4 %collective-permute-start = (bf16[130,2048]{1,0:T(8,128)(2,1)S(1)}, bf16[130,2048]{1,0:T(8,128)(2,1)}, u32[]{:S(2)}, u32[]{:S(2)}) collective-permute-start(bf16[130,2048]{1,0:T(8,128)(2,1)S(1)} %pad_maximum_fusion.4), channel_id=1, source_target_pairs={{0,1},{1,0},{2,3},{3,2},{4,5},{5,4},{6,7},{7,6},{8,9},{9,8},{10,11... | collective-permute-start | bytes 1597448 | tf_op jit(solution)/shard_map/ppermute | solution.py:323
  26.8 71.3 %collective-permute-start.4 = (bf16[256,1536]{1,0:T(8,128)(2,1)}, bf16[256,1536]{1,0:T(8,128)(2,1)S(1)}, u32[]{:S(2)}, u32[]{:S(2)}) collective-permute-start(bf16[256,1536]{1,0:T(8,128)(2,1)} %pad_maximum_fusion.2), channel_id=1, source_target_pairs={{0,2},{1,3},{2,0},{3,1},{4,6},{5,7},{6,4},{7,5},{8,10},{9,11},{10,... | collective-permute-start | bytes 2359304 | tf_op jit(solution)/shard_map/ppermute | solution.py:323
  29.6 68.5 %collective-permute-start.3 = (bf16[256,1536]{1,0:T(8,128)(2,1)}, bf16[256,1536]{1,0:T(8,128)(2,1)}, u32[]{:S(2)}, u32[]{:S(2)}) collective-permute-start(bf16[256,1536]{1,0:T(8,128)(2,1)} %pad_maximum_fusion.1), channel_id=1, source_target_pairs={{0,1},{1,0},{2,3},{3,2},{4,5},{5,4},{6,7},{7,6},{8,9},{9,8},{10,11... | collective-permute-start | bytes 2359304 | tf_op jit(solution)/shard_map/ppermute | solution.py:323
  50.9 47.2 %collective-permute-start.5 = (bf16[256,1536]{1,0:T(8,128)(2,1)}, bf16[256,1536]{1,0:T(8,128)(2,1)}, u32[]{:S(2)}, u32[]{:S(2)}) collective-permute-start(bf16[256,1536]{1,0:T(8,128)(2,1)} %pad_maximum_fusion.3), channel_id=1, source_target_pairs={{0,3},{1,2},{2,1},{3,0},{4,7},{5,6},{6,5},{7,4},{8,11},{9,10},{10,... | collective-permute-start | bytes 2359304 | tf_op jit(solution)/shard_map/ppermute | solution.py:323
  122.4 24.4 %collective-permute-start.9 = (bf16[128,2048]{1,0:T(8,128)(2,1)S(1)}, bf16[128,2048]{1,0:T(8,128)(2,1)S(1)}, u32[]{:S(2)}, u32[]{:S(2)}) collective-permute-start(bf16[128,2048]{1,0:T(8,128)(2,1)S(1)} %get-tuple-element.185), channel_id=1, source_target_pairs={{0,1},{1,0},{2,3},{3,2},{4,5},{5,4},{6,7},{7,6},{8,9},{9,8},{10,11... | collective-permute-start | bytes 1572872 | tf_op jit(solution)/shard_map/ppermute | solution.py:323
  124.3 34.4 %collective-permute-start.11 = (bf16[128,2048]{1,0:T(8,128)(2,1)S(1)}, bf16[128,2048]{1,0:T(8,128)(2,1)S(1)}, u32[]{:S(2)}, u32[]{:S(2)}) collective-permute-start(bf16[128,2048]{1,0:T(8,128)(2,1)S(1)} %get-tuple-element.186), channel_id=1, source_target_pairs={{0,3},{1,2},{2,1},{3,0},{4,7},{5,6},{6,5},{7,4},{8,11},{9,10},{10,... | collective-permute-start | bytes 1572872 | tf_op jit(solution)/shard_map/ppermute | solution.py:323
  125.8 33.0 %collective-permute-start.10 = (bf16[128,2048]{1,0:T(8,128)(2,1)S(1)}, bf16[128,2048]{1,0:T(8,128)(2,1)S(1)}, u32[]{:S(2)}, u32[]{:S(2)}) collective-permute-start(bf16[128,2048]{1,0:T(8,128)(2,1)S(1)} %get-tuple-element.187), channel_id=1, source_target_pairs={{0,2},{1,3},{2,0},{3,1},{4,6},{5,7},{6,4},{7,5},{8,10},{9,11},{10,... | collective-permute-start | bytes 1572872 | tf_op jit(solution)/shard_map/ppermute | solution.py:323
  161.4 253.5 %reduce-scatter.2.cloned.1.call-start = ((), (), s32[]{:S(2)}) async-start(), calls=%async_computation.3 | async-start | bytes 9437184 | tf_op jit(solution)/shard_map/reduce_scatter | solution.py:604
  172.8 19.8 %collective-permute-start.14 = (bf16[128,2048]{1,0:T(8,128)(2,1)}, bf16[128,2048]{1,0:T(8,128)(2,1)}, u32[]{:S(2)}, u32[]{:S(2)}) collective-permute-start(bf16[128,2048]{1,0:T(8,128)(2,1)} %add_convert_fusion.1.refs_0_), channel_id=1, source_target_pairs={{0,3},{1,2},{2,1},{3,0},{4,7},{5,6},{6,5},{7,4},{8,11},{9,10},{10,... | collective-permute-start | bytes 1572872 | tf_op jit(solution)/shard_map/ppermute | solution.py:323
  173.3 28.8 %collective-permute-start.13 = (bf16[128,2048]{1,0:T(8,128)(2,1)}, bf16[128,2048]{1,0:T(8,128)(2,1)}, u32[]{:S(2)}, u32[]{:S(2)}) collective-permute-start(bf16[128,2048]{1,0:T(8,128)(2,1)} %add_convert_fusion.1.refs_0_), channel_id=1, source_target_pairs={{0,2},{1,3},{2,0},{3,1},{4,6},{5,7},{6,4},{7,5},{8,10},{9,11},{10,... | collective-permute-start | bytes 1572872 | tf_op jit(solution)/shard_map/ppermute | solution.py:323
  174.9 27.2 %collective-permute-start.12 = (bf16[128,2048]{1,0:T(8,128)(2,1)}, bf16[128,2048]{1,0:T(8,128)(2,1)}, u32[]{:S(2)}, u32[]{:S(2)}) collective-permute-start(bf16[128,2048]{1,0:T(8,128)(2,1)} %add_convert_fusion.1.refs_0_), channel_id=1, source_target_pairs={{0,1},{1,0},{2,3},{3,2},{4,5},{5,4},{6,7},{7,6},{8,9},{9,8},{10,11... | collective-permute-start | bytes 1572872 | tf_op jit(solution)/shard_map/ppermute | solution.py:323
  226.4 27.3 %collective-permute-start.17 = (bf16[128,2048]{1,0:T(8,128)(2,1)S(1)}, bf16[128,2048]{1,0:T(8,128)(2,1)S(1)}, u32[]{:S(2)}, u32[]{:S(2)}) collective-permute-start(bf16[128,2048]{1,0:T(8,128)(2,1)S(1)} %get-tuple-element.188), channel_id=1, source_target_pairs={{0,3},{1,2},{2,1},{3,0},{4,7},{5,6},{6,5},{7,4},{8,11},{9,10},{10,... | collective-permute-start | bytes 1572872 | tf_op jit(solution)/shard_map/ppermute | solution.py:323
  227.9 34.5 %collective-permute-start.16 = (bf16[128,2048]{1,0:T(8,128)(2,1)S(1)}, bf16[128,2048]{1,0:T(8,128)(2,1)S(1)}, u32[]{:S(2)}, u32[]{:S(2)}) collective-permute-start(bf16[128,2048]{1,0:T(8,128)(2,1)S(1)} %get-tuple-element.189), channel_id=1, source_target_pairs={{0,2},{1,3},{2,0},{3,1},{4,6},{5,7},{6,4},{7,5},{8,10},{9,11},{10,... | collective-permute-start | bytes 1572872 | tf_op jit(solution)/shard_map/ppermute | solution.py:323
  229.3 34.5 %collective-permute-start.15 = (bf16[128,2048]{1,0:T(8,128)(2,1)S(1)}, bf16[128,2048]{1,0:T(8,128)(2,1)S(1)}, u32[]{:S(2)}, u32[]{:S(2)}) collective-permute-start(bf16[128,2048]{1,0:T(8,128)(2,1)S(1)} %get-tuple-element.190), channel_id=1, source_target_pairs={{0,1},{1,0},{2,3},{3,2},{4,5},{5,4},{6,7},{7,6},{8,9},{9,8},{10,11... | collective-permute-start | bytes 1572872 | tf_op jit(solution)/shard_map/ppermute | solution.py:323
  280.4 18.9 %collective-permute-start.21 = (bf16[256,1024]{1,0:T(8,128)(2,1)S(1)}, bf16[256,1024]{1,0:T(8,128)(2,1)S(1)}, u32[]{:S(2)}, u32[]{:S(2)}) collective-permute-start(bf16[256,1024]{1,0:T(8,128)(2,1)S(1)} %pad_maximum_fusion.6), channel_id=1, source_target_pairs={{0,1},{1,0},{2,3},{3,2},{4,5},{5,4},{6,7},{7,6},{8,9},{9,8},{10,11... | collective-permute-start | bytes 1572872 | tf_op jit(solution)/shard_map/ppermute | solution.py:323
  281.7 17.7 %collective-permute-start.19 = (bf16[256,1024]{1,0:T(8,128)(2,1)S(1)}, bf16[256,1024]{1,0:T(8,128)(2,1)S(1)}, u32[]{:S(2)}, u32[]{:S(2)}) collective-permute-start(bf16[256,1024]{1,0:T(8,128)(2,1)S(1)} %pad_maximum_fusion.5), channel_id=1, source_target_pairs={{0,2},{1,3},{2,0},{3,1},{4,6},{5,7},{6,4},{7,5},{8,10},{9,11},{10,... | collective-permute-start | bytes 1572872 | tf_op jit(solution)/shard_map/ppermute | solution.py:323
  325.2 185.5 %all-gather.8.cloned.1.call-start = ((), (), s32[]{:S(2)}) async-start(), calls=%async_computation.4 | async-start | bytes 9437184 | tf_op jit(solution)/shard_map/all_gather | solution.py:674
  340.1 36.6 %collective-permute-start.27 = (bf16[128,2048]{1,0:T(8,128)(2,1)}, bf16[128,2048]{1,0:T(8,128)(2,1)}, u32[]{:S(2)}, u32[]{:S(2)}) collective-permute-start(bf16[128,2048]{1,0:T(8,128)(2,1)} %get-tuple-element.182), channel_id=1, source_target_pairs={{0,3},{1,2},{2,1},{3,0},{4,7},{5,6},{6,5},{7,4},{8,11},{9,10},{10,... | collective-permute-start | bytes 1572872 | tf_op jit(solution)/shard_map/ppermute | solution.py:323
  341.5 35.2 %collective-permute-start.26 = (bf16[128,2048]{1,0:T(8,128)(2,1)S(1)}, bf16[128,2048]{1,0:T(8,128)(2,1)}, u32[]{:S(2)}, u32[]{:S(2)}) collective-permute-start(bf16[128,2048]{1,0:T(8,128)(2,1)S(1)} %get-tuple-element.183), channel_id=1, source_target_pairs={{0,2},{1,3},{2,0},{3,1},{4,6},{5,7},{6,4},{7,5},{8,10},{9,11},{10,... | collective-permute-start | bytes 1572872 | tf_op jit(solution)/shard_map/ppermute | solution.py:323
  342.6 34.2 %collective-permute-start.25 = (bf16[128,2048]{1,0:T(8,128)(2,1)S(1)}, bf16[128,2048]{1,0:T(8,128)(2,1)}, u32[]{:S(2)}, u32[]{:S(2)}) collective-permute-start(bf16[128,2048]{1,0:T(8,128)(2,1)S(1)} %get-tuple-element.184), channel_id=1, source_target_pairs={{0,1},{1,0},{2,3},{3,2},{4,5},{5,4},{6,7},{7,6},{8,9},{9,8},{10,11... | collective-permute-start | bytes 1572872 | tf_op jit(solution)/shard_map/ppermute | solution.py:323
  381.6 24.8 %collective-permute-start.24 = (f32[4,512]{1,0:T(4,128)S(1)}, f32[4,512]{1,0:T(4,128)S(1)}, u32[]{:S(2)}, u32[]{:S(2)}) collective-permute-start(f32[4,512]{1,0:T(4,128)S(1)} %get-tuple-element.217), channel_id=1, source_target_pairs={{0,3},{1,2},{2,1},{3,0},{4,7},{5,6},{6,5},{7,4},{8,11},{9,10},{10,... | collective-permute-start | bytes 24584 | tf_op jit(solution)/shard_map/ppermute | solution.py:323
  383.1 23.3 %collective-permute-start.23 = (f32[4,512]{1,0:T(4,128)S(1)}, f32[4,512]{1,0:T(4,128)S(1)}, u32[]{:S(2)}, u32[]{:S(2)}) collective-permute-start(f32[4,512]{1,0:T(4,128)S(1)} %get-tuple-element.218), channel_id=1, source_target_pairs={{0,2},{1,3},{2,0},{3,1},{4,6},{5,7},{6,4},{7,5},{8,10},{9,11},{10,... | collective-permute-start | bytes 24584 | tf_op jit(solution)/shard_map/ppermute | solution.py:323
  384.2 22.3 %collective-permute-start.22 = (f32[4,512]{1,0:T(4,128)S(1)}, f32[4,512]{1,0:T(4,128)S(1)}, u32[]{:S(2)}, u32[]{:S(2)}) collective-permute-start(f32[4,512]{1,0:T(4,128)S(1)} %get-tuple-element.219), channel_id=1, source_target_pairs={{0,1},{1,0},{2,3},{3,2},{4,5},{5,4},{6,7},{7,6},{8,9},{9,8},{10,11... | collective-permute-start | bytes 24584 | tf_op jit(solution)/shard_map/ppermute | solution.py:323
  428.6 51.9 %collective-permute-start.35 = (bf16[1024,2048]{1,0:T(8,128)(2,1)}, bf16[1024,2048]{1,0:T(8,128)(2,1)}, u32[]{:S(2)}, u32[]{:S(2)}) collective-permute-start(bf16[1024,2048]{1,0:T(8,128)(2,1)} %convolution_convert_fusion.2.part_ref), channel_id=1, source_target_pairs={{0,4},{4,0},{8,12},{12,8},{16,20},{20,16},{24,28},{28,24},{1,5},{5... | collective-permute-start | bytes 12582920 | tf_op jit(solution)/shard_map/ppermute | solution.py:411
  453.5 33.6 %collective-permute-start.38 = (bf16[2048,1024]{1,0:T(8,128)(2,1)}, bf16[2048,1024]{1,0:T(8,128)(2,1)}, u32[]{:S(2)}, u32[]{:S(2)}) collective-permute-start(bf16[2048,1024]{1,0:T(8,128)(2,1)} %convolution_convert_fusion.1.part_ref), channel_id=1, source_target_pairs={{0,4},{4,0},{8,12},{12,8},{16,20},{20,16},{24,28},{28,24},{1,5},{5... | collective-permute-start | bytes 12582920 | tf_op jit(solution)/shard_map/ppermute | solution.py:411
  467.3 27.3 %collective-permute-start.34 = (bf16[128,2048]{1,0:T(8,128)(2,1)S(1)}, bf16[128,2048]{1,0:T(8,128)(2,1)S(1)}, u32[]{:S(2)}, u32[]{:S(2)}) collective-permute-start(bf16[128,2048]{1,0:T(8,128)(2,1)S(1)} %get-tuple-element.179), channel_id=1, source_target_pairs={{0,3},{1,2},{2,1},{3,0},{4,7},{5,6},{6,5},{7,4},{8,11},{9,10},{10,... | collective-permute-start | bytes 1572872 | tf_op jit(solution)/shard_map/ppermute | solution.py:323
  468.8 25.8 %collective-permute-start.33 = (bf16[128,2048]{1,0:T(8,128)(2,1)S(1)}, bf16[128,2048]{1,0:T(8,128)(2,1)S(1)}, u32[]{:S(2)}, u32[]{:S(2)}) collective-permute-start(bf16[128,2048]{1,0:T(8,128)(2,1)S(1)} %get-tuple-element.180), channel_id=1, source_target_pairs={{0,2},{1,3},{2,0},{3,1},{4,6},{5,7},{6,4},{7,5},{8,10},{9,11},{10,... | collective-permute-start | bytes 1572872 | tf_op jit(solution)/shard_map/ppermute | solution.py:323
  472.5 22.1 %collective-permute-start.32 = (bf16[128,2048]{1,0:T(8,128)(2,1)S(1)}, bf16[128,2048]{1,0:T(8,128)(2,1)S(1)}, u32[]{:S(2)}, u32[]{:S(2)}) collective-permute-start(bf16[128,2048]{1,0:T(8,128)(2,1)S(1)} %get-tuple-element.181), channel_id=1, source_target_pairs={{0,1},{1,0},{2,3},{3,2},{4,5},{5,4},{6,7},{7,6},{8,9},{9,8},{10,11... | collective-permute-start | bytes 1572872 | tf_op jit(solution)/shard_map/ppermute | solution.py:323
  (55 other events, 765.3 us)
Sparse Core Ops, SparseCore 0:
  11.5 154.4 all-gather.3
  169.4 146.0 all-gather.5
  325.3 89.5 reduce-scatter.1
  428.6 82.0 all-gather.7

commit v6 on v5

--- a/solution.py
+++ b/solution.py
@@ -181,27 +181,32 @@
     )(x, query_grad, key_grad, value_grad, context, grad)
 
 
-def gelu_blocks_body(tile, member_ref, *refs):
-    count = len(refs) - 7
-    blocks, (w_ref, b_ref, g_ref, act_ref, grad_ref, sum_ref, x_ref) = refs[:count], refs[count:]
-    rows = blocks[0].shape[0]
+def gelu_halves_body(tile, steps, member_ref, *refs):
+    pieces, (w_ref, b_ref, g_ref, act_ref, grad_ref, sum_ref, x_ref) = refs[:-7], refs[-7:]
+    rows, width = pieces[0].shape
 
     @pl.when(pl.program_id(0) == 0)
     def _():
-        for k, block in enumerate(blocks):
-            start = pl.multiple_of(member_ref[k] * rows, rows)
-            x_ref[pl.ds(start, rows), :] = block[...]
+        at = 0
+        for side in range(2):
+            for group in steps[side]:
+                for i, k in enumerate(group):
+                    start = pl.multiple_of(member_ref[k] * rows, rows)
+                    part = pieces[at][i * rows : (i + 1) * rows, :]
+                    x_ref[pl.ds(start, rows), side * width : (side + 1) * width] = part
+                at += 1
 
     gelu_tiles(tile, True, x_ref, w_ref, b_ref, g_ref, act_ref, grad_ref, sum_ref)
 
 
-def gelu_product_blocks(blocks, members, weight, bias, grad, col_tile):
-    (rows, depth), count, width = blocks[0].shape, len(blocks), weight.shape[1]
-    tall = count * rows
+def gelu_product_halves(pieces, steps, members, weight, bias, grad, col_tile):
+    parts = [piece for side in pieces for piece in side]
+    tall, width = grad.shape
+    depth = weight.shape[0]
     grid = pltpu.PrefetchScalarGridSpec(
         num_scalar_prefetch=1,
         grid=(width // col_tile,),
-        in_specs=[pl.BlockSpec((rows, depth), lambda j, s: (0, 0))] * count
+        in_specs=[pl.BlockSpec(part.shape, lambda j, s: (0, 0)) for part in parts]
         + [
             pl.BlockSpec((depth, col_tile), lambda j, s: (0, j)),
             pl.BlockSpec((1, col_tile), lambda j, s: (0, j)),
@@ -215,7 +220,7 @@
         scratch_shapes=[pltpu.VMEM((tall, depth), bf16)],
     )
     return pl.pallas_call(
-        functools.partial(gelu_blocks_body, col_tile),
+        functools.partial(gelu_halves_body, col_tile, steps),
         grid_spec=grid,
         out_shape=[jax.ShapeDtypeStruct((tall, width), bf16)] * 2
         + [jax.ShapeDtypeStruct((1, width), f32)],
@@ -225,7 +230,7 @@
             bytes_accessed=2 * (tall * depth + depth * width + 3 * tall * width),
             transcendentals=tall * width,
         ),
-    )(members, *blocks, weight, bias[None], grad)
+    )(members, *parts, weight, bias[None], grad)
 
 
 def qkv_body(count, at_ref, x_ref, own_ref, *refs):
@@ -331,24 +336,76 @@
     return exchange([block] * lax.axis_size("group"))
 
 
-def gather_halves(block):
-    count, width = lax.axis_size("group"), block.shape[1] // 2
-    bits = [1 << b for b in range(count.bit_length() - 1)]
-    held = []
-    for side, path in enumerate((bits, bits[::-1])):
-        held.append((block[:, side * width : (side + 1) * width], [0], path))
-    for turn in range(len(bits)):
-        moved = []
-        for value, members, path in held:
-            bit = path[turn]
-            arrived = swap(value, bit)
-            moved.append((jnp.concatenate([value, arrived]), members + [m ^ bit for m in members], path))
-        held = moved
-    rows, sides = block.shape[0], []
-    for value, members, _ in held:
-        at = {m: value[i * rows : (i + 1) * rows] for i, m in enumerate(members)}
-        sides.append([at[k] for k in range(count)])
-    return sides
+def group_bits():
+    bits = [1 << b for b in range(lax.axis_size("group").bit_length() - 1)]
+    return bits, bits[::-1]
+
+
+def half_columns(block, side):
+    width = block.shape[1] // 2
+    return block[:, side * width : (side + 1) * width]
+
+
+def gather_halves(block, fill=None):
+    pieces = [[half_columns(block, side)] for side in range(2)]
+    steps = [[[0]], [[0]]]
+    paths = group_bits()
+    for turn in range(len(paths[0])):
+        arrived = []
+        for side in range(2):
+            mine = pieces[side]
+            sent = mine[0] if turn == 0 else jnp.concatenate(mine)
+            arrived.append(swap(sent, paths[side][turn]))
+        if fill is not None:
+            arrived = fill(turn, arrived)
+        for side in range(2):
+            known = [k for group in steps[side] for k in group]
+            pieces[side].append(arrived[side])
+            steps[side].append([k ^ paths[side][turn] for k in known])
+    return pieces, steps
+
+
+def ordered_halves(pieces, steps):
+    me = lax.axis_index("group")
+    count = lax.axis_size("group")
+    rows, width = pieces[0][0].shape
+    whole = jnp.zeros((count * rows, 2 * width), pieces[0][0].dtype)
+    for side in range(2):
+        for piece, group in zip(pieces[side], steps[side]):
+            for i, k in enumerate(group):
+                part = piece[i * rows : (i + 1) * rows]
+                whole = lax.dynamic_update_slice(whole, part, ((me ^ k) * rows, side * width))
+    return whole
+
+
+def scatter_halves(partial, fill=None):
+    me = lax.axis_index("group")
+    count = lax.axis_size("group")
+    rows = partial.shape[0] // count
+    blocks = []
+    for side in range(2):
+        columns = half_columns(partial, side)
+        blocks.append(
+            [lax.dynamic_slice_in_dim(columns, (me ^ k) * rows, rows, 0) for k in range(count)]
+        )
+    held = [list(range(count)), list(range(count))]
+    paths = group_bits()[::-1]
+    for turn in range(len(paths[0])):
+        arrived, leaving = [], []
+        for side in range(2):
+            bit = paths[side][turn]
+            leaving.append([k for k in held[side] if k & bit])
+            sent = jnp.concatenate([blocks[side][k] for k in leaving[side]]).astype(bf16)
+            arrived.append(swap(sent, bit))
+        if fill is not None:
+            arrived = fill(turn, arrived)
+        for side in range(2):
+            bit = paths[side][turn]
+            for i, k in enumerate(leaving[side]):
+                part = arrived[side][i * rows : (i + 1) * rows].astype(f32)
+                blocks[side][k ^ bit] = blocks[side][k ^ bit].astype(f32) + part
+            held[side] = [k for k in held[side] if not k & bit]
+    return jnp.concatenate([blocks[0][0], blocks[1][0]], 1).astype(f32)
 
 
 def in_order(blocks):
@@ -559,19 +616,22 @@
     qkv_bias = jnp.concatenate([query_bias, jnp.zeros_like(query_bias), value_bias])
     qkv = qkv_product(attn_in, own, arrived + others, starts, qkv_bias)
     context = attention(qkv)
-    attn_out = scatter_sum(matmul(context, out_weight)) + obias
+    attn_out = scatter_halves(matmul(context, out_weight)) + obias
     hidden = tokens.astype(f32) + active * attn_out
     normed_two, factor_two = layer_norm(hidden)
     ffn_in = (normed_two * gain_two + shift_two).astype(bf16)
     act_grad = nt(branch_all, down_weight).astype(bf16)
-    ffn_blocks = gather_blocks(ffn_in)
-    ffn_blocks = ffn_blocks[:1] + [after(block, act_grad) for block in ffn_blocks[1:]]
+
+    def late_act_grad(turn, arrived):
+        return [after(block, act_grad) for block in arrived] if turn > 0 else arrived
+
+    ffn_held, ffn_steps = gather_halves(ffn_in, late_act_grad)
     ffn_wide = lax.all_gather(ffn_in, everyone, axis=0, tiled=True)
     here = jnp.full((1,), core, jnp.int32)
     ff = up_weight.shape[1]
     members = (me ^ jnp.arange(count, dtype=jnp.int32)).astype(jnp.int32)
-    act_low, pre_grad, _ = gelu_product_blocks(
-        ffn_blocks, members, up_weight, up_bias, act_grad, 256
+    act_low, pre_grad, _ = gelu_product_halves(
+        ffn_held, ffn_steps, members, up_weight, up_bias, act_grad, 256
     )
     order = Order()
     order.mark(act_low, pre_grad)
@@ -588,14 +648,19 @@
     hidden_grad = grad_out + norm_back(ffn_in_grad * gain_two, normed_two, factor_two)
     attn_grad = (active * hidden_grad).astype(bf16)
     order.mark(attn_grad)
-    attn_sides = gather_halves(attn_grad)
-    branch = matmul(order(act_low), down_weight)
-    order.mark(branch)
-    branch_sums = column_sums(order(branch_wide))
-    order.mark(branch_sums)
-
-    attn_sides = order(*(attn_sides[0] + attn_sides[1]))
-    attn_all = in_order([jnp.concatenate(pair, 1) for pair in zip(attn_sides[:count], attn_sides[count:])])
+    side_work = {}
+
+    def meanwhile(turn, arrived):
+        if turn == 0:
+            side_work["branch"] = matmul(order(act_low), down_weight)
+            order.mark(side_work["branch"])
+        else:
+            side_work["sums"] = column_sums(order(branch_wide))
+            order.mark(side_work["sums"])
+        return order(*arrived)
+
+    attn_all = ordered_halves(*gather_halves(attn_grad, meanwhile))
+    branch, branch_sums = side_work["branch"], side_work["sums"]
     context_grad = nt(attn_all, out_weight).astype(bf16)
     qkv_grads = attention_back(qkv, context_grad)
 

time: 531 us -> 522 us (0.983)
  waiting for transfers between devices: 159 us -> 140 us
    ppermute x31 -> x33, waiting for transfers between devices: 126 us -> 111 us  [swap(): return lax.ppermute(block, 'group', [(i, i ^ step) for i in range(count)])]
    unnamed x102 -> x100, local copies, waits for them, and re-layouts: 27.5 us -> 30.3 us
    ppermute x31 -> x33, starting transfers between devices: 36.9 us -> 38.8 us  [swap(): return lax.ppermute(block, 'group', [(i, i ^ step) for i in range(count)])]
  transfers between devices with their start and end apart: 44 -> 46, of which waited for: 21 -> 23; matrix products, arithmetic and copies ran while one was open for 31% -> 32% of each run, Pallas kernels for 19% -> 20%
where the time goes in v6:
time: 522 us; the launch traced here: 516 us
  waiting for transfers between devices  140 us (27%)
  Pallas kernels  108 us (21%)
  matrix products  99.5 us (19%)
  local copies, waits for them, and re-layouts  62.8 us (12%)
  starting transfers between devices  56.4 us (11%)
  other arithmetic  33.5 us (6%)
  between operations  15.8 us (3%)
    ppermute x33, waiting for transfers between devices, swap(): return lax.ppermute(block, 'group', [(i, i ^ step) for i in range(count)])  111 us
    dot_general x5, matrix products, nt(): lax.dot_general(left, right, (((1,), (1,)), ((), ())), preferred_element_...  46.8 us
    dot_general x2, matrix products, tn(): lax.dot_general(left, right, (((0,), (0,)), ((), ())), preferred_element_...  45 us
    ppermute x33, starting transfers between devices, swap(): return lax.ppermute(block, 'group', [(i, i ^ step) for i in range(count)])  38.8 us
    pallas_call x1, Pallas kernels, gelu_product(): pl.pallas_call(functools.partial(gelu_body, min(256, col_tile)), grid_spe...  32.7 us
    unnamed x100, local copies, waits for them, and re-layouts  30.3 us
    pallas_call x4, Pallas kernels, put_half(): pl.pallas_call(put_body, grid_spec=pltpu.PrefetchScalarGridSpec(num_scala...  24.9 us
    all_gather x1, waiting for transfers between devices, shards(): attn_wgrad = lax.all_gather(piece, 'replica', axis=1, tiled=True)  16.1 us
  transfers between devices with their start and end apart: 46, of which 23 were waited for; matrix products, arithmetic and copies ran while one was open for 32% of the time, Pallas kernels for 20%

profile of v6, /device:TPU:0, one launch (start us, length us, event | category | flops | bytes accessed | tf_op | source)
XLA Modules:
  0.0 516.2 jit_solution(4991719651275439640)
XLA Ops:
  17.0 4.0 collective-permute-start.2
  38.4 12.4 %collective-permute-done = bf16[130,2048]{1,0:T(8,128)(2,1)} collective-permute-done((bf16[130,2048]{1,0:T(8,128)(2,1)S(1)}, bf16[130,2048]{1,0:T(8,128)(2,1)}, u32[]{:S(2)}, u32[]{:S(2)}) %collective-permute-start) | collective-permute-done | bytes 532512 | tf_op jit(solution)/shard_map/ppermute | solution.py:328
  65.7 3.8 fusion.5.x_ref
  69.4 28.7 %collective-permute-done.5.refs_2_ = bf16[256,1536]{1,0:T(8,128)(2,1)} collective-permute-done((bf16[256,1536]{1,0:T(8,128)(2,1)}, bf16[256,1536]{1,0:T(8,128)(2,1)}, u32[]{:S(2)}, u32[]{:S(2)}) %collective-permute-start.5) | collective-permute-done | bytes 786464 | tf_op jit(solution)/shard_map/ppermute | solution.py:328
  106.9 5.8 %shard_map.314.q_ref.k_ref.v_ref = bf16[512,1536]{1,0:T(8,128)(2,1)S(1)} custom-call(s32[7]{0:T(128)S(1)} %stack.46.at_ref, bf16[512,2048]{1,0:T(8,128)(2,1)S(1)} %copy-done.11, bf16[512,1536]{1,0:T(8,128)(2,1)S(1)} %copy-done.8, bf16[256,1536]{1,0:T(8,128)(2,1)} %collective-permute-done.3.refs_0_, bf16[256,1536]{1,0:T(8,128)(2,1)S(1)} %collective-permute-done.4.refs_1_, ...), custom_call_target="tpu_custom_call" | custom-call | flops 3221225472 | bytes 9961472 | tf_op jit(solution)/shard_map/pallas_call | solution.py:253
  113.6 7.2 %shard_map.315.context_ref = bf16[512,512]{1,0:T(8,128)(2,1)S(1)} custom-call(bf16[512,1536]{1,0:T(8,128)(2,1)S(1)} %shard_map.314.q_ref.k_ref.v_ref, bf16[512,1536]{1,0:T(8,128)(2,1)S(1)} %shard_map.314.q_ref.k_ref.v_ref, bf16[512,1536]{1,0:T(8,128)(2,1)S(1)} %shard_map.314.q_ref.k_ref.v_ref), custom_call_target="tpu_custom_call" | custom-call | flops 536870912 | bytes 2097152 | tf_op jit(solution)/shard_map/pallas_call | solution.py:93
  126.6 20.0 %collective-permute-done.11 = bf16[256,1024]{1,0:T(8,128)(2,1)S(1)} collective-permute-done((bf16[256,1024]{1,0:T(8,128)(2,1)S(1)}, bf16[256,1024]{1,0:T(8,128)(2,1)S(1)}, u32[]{:S(2)}, u32[]{:S(2)}) %collective-permute-start.11) | collective-permute-done | bytes 524320 | tf_op jit(solution)/shard_map/ppermute | solution.py:328
  148.9 5.9 %collective-permute-done.12 = bf16[128,1024]{1,0:T(8,128)(2,1)S(1)} collective-permute-done((bf16[128,1024]{1,0:T(8,128)(2,1)S(1)}, bf16[128,1024]{1,0:T(8,128)(2,1)S(1)}, u32[]{:S(2)}, u32[]{:S(2)}) %collective-permute-start.12) | collective-permute-done | bytes 262176 | tf_op jit(solution)/shard_map/ppermute | solution.py:328
  158.8 11.4 %reduce-scatter.2.cloned.1.call-start = ((), (), s32[]{:S(2)}) async-start(), calls=%async_computation.3 | async-start | bytes 9437184 | tf_op jit(solution)/shard_map/reduce_scatter | solution.py:669
  172.2 6.1 %collective-permute-done.15.refs_4_ = bf16[128,1024]{1,0:T(8,128)(2,1)S(1)} collective-permute-done((bf16[128,1024]{1,0:T(8,128)(2,1)S(1)}, bf16[128,1024]{1,0:T(8,128)(2,1)S(1)}, u32[]{:S(2)}, u32[]{:S(2)}) %collective-permute-start.15) | collective-permute-done | bytes 262176 | tf_op jit(solution)/shard_map/ppermute | solution.py:328
  182.0 8.6 %convolution_convert_fusion.4.refs_8_ = bf16[512,2048]{1,0:T(8,128)(2,1)S(1)} fusion(bf16[2048,2048]{1,0:T(8,128)(2,1)} %param.35, bf16[4096,2048]{1,0:T(8,128)(2,1)} %all-gather.4.cloned.1.call-done, s32[]{:T(128)S(6)} %select_n.167), kind=kOutput, calls=%fused_computation.18 | convolution fusion | flops 4296015872 | bytes 12582916 | tf_op jit(solution)/shard_map/dot_general | solution.py:37
  197.1 12.6 %shard_map.316 = (bf16[512,2048]{1,0:T(8,128)(2,1)S(1)}, bf16[512,2048]{1,0:T(8,128)(2,1)S(1)}, f32[1,2048]{1,0:T(1,128)}) custom-call(s32[4]{0:T(128)S(1)} %iota_xor_fusion.member_ref, bf16[128,1024]{1,0:T(8,128)(2,1)S(1)} %get-tuple-element.202.refs_0_, bf16[128,1024]{1,0:T(8,128)(2,1)} %collective-permute-done.13.refs_1_, ...), custom_call_target="tpu_custom_call" | custom-call | flops 4294967296 | bytes 16777216 | tf_op jit(solution)/shard_map/pallas_call | solution.py:222
  209.7 8.1 %convolution_convert_fusion.3 = bf16[512,2048]{1,0:T(8,128)(2,1)S(1)} fusion(bf16[512,2048]{1,0:T(8,128)(2,1)S(1)} %get-tuple-element.93, bf16[2048,2048]{1,0:T(8,128)(2,1)} %refs_1_.1), kind=kOutput, calls=%fused_computation.17 | convolution fusion | flops 4296015872 | bytes 12582912 | tf_op jit(solution)/shard_map/dot_general | solution.py:37
  221.7 23.6 %convolution_convert_fusion.refs_3_ = bf16[4096,1024]{1,0:T(8,128)(2,1)} fusion(bf16[4096,2048]{1,0:T(8,128)(2,1)} %all-gather.4.cloned.1.call-done, bf16[2048,2048]{1,0:T(8,128)(2,1)} %param.35, s32[]{:T(128)S(6)} %select_n.168), kind=kOutput, calls=%fused_computation.1 | convolution fusion | flops 17184063488 | bytes 29360132 | tf_op jit(solution)/shard_map/dot_general | solution.py:37
  245.3 7.6 %collective-permute-done.18 = bf16[128,2048]{1,0:T(8,128)(2,1)S(1)} collective-permute-done((bf16[128,2048]{1,0:T(8,128)(2,1)S(1)}, bf16[128,2048]{1,0:T(8,128)(2,1)S(1)}, u32[]{:S(2)}, u32[]{:S(2)}) %collective-permute-start.18) | collective-permute-done | bytes 524320 | tf_op jit(solution)/shard_map/ppermute | solution.py:328
  260.1 6.4 %fusion.38 = f32[512,2048]{1,0:T(8,128)} fusion(bf16[512,2048]{1,0:T(8,128)(2,1)S(1)} %get-tuple-element.99, bf16[2048,2048]{1,0:T(8,128)(2,1)S(1)} %bitcast.98), kind=kOutput, calls=%fused_computation.156 | convolution fusion | flops 4294967296 | bytes 14680064 | tf_op jit(solution)/shard_map/dot_general | solution.py:319
  266.6 5.6 %collective-permute-done.21 = bf16[128,1024]{1,0:T(8,128)(2,1)S(1)} collective-permute-done((bf16[128,1024]{1,0:T(8,128)(2,1)S(1)}, bf16[128,1024]{1,0:T(8,128)(2,1)S(1)}, u32[]{:S(2)}, u32[]{:S(2)}) %collective-permute-start.21) | collective-permute-done | bytes 262176 | tf_op jit(solution)/shard_map/ppermute | solution.py:328
  275.3 4.5 convert_reduce_fusion
  279.9 9.9 %collective-permute-done.23 = bf16[256,1024]{1,0:T(8,128)(2,1)S(1)} collective-permute-done((bf16[256,1024]{1,0:T(8,128)(2,1)S(1)}, bf16[256,1024]{1,0:T(8,128)(2,1)S(1)}, u32[]{:S(2)}, u32[]{:S(2)}) %collective-permute-start.23) | collective-permute-done | bytes 524320 | tf_op jit(solution)/shard_map/ppermute | solution.py:328
  292.2 13.3 %shard_map.317 = (bf16[512,512]{1,0:T(8,128)(2,1)S(1)}, bf16[512,512]{1,0:T(8,128)(2,1)S(1)}, bf16[512,512]{1,0:T(8,128)(2,1)S(1)}) custom-call(bf16[512,1536]{1,0:T(8,128)(2,1)S(1)} %copy-done.3, bf16[512,1536]{1,0:T(8,128)(2,1)S(1)} %copy-done.3, bf16[512,1536]{1,0:T(8,128)(2,1)S(1)} %copy-done.3, bf16[512,512]{1,0:T(8,128)(2,1)S(1)} %convolution_convert_fusion.5.g_ref), custom_call_target="tpu_custom_call" | custom-call | flops 1342177280 | bytes 3670016 | tf_op jit(solution)/shard_map/pallas_call | solution.py:106
  305.6 5.5 %shard_map.318 = bf16[4,512,2048]{2,1,0:T(8,128)(2,1)S(1)} custom-call(bf16[512,2048]{1,0:T(8,128)(2,1)S(1)} %copy-done.12, bf16[512,512]{1,0:T(8,128)(2,1)S(1)} %get-tuple-element.105.q_ref, bf16[512,512]{1,0:T(8,128)(2,1)S(1)} %get-tuple-element.106.k_ref, bf16[512,512]{1,0:T(8,128)(2,1)S(1)} %get-tuple-element.107.v_ref, ...), custom_call_target="tpu_custom_call" | custom-call | flops 4294967296 | bytes 14680064 | tf_op jit(solution)/shard_map/pallas_call | solution.py:169
  323.4 5.2 %fusion.6 = (f32[2048]{0:T(1024)S(1)}, f32[2048]{0:T(1024)S(1)}, f32[512,2048]{1,0:T(8,128)S(1)}) fusion(bf16[512,2048]{1,0:T(8,128)(2,1)} %slice_dynamic-update-slice_fusion, f32[512]{0:T(512)S(1)} %add_rsqrt_fusion, f32[512]{0:T(512)S(1)} %broadcast_multiply_fusion, bf16[512,1536]{1,0:T(8,128)(2,1)S(1)} %constant_dynamic-update-slice_fusion.12, ...), kind=kOutput, calls=%fused_computation.10 | convolution fusion | flops 3227512832 | bytes 14176256 | tf_op jit(solution)/shard_map/dot_general | solution.py:37
  333.6 32.7 %shard_map.319 = (bf16[4096,1024]{1,0:T(8,128)(2,1)S(1)}, bf16[4096,1024]{1,0:T(8,128)(2,1)S(1)}, f32[1,1024]{1,0:T(1,128)S(1)}) custom-call(s32[1]{0:T(128)} %bitcast.22.place_ref, bf16[4096,2048]{1,0:T(8,128)(2,1)} %all-gather.6.cloned.1.call-done.refs_0_, bf16[2048,2048]{1,0:T(8,128)(2,1)} %refs_1_.1, ...), custom_call_target="tpu_custom_call" | custom-call | flops 17179869184 | bytes 46137344 | tf_op jit(solution)/shard_map/pallas_call | solution.py:150
  376.5 21.3 %convolution_convert_fusion.2.part_ref = bf16[1024,2048]{1,0:T(8,128)(2,1)} fusion(bf16[4096,1024]{1,0:T(8,128)(2,1)S(1)} %get-tuple-element.124, bf16[4096,2048]{1,0:T(8,128)(2,1)} %all-gather.4.cloned.1.call-done), kind=kOutput, calls=%fused_computation.15 | convolution fusion | flops 17181966336 | bytes 29360128 | tf_op jit(solution)/shard_map/dot_general | solution.py:39
  397.8 6.3 %reduce-scatter.2.cloned.1.call-done = bf16[4,64,2048]{2,1,0:T(8,128)(2,1)} async-done(((bf16[4,512,2048]{2,1,0:T(8,128)(2,1)}), bf16[4,64,2048]{2,1,0:T(8,128)(2,1)}) %reduce-scatter.2.cloned.1.call-update) | async-done | bytes 1048592 | tf_op jit(solution)/shard_map/reduce_scatter | solution.py:669
  418.9 23.7 %convolution_convert_fusion.1.part_ref = bf16[2048,1024]{1,0:T(8,128)(2,1)} fusion(bf16[4096,2048]{1,0:T(8,128)(2,1)} %all-gather.6.cloned.1.call-done.refs_0_, bf16[4096,1024]{1,0:T(8,128)(2,1)} %copy-done.20), kind=kOutput, calls=%fused_computation.14 | convolution fusion | flops 17181966336 | bytes 29360128 | tf_op jit(solution)/shard_map/dot_general | solution.py:39
  449.5 4.2 shard_map.320.refs_0_
  460.7 7.3 %shard_map.321.refs_0_ = f32[2048,2048]{1,0:T(8,128)} custom-call(s32[1]{0:T(128)} %bitcast.22.place_ref, bf16[2048,1024]{1,0:T(8,128)(2,1)} %convolution_convert_fusion.1.part_ref), custom_call_target="tpu_custom_call" | custom-call | bytes 12582912 | tf_op jit(solution)/shard_map/pallas_call | solution.py:289
  468.1 6.0 %shard_map.322 = f32[2048,2048]{1,0:T(8,128)} custom-call(s32[1]{0:T(128)S(6)} %sub.68.place_ref, bf16[1024,2048]{1,0:T(8,128)(2,1)} %collective-permute-done.37.part_ref, f32[2048,2048]{1,0:T(8,128)} %shard_map.320.refs_0_), custom_call_target="tpu_custom_call", output_to_operand_aliasing={{}: (2, {})} | custom-call | bytes 12582912 | tf_op jit(solution)/shard_map/pallas_call | solution.py:289
  474.7 7.4 %shard_map.323 = f32[2048,2048]{1,0:T(8,128)} custom-call(s32[1]{0:T(128)S(6)} %sub.68.place_ref, bf16[2048,1024]{1,0:T(8,128)(2,1)} %collective-permute-done.40.part_ref, f32[2048,2048]{1,0:T(8,128)} %shard_map.321.refs_0_), custom_call_target="tpu_custom_call", output_to_operand_aliasing={{}: (2, {})} | custom-call | bytes 12582912 | tf_op jit(solution)/shard_map/pallas_call | solution.py:289
  483.8 16.1 %all-gather.8.cloned.1.call-done.block_ref = bf16[4,512,2048]{2,1,0:T(8,128)(2,1)} async-done(((bf16[4,64,2048]{2,1,0:T(8,128)(2,1)}), bf16[4,512,2048]{2,1,0:T(8,128)(2,1)}) %all-gather.8.cloned.1.call-update) | async-done | bytes 8388624 | tf_op jit(solution)/shard_map/all_gather | solution.py:739
  503.3 6.2 %shard_map.324 = (f32[512,2048]{1,0:T(8,128)}, f32[512,2048]{1,0:T(8,128)}, f32[512,2048]{1,0:T(8,128)}, f32[512,2048]{1,0:T(8,128)}) custom-call(bf16[4,512,2048]{2,1,0:T(8,128)(2,1)S(1)} %copy-done.5), custom_call_target="tpu_custom_call" | custom-call | bytes 25165824 | tf_op jit(solution)/shard_map/pallas_call | solution.py:305
  (304 shorter events, 152.9 us)
Async XLA Ops:
  7.2 174.8 %all-gather.4.cloned.1.call-start = ((), (), s32[]{:S(2)}) async-start(), calls=%async_computation.1 | async-start | bytes 17301504 | tf_op jit(solution)/shard_map/all_gather | solution.py:612
  10.7 322.8 %all-gather.6.cloned.1.call-start = ((), (), s32[]{:S(2)}) async-start(), calls=%async_computation.2 | async-start | bytes 17301504 | tf_op jit(solution)/shard_map/all_gather | solution.py:629
  17.0 39.0 %collective-permute-start.2 = (bf16[130,2048]{1,0:T(8,128)(2,1)S(1)}, bf16[130,2048]{1,0:T(8,128)(2,1)}, u32[]{:S(2)}, u32[]{:S(2)}) collective-permute-start(bf16[130,2048]{1,0:T(8,128)(2,1)S(1)} %pad_maximum_fusion.4), channel_id=1, source_target_pairs={{0,3},{1,2},{2,1},{3,0},{4,7},{5,6},{6,5},{7,4},{8,11},{9,10},{10,... | collective-permute-start | bytes 1597448 | tf_op jit(solution)/shard_map/ppermute | solution.py:328
  21.0 33.2 %collective-permute-start.1 = (bf16[130,2048]{1,0:T(8,128)(2,1)S(1)}, bf16[130,2048]{1,0:T(8,128)(2,1)}, u32[]{:S(2)}, u32[]{:S(2)}) collective-permute-start(bf16[130,2048]{1,0:T(8,128)(2,1)S(1)} %pad_maximum_fusion.4), channel_id=1, source_target_pairs={{0,2},{1,3},{2,0},{3,1},{4,6},{5,7},{6,4},{7,5},{8,10},{9,11},{10,... | collective-permute-start | bytes 1597448 | tf_op jit(solution)/shard_map/ppermute | solution.py:328
  21.5 29.4 %collective-permute-start = (bf16[130,2048]{1,0:T(8,128)(2,1)S(1)}, bf16[130,2048]{1,0:T(8,128)(2,1)}, u32[]{:S(2)}, u32[]{:S(2)}) collective-permute-start(bf16[130,2048]{1,0:T(8,128)(2,1)S(1)} %pad_maximum_fusion.4), channel_id=1, source_target_pairs={{0,1},{1,0},{2,3},{3,2},{4,5},{5,4},{6,7},{7,6},{8,9},{9,8},{10,11... | collective-permute-start | bytes 1597448 | tf_op jit(solution)/shard_map/ppermute | solution.py:328
  26.8 71.3 %collective-permute-start.4 = (bf16[256,1536]{1,0:T(8,128)(2,1)}, bf16[256,1536]{1,0:T(8,128)(2,1)S(1)}, u32[]{:S(2)}, u32[]{:S(2)}) collective-permute-start(bf16[256,1536]{1,0:T(8,128)(2,1)} %pad_maximum_fusion.2), channel_id=1, source_target_pairs={{0,2},{1,3},{2,0},{3,1},{4,6},{5,7},{6,4},{7,5},{8,10},{9,11},{10,... | collective-permute-start | bytes 2359304 | tf_op jit(solution)/shard_map/ppermute | solution.py:328
  29.6 68.5 %collective-permute-start.3 = (bf16[256,1536]{1,0:T(8,128)(2,1)}, bf16[256,1536]{1,0:T(8,128)(2,1)}, u32[]{:S(2)}, u32[]{:S(2)}) collective-permute-start(bf16[256,1536]{1,0:T(8,128)(2,1)} %pad_maximum_fusion.1), channel_id=1, source_target_pairs={{0,1},{1,0},{2,3},{3,2},{4,5},{5,4},{6,7},{7,6},{8,9},{9,8},{10,11... | collective-permute-start | bytes 2359304 | tf_op jit(solution)/shard_map/ppermute | solution.py:328
  50.9 47.2 %collective-permute-start.5 = (bf16[256,1536]{1,0:T(8,128)(2,1)}, bf16[256,1536]{1,0:T(8,128)(2,1)}, u32[]{:S(2)}, u32[]{:S(2)}) collective-permute-start(bf16[256,1536]{1,0:T(8,128)(2,1)} %pad_maximum_fusion.3), channel_id=1, source_target_pairs={{0,3},{1,2},{2,1},{3,0},{4,7},{5,6},{6,5},{7,4},{8,11},{9,10},{10,... | collective-permute-start | bytes 2359304 | tf_op jit(solution)/shard_map/ppermute | solution.py:328
  122.9 23.7 %collective-permute-start.11 = (bf16[256,1024]{1,0:T(8,128)(2,1)S(1)}, bf16[256,1024]{1,0:T(8,128)(2,1)S(1)}, u32[]{:S(2)}, u32[]{:S(2)}) collective-permute-start(bf16[256,1024]{1,0:T(8,128)(2,1)S(1)} %pad_maximum_fusion.6), channel_id=1, source_target_pairs={{0,1},{1,0},{2,3},{3,2},{4,5},{5,4},{6,7},{7,6},{8,9},{9,8},{10,11... | collective-permute-start | bytes 1572872 | tf_op jit(solution)/shard_map/ppermute | solution.py:328
  124.9 23.3 %collective-permute-start.9 = (bf16[256,1024]{1,0:T(8,128)(2,1)S(1)}, bf16[256,1024]{1,0:T(8,128)(2,1)S(1)}, u32[]{:S(2)}, u32[]{:S(2)}) collective-permute-start(bf16[256,1024]{1,0:T(8,128)(2,1)S(1)} %pad_maximum_fusion.5), channel_id=1, source_target_pairs={{0,2},{1,3},{2,0},{3,1},{4,6},{5,7},{6,4},{7,5},{8,10},{9,11},{10,... | collective-permute-start | bytes 1572872 | tf_op jit(solution)/shard_map/ppermute | solution.py:328
  158.8 245.4 %reduce-scatter.2.cloned.1.call-start = ((), (), s32[]{:S(2)}) async-start(), calls=%async_computation.3 | async-start | bytes 9437184 | tf_op jit(solution)/shard_map/reduce_scatter | solution.py:669
  179.1 14.6 %collective-permute-start.16 = (bf16[256,1024]{1,0:T(8,128)(2,1)}, bf16[256,1024]{1,0:T(8,128)(2,1)}, u32[]{:S(2)}, u32[]{:S(2)}) collective-permute-start(bf16[256,1024]{1,0:T(8,128)(2,1)} %pad_maximum_fusion.8), channel_id=1, source_target_pairs={{0,1},{1,0},{2,3},{3,2},{4,5},{5,4},{6,7},{7,6},{8,9},{9,8},{10,11... | collective-permute-start | bytes 1572872 | tf_op jit(solution)/shard_map/ppermute | solution.py:328
  181.5 12.3 %collective-permute-start.14 = (bf16[256,1024]{1,0:T(8,128)(2,1)}, bf16[256,1024]{1,0:T(8,128)(2,1)}, u32[]{:S(2)}, u32[]{:S(2)}) collective-permute-start(bf16[256,1024]{1,0:T(8,128)(2,1)} %pad_maximum_fusion.7), channel_id=1, source_target_pairs={{0,2},{1,3},{2,0},{3,1},{4,6},{5,7},{6,4},{7,5},{8,10},{9,11},{10,... | collective-permute-start | bytes 1572872 | tf_op jit(solution)/shard_map/ppermute | solution.py:328
  218.1 27.2 %collective-permute-start.19 = (bf16[128,2048]{1,0:T(8,128)(2,1)S(1)}, bf16[128,2048]{1,0:T(8,128)(2,1)S(1)}, u32[]{:S(2)}, u32[]{:S(2)}) collective-permute-start(bf16[128,2048]{1,0:T(8,128)(2,1)S(1)} %get-tuple-element.177), channel_id=1, source_target_pairs={{0,3},{1,2},{2,1},{3,0},{4,7},{5,6},{6,5},{7,4},{8,11},{9,10},{10,... | collective-permute-start | bytes 1572872 | tf_op jit(solution)/shard_map/ppermute | solution.py:328
  219.5 33.4 %collective-permute-start.18 = (bf16[128,2048]{1,0:T(8,128)(2,1)S(1)}, bf16[128,2048]{1,0:T(8,128)(2,1)S(1)}, u32[]{:S(2)}, u32[]{:S(2)}) collective-permute-start(bf16[128,2048]{1,0:T(8,128)(2,1)S(1)} %get-tuple-element.178), channel_id=1, source_target_pairs={{0,2},{1,3},{2,0},{3,1},{4,6},{5,7},{6,4},{7,5},{8,10},{9,11},{10,... | collective-permute-start | bytes 1572872 | tf_op jit(solution)/shard_map/ppermute | solution.py:328
  221.4 34.4 %collective-permute-start.17 = (bf16[128,2048]{1,0:T(8,128)(2,1)S(1)}, bf16[128,2048]{1,0:T(8,128)(2,1)S(1)}, u32[]{:S(2)}, u32[]{:S(2)}) collective-permute-start(bf16[128,2048]{1,0:T(8,128)(2,1)S(1)} %get-tuple-element.179), channel_id=1, source_target_pairs={{0,1},{1,0},{2,3},{3,2},{4,5},{5,4},{6,7},{7,6},{8,9},{9,8},{10,11... | collective-permute-start | bytes 1572872 | tf_op jit(solution)/shard_map/ppermute | solution.py:328
  258.7 13.5 %collective-permute-start.21 = (bf16[128,1024]{1,0:T(8,128)(2,1)S(1)}, bf16[128,1024]{1,0:T(8,128)(2,1)S(1)}, u32[]{:S(2)}, u32[]{:S(2)}) collective-permute-start(bf16[128,1024]{1,0:T(8,128)(2,1)S(1)} %get-tuple-element.198), channel_id=1, source_target_pairs={{0,2},{1,3},{2,0},{3,1},{4,6},{5,7},{6,4},{7,5},{8,10},{9,11},{10,... | collective-permute-start | bytes 786440 | tf_op jit(solution)/shard_map/ppermute | solution.py:328
  258.8 13.9 %collective-permute-start.20 = (bf16[128,1024]{1,0:T(8,128)(2,1)S(1)}, bf16[128,1024]{1,0:T(8,128)(2,1)S(1)}, u32[]{:S(2)}, u32[]{:S(2)}) collective-permute-start(bf16[128,1024]{1,0:T(8,128)(2,1)S(1)} %get-tuple-element.200), channel_id=1, source_target_pairs={{0,1},{1,0},{2,3},{3,2},{4,5},{5,4},{6,7},{7,6},{8,9},{9,8},{10,11... | collective-permute-start | bytes 786440 | tf_op jit(solution)/shard_map/ppermute | solution.py:328
  272.7 17.2 %collective-permute-start.23 = (bf16[256,1024]{1,0:T(8,128)(2,1)S(1)}, bf16[256,1024]{1,0:T(8,128)(2,1)S(1)}, u32[]{:S(2)}, u32[]{:S(2)}) collective-permute-start(bf16[256,1024]{1,0:T(8,128)(2,1)S(1)} %pad_maximum_fusion.10), channel_id=1, source_target_pairs={{0,1},{1,0},{2,3},{3,2},{4,5},{5,4},{6,7},{7,6},{8,9},{9,8},{10,11... | collective-permute-start | bytes 1572872 | tf_op jit(solution)/shard_map/ppermute | solution.py:328
  274.0 15.8 %collective-permute-start.22 = (bf16[256,1024]{1,0:T(8,128)(2,1)S(1)}, bf16[256,1024]{1,0:T(8,128)(2,1)S(1)}, u32[]{:S(2)}, u32[]{:S(2)}) collective-permute-start(bf16[256,1024]{1,0:T(8,128)(2,1)S(1)} %pad_maximum_fusion.9), channel_id=1, source_target_pairs={{0,2},{1,3},{2,0},{3,1},{4,6},{5,7},{6,4},{7,5},{8,10},{9,11},{10,... | collective-permute-start | bytes 1572872 | tf_op jit(solution)/shard_map/ppermute | solution.py:328
  314.6 185.3 %all-gather.8.cloned.1.call-start = ((), (), s32[]{:S(2)}) async-start(), calls=%async_computation.4 | async-start | bytes 9437184 | tf_op jit(solution)/shard_map/all_gather | solution.py:739
  329.6 40.0 %collective-permute-start.29 = (bf16[128,2048]{1,0:T(8,128)(2,1)}, bf16[128,2048]{1,0:T(8,128)(2,1)}, u32[]{:S(2)}, u32[]{:S(2)}) collective-permute-start(bf16[128,2048]{1,0:T(8,128)(2,1)} %get-tuple-element.172), channel_id=1, source_target_pairs={{0,3},{1,2},{2,1},{3,0},{4,7},{5,6},{6,5},{7,4},{8,11},{9,10},{10,... | collective-permute-start | bytes 1572872 | tf_op jit(solution)/shard_map/ppermute | solution.py:328
  330.9 38.7 %collective-permute-start.28 = (bf16[128,2048]{1,0:T(8,128)(2,1)S(1)}, bf16[128,2048]{1,0:T(8,128)(2,1)}, u32[]{:S(2)}, u32[]{:S(2)}) collective-permute-start(bf16[128,2048]{1,0:T(8,128)(2,1)S(1)} %get-tuple-element.173), channel_id=1, source_target_pairs={{0,2},{1,3},{2,0},{3,1},{4,6},{5,7},{6,4},{7,5},{8,10},{9,11},{10,... | collective-permute-start | bytes 1572872 | tf_op jit(solution)/shard_map/ppermute | solution.py:328
  331.7 38.0 %collective-permute-start.27 = (bf16[128,2048]{1,0:T(8,128)(2,1)S(1)}, bf16[128,2048]{1,0:T(8,128)(2,1)}, u32[]{:S(2)}, u32[]{:S(2)}) collective-permute-start(bf16[128,2048]{1,0:T(8,128)(2,1)S(1)} %get-tuple-element.174), channel_id=1, source_target_pairs={{0,1},{1,0},{2,3},{3,2},{4,5},{5,4},{6,7},{7,6},{8,9},{9,8},{10,11... | collective-permute-start | bytes 1572872 | tf_op jit(solution)/shard_map/ppermute | solution.py:328
  373.0 24.8 %collective-permute-start.26 = (f32[4,512]{1,0:T(4,128)S(1)}, f32[4,512]{1,0:T(4,128)S(1)}, u32[]{:S(2)}, u32[]{:S(2)}) collective-permute-start(f32[4,512]{1,0:T(4,128)S(1)} %get-tuple-element.209), channel_id=1, source_target_pairs={{0,3},{1,2},{2,1},{3,0},{4,7},{5,6},{6,5},{7,4},{8,11},{9,10},{10,... | collective-permute-start | bytes 24584 | tf_op jit(solution)/shard_map/ppermute | solution.py:328
  374.3 23.5 %collective-permute-start.25 = (f32[4,512]{1,0:T(4,128)S(1)}, f32[4,512]{1,0:T(4,128)S(1)}, u32[]{:S(2)}, u32[]{:S(2)}) collective-permute-start(f32[4,512]{1,0:T(4,128)S(1)} %get-tuple-element.210), channel_id=1, source_target_pairs={{0,2},{1,3},{2,0},{3,1},{4,6},{5,7},{6,4},{7,5},{8,10},{9,11},{10,... | collective-permute-start | bytes 24584 | tf_op jit(solution)/shard_map/ppermute | solution.py:328
  375.1 22.7 %collective-permute-start.24 = (f32[4,512]{1,0:T(4,128)S(1)}, f32[4,512]{1,0:T(4,128)S(1)}, u32[]{:S(2)}, u32[]{:S(2)}) collective-permute-start(f32[4,512]{1,0:T(4,128)S(1)} %get-tuple-element.211), channel_id=1, source_target_pairs={{0,1},{1,0},{2,3},{3,2},{4,5},{5,4},{6,7},{7,6},{8,9},{9,8},{10,11... | collective-permute-start | bytes 24584 | tf_op jit(solution)/shard_map/ppermute | solution.py:328
  417.8 50.3 %collective-permute-start.37 = (bf16[1024,2048]{1,0:T(8,128)(2,1)}, bf16[1024,2048]{1,0:T(8,128)(2,1)}, u32[]{:S(2)}, u32[]{:S(2)}) collective-permute-start(bf16[1024,2048]{1,0:T(8,128)(2,1)} %convolution_convert_fusion.2.part_ref), channel_id=1, source_target_pairs={{0,4},{4,0},{8,12},{12,8},{16,20},{20,16},{24,28},{28,24},{1,5},{5... | collective-permute-start | bytes 12582920 | tf_op jit(solution)/shard_map/ppermute | solution.py:468
  442.7 32.0 %collective-permute-start.40 = (bf16[2048,1024]{1,0:T(8,128)(2,1)}, bf16[2048,1024]{1,0:T(8,128)(2,1)}, u32[]{:S(2)}, u32[]{:S(2)}) collective-permute-start(bf16[2048,1024]{1,0:T(8,128)(2,1)} %convolution_convert_fusion.1.part_ref), channel_id=1, source_target_pairs={{0,4},{4,0},{8,12},{12,8},{16,20},{20,16},{24,28},{28,24},{1,5},{5... | collective-permute-start | bytes 12582920 | tf_op jit(solution)/shard_map/ppermute | solution.py:468
  456.5 25.6 %collective-permute-start.36 = (bf16[128,2048]{1,0:T(8,128)(2,1)S(1)}, bf16[128,2048]{1,0:T(8,128)(2,1)S(1)}, u32[]{:S(2)}, u32[]{:S(2)}) collective-permute-start(bf16[128,2048]{1,0:T(8,128)(2,1)S(1)} %get-tuple-element.169), channel_id=1, source_target_pairs={{0,3},{1,2},{2,1},{3,0},{4,7},{5,6},{6,5},{7,4},{8,11},{9,10},{10,... | collective-permute-start | bytes 1572872 | tf_op jit(solution)/shard_map/ppermute | solution.py:328
  458.0 24.6 %collective-permute-start.35 = (bf16[128,2048]{1,0:T(8,128)(2,1)S(1)}, bf16[128,2048]{1,0:T(8,128)(2,1)S(1)}, u32[]{:S(2)}, u32[]{:S(2)}) collective-permute-start(bf16[128,2048]{1,0:T(8,128)(2,1)S(1)} %get-tuple-element.170), channel_id=1, source_target_pairs={{0,2},{1,3},{2,0},{3,1},{4,6},{5,7},{6,4},{7,5},{8,10},{9,11},{10,... | collective-permute-start | bytes 1572872 | tf_op jit(solution)/shard_map/ppermute | solution.py:328
  459.2 23.5 %collective-permute-start.34 = (bf16[128,2048]{1,0:T(8,128)(2,1)S(1)}, bf16[128,2048]{1,0:T(8,128)(2,1)S(1)}, u32[]{:S(2)}, u32[]{:S(2)}) collective-permute-start(bf16[128,2048]{1,0:T(8,128)(2,1)S(1)} %get-tuple-element.171), channel_id=1, source_target_pairs={{0,1},{1,0},{2,3},{3,2},{4,5},{5,4},{6,7},{7,6},{8,9},{9,8},{10,11... | collective-permute-start | bytes 1572872 | tf_op jit(solution)/shard_map/ppermute | solution.py:328
  (56 other events, 624.0 us)
Sparse Core Ops, SparseCore 0:
  11.5 153.9 all-gather.3
  169.0 136.7 all-gather.5
  314.7 89.3 reduce-scatter.1
  417.8 82.0 all-gather.7

commit v7 on v6

--- a/solution.py
+++ b/solution.py
@@ -640,15 +640,19 @@
 
     partial = nt(pre_grad, up_weight).astype(bf16)
     order.mark(partial)
-    ffn_in_grad = scatter_terms(partial)
-    wide_grad = nt(order(branch_wide), down_half).astype(bf16)
-    order.mark(wide_grad)
-
-    ffn_in_grad = add_terms(order(*ffn_in_grad))
+    side_work = {}
+
+    def product_meanwhile(turn, arrived):
+        if turn == 0:
+            side_work["wide"] = nt(order(branch_wide), down_half).astype(bf16)
+            order.mark(side_work["wide"])
+        return order(*arrived)
+
+    ffn_in_grad = scatter_halves(partial, product_meanwhile)
+    wide_grad = side_work["wide"]
     hidden_grad = grad_out + norm_back(ffn_in_grad * gain_two, normed_two, factor_two)
     attn_grad = (active * hidden_grad).astype(bf16)
     order.mark(attn_grad)
-    side_work = {}
 
     def meanwhile(turn, arrived):
         if turn == 0:

time: 522 us -> 522 us (level)
  starting transfers between devices: 56.4 us -> 44.9 us
  matrix products: 99.5 us -> 107 us
    reduce_scatter x1, starting transfers between devices: 11.4 us -> 0.3 us  [shards(): piece = lax.psum_scatter(parts, 'replica', scatter_dimension=1, tiled=True)]
    dot_general x2, matrix products: 7.7 us -> 16.1 us  [matmul(): return jnp.dot(left, right, preferred_element_type=f32)]
    ppermute x33 -> x34, waiting for transfers between devices: 111 us -> 107 us  [swap(): return lax.ppermute(block, 'group', [(i, i ^ step) for i in range(count)])]
    ppermute x33 -> x34, starting transfers between devices: 38.8 us -> 38.5 us  [swap(): return lax.ppermute(block, 'group', [(i, i ^ step) for i in range(count)])]
  transfers between devices with their start and end apart: 46 -> 47, of which waited for: 23 -> 21; matrix products, arithmetic and copies ran while one was open for 32% -> 34% of each run, Pallas kernels for 20% -> 20%
where the time goes in v7:
time: 522 us; the launch traced here: 512 us
  waiting for transfers between devices  137 us (26%)
  Pallas kernels  108 us (21%)
  matrix products  107 us (20%)
  local copies, waits for them, and re-layouts  65 us (12%)
  starting transfers between devices  44.9 us (9%)
  other arithmetic  33.7 us (6%)
  between operations  16.1 us (3%)
    ppermute x34, waiting for transfers between devices, swap(): return lax.ppermute(block, 'group', [(i, i ^ step) for i in range(count)])  107 us
    dot_general x5, matrix products, nt(): lax.dot_general(left, right, (((1,), (1,)), ((), ())), preferred_element_...  46.1 us
    dot_general x2, matrix products, tn(): lax.dot_general(left, right, (((0,), (0,)), ((), ())), preferred_element_...  45 us
    ppermute x34, starting transfers between devices, swap(): return lax.ppermute(block, 'group', [(i, i ^ step) for i in range(count)])  38.5 us
    pallas_call x1, Pallas kernels, gelu_product(): pl.pallas_call(functools.partial(gelu_body, min(256, col_tile)), grid_spe...  32.7 us
    unnamed x100, local copies, waits for them, and re-layouts  30.1 us
    pallas_call x4, Pallas kernels, put_half(): pl.pallas_call(put_body, grid_spec=pltpu.PrefetchScalarGridSpec(num_scala...  24.9 us
    dot_general x2, matrix products, matmul(): return jnp.dot(left, right, preferred_element_type=f32)  16.1 us
  transfers between devices with their start and end apart: 47, of which 21 were waited for; matrix products, arithmetic and copies ran while one was open for 34% of the time, Pallas kernels for 20%

profile of v7, /device:TPU:0, one launch (start us, length us, event | category | flops | bytes accessed | tf_op | source)
XLA Modules:
  0.0 512.3 jit_solution(17844349530486024520)
XLA Ops:
  17.0 4.0 collective-permute-start.2
  40.8 10.0 %collective-permute-done = bf16[130,2048]{1,0:T(8,128)(2,1)} collective-permute-done((bf16[130,2048]{1,0:T(8,128)(2,1)S(1)}, bf16[130,2048]{1,0:T(8,128)(2,1)}, u32[]{:S(2)}, u32[]{:S(2)}) %collective-permute-start) | collective-permute-done | bytes 532512 | tf_op jit(solution)/shard_map/ppermute | solution.py:328
  65.7 3.8 fusion.5.x_ref
  69.4 28.7 %collective-permute-done.5.refs_2_ = bf16[256,1536]{1,0:T(8,128)(2,1)} collective-permute-done((bf16[256,1536]{1,0:T(8,128)(2,1)}, bf16[256,1536]{1,0:T(8,128)(2,1)}, u32[]{:S(2)}, u32[]{:S(2)}) %collective-permute-start.5) | collective-permute-done | bytes 786464 | tf_op jit(solution)/shard_map/ppermute | solution.py:328
  106.9 5.8 %shard_map.314.q_ref.k_ref.v_ref = bf16[512,1536]{1,0:T(8,128)(2,1)S(1)} custom-call(s32[7]{0:T(128)S(1)} %stack.46.at_ref, bf16[512,2048]{1,0:T(8,128)(2,1)S(1)} %copy-done.11, bf16[512,1536]{1,0:T(8,128)(2,1)S(1)} %copy-done.8, bf16[256,1536]{1,0:T(8,128)(2,1)} %collective-permute-done.3.refs_0_, bf16[256,1536]{1,0:T(8,128)(2,1)S(1)} %collective-permute-done.4.refs_1_, ...), custom_call_target="tpu_custom_call" | custom-call | flops 3221225472 | bytes 9961472 | tf_op jit(solution)/shard_map/pallas_call | solution.py:253
  113.6 7.2 %shard_map.315.context_ref = bf16[512,512]{1,0:T(8,128)(2,1)S(1)} custom-call(bf16[512,1536]{1,0:T(8,128)(2,1)S(1)} %shard_map.314.q_ref.k_ref.v_ref, bf16[512,1536]{1,0:T(8,128)(2,1)S(1)} %shard_map.314.q_ref.k_ref.v_ref, bf16[512,1536]{1,0:T(8,128)(2,1)S(1)} %shard_map.314.q_ref.k_ref.v_ref), custom_call_target="tpu_custom_call" | custom-call | flops 536870912 | bytes 2097152 | tf_op jit(solution)/shard_map/pallas_call | solution.py:93
  126.6 20.0 %collective-permute-done.11 = bf16[256,1024]{1,0:T(8,128)(2,1)S(1)} collective-permute-done((bf16[256,1024]{1,0:T(8,128)(2,1)S(1)}, bf16[256,1024]{1,0:T(8,128)(2,1)S(1)}, u32[]{:S(2)}, u32[]{:S(2)}) %collective-permute-start.11) | collective-permute-done | bytes 524320 | tf_op jit(solution)/shard_map/ppermute | solution.py:328
  148.9 5.9 %collective-permute-done.12 = bf16[128,1024]{1,0:T(8,128)(2,1)S(1)} collective-permute-done((bf16[128,1024]{1,0:T(8,128)(2,1)S(1)}, bf16[128,1024]{1,0:T(8,128)(2,1)S(1)}, u32[]{:S(2)}, u32[]{:S(2)}) %collective-permute-start.12) | collective-permute-done | bytes 262176 | tf_op jit(solution)/shard_map/ppermute | solution.py:328
  161.1 6.2 %collective-permute-done.15.refs_4_ = bf16[128,1024]{1,0:T(8,128)(2,1)S(1)} collective-permute-done((bf16[128,1024]{1,0:T(8,128)(2,1)S(1)}, bf16[128,1024]{1,0:T(8,128)(2,1)S(1)}, u32[]{:S(2)}, u32[]{:S(2)}) %collective-permute-start.15) | collective-permute-done | bytes 262176 | tf_op jit(solution)/shard_map/ppermute | solution.py:328
  171.1 8.6 %convolution_convert_fusion.4.refs_8_ = bf16[512,2048]{1,0:T(8,128)(2,1)S(1)} fusion(bf16[2048,2048]{1,0:T(8,128)(2,1)} %param.35, bf16[4096,2048]{1,0:T(8,128)(2,1)} %all-gather.4.cloned.1.call-done, s32[]{:T(128)S(6)} %select_n.93), kind=kOutput, calls=%fused_computation.18 | convolution fusion | flops 4296015872 | bytes 12582916 | tf_op jit(solution)/shard_map/dot_general | solution.py:37
  179.7 4.4 collective-permute-done.16.refs_5_
  186.3 3.4 copy-done.19
  189.7 12.4 %shard_map.316 = (bf16[512,2048]{1,0:T(8,128)(2,1)S(1)}, bf16[512,2048]{1,0:T(8,128)(2,1)S(1)}, f32[1,2048]{1,0:T(1,128)}) custom-call(s32[4]{0:T(128)S(1)} %iota_xor_fusion.member_ref, bf16[128,1024]{1,0:T(8,128)(2,1)S(1)} %get-tuple-element.203.refs_0_, bf16[128,1024]{1,0:T(8,128)(2,1)} %collective-permute-done.13.refs_1_, ...), custom_call_target="tpu_custom_call" | custom-call | flops 4294967296 | bytes 16777216 | tf_op jit(solution)/shard_map/pallas_call | solution.py:222
  202.1 8.3 %convolution_convert_fusion.3 = bf16[512,2048]{1,0:T(8,128)(2,1)S(1)} fusion(bf16[512,2048]{1,0:T(8,128)(2,1)S(1)} %get-tuple-element.93, bf16[2048,2048]{1,0:T(8,128)(2,1)} %refs_1_.1), kind=kOutput, calls=%fused_computation.17 | convolution fusion | flops 4296015872 | bytes 12582912 | tf_op jit(solution)/shard_map/dot_general | solution.py:37
  212.7 22.7 %convolution_convert_fusion.refs_3_ = bf16[4096,1024]{1,0:T(8,128)(2,1)} fusion(bf16[4096,2048]{1,0:T(8,128)(2,1)} %all-gather.4.cloned.1.call-done, bf16[2048,2048]{1,0:T(8,128)(2,1)S(1)} %bitcast.98, s32[]{:T(128)S(6)} %select_n.172), kind=kOutput, calls=%fused_computation.1 | convolution fusion | flops 17184063488 | bytes 29360132 | tf_op jit(solution)/shard_map/dot_general | solution.py:37
  237.6 12.2 %collective-permute-done.20 = bf16[128,1024]{1,0:T(8,128)(2,1)S(1)} collective-permute-done((bf16[128,1024]{1,0:T(8,128)(2,1)S(1)}, bf16[128,1024]{1,0:T(8,128)(2,1)S(1)}, u32[]{:S(2)}, u32[]{:S(2)}) %collective-permute-start.20) | collective-permute-done | bytes 262176 | tf_op jit(solution)/shard_map/ppermute | solution.py:328
  255.5 14.9 %fusion.40 = f32[512,2048]{1,0:T(8,128)} fusion(bf16[512,2048]{1,0:T(8,128)(2,1)S(1)} %get-tuple-element.99, bf16[2048,2048]{1,0:T(8,128)(2,1)S(1)} %bitcast.98), kind=kOutput, calls=%fused_computation.164 | convolution fusion | flops 4294967296 | bytes 14680064 | tf_op jit(solution)/shard_map/dot_general | solution.py:319
  274.0 4.5 convert_reduce_fusion
  278.6 7.0 %collective-permute-done.24 = bf16[256,1024]{1,0:T(8,128)(2,1)S(1)} collective-permute-done((bf16[256,1024]{1,0:T(8,128)(2,1)S(1)}, bf16[256,1024]{1,0:T(8,128)(2,1)S(1)}, u32[]{:S(2)}, u32[]{:S(2)}) %collective-permute-start.24) | collective-permute-done | bytes 524320 | tf_op jit(solution)/shard_map/ppermute | solution.py:328
  288.0 13.3 %shard_map.317 = (bf16[512,512]{1,0:T(8,128)(2,1)S(1)}, bf16[512,512]{1,0:T(8,128)(2,1)S(1)}, bf16[512,512]{1,0:T(8,128)(2,1)S(1)}) custom-call(bf16[512,1536]{1,0:T(8,128)(2,1)S(1)} %copy-done.3, bf16[512,1536]{1,0:T(8,128)(2,1)S(1)} %copy-done.3, bf16[512,1536]{1,0:T(8,128)(2,1)S(1)} %copy-done.3, bf16[512,512]{1,0:T(8,128)(2,1)S(1)} %convolution_convert_fusion.5.g_ref), custom_call_target="tpu_custom_call" | custom-call | flops 1342177280 | bytes 3670016 | tf_op jit(solution)/shard_map/pallas_call | solution.py:106
  301.4 5.5 %shard_map.318 = bf16[4,512,2048]{2,1,0:T(8,128)(2,1)S(1)} custom-call(bf16[512,2048]{1,0:T(8,128)(2,1)S(1)} %copy-done.12, bf16[512,512]{1,0:T(8,128)(2,1)S(1)} %get-tuple-element.105.q_ref, bf16[512,512]{1,0:T(8,128)(2,1)S(1)} %get-tuple-element.106.k_ref, bf16[512,512]{1,0:T(8,128)(2,1)S(1)} %get-tuple-element.107.v_ref, ...), custom_call_target="tpu_custom_call" | custom-call | flops 4294967296 | bytes 14680064 | tf_op jit(solution)/shard_map/pallas_call | solution.py:169
  319.2 5.2 %fusion.6 = (f32[2048]{0:T(1024)S(1)}, f32[2048]{0:T(1024)S(1)}, f32[512,2048]{1,0:T(8,128)S(1)}) fusion(bf16[512,2048]{1,0:T(8,128)(2,1)} %slice_dynamic-update-slice_fusion, f32[512]{0:T(512)S(1)} %add_rsqrt_fusion, f32[512]{0:T(512)S(1)} %broadcast_multiply_fusion, bf16[512,1536]{1,0:T(8,128)(2,1)S(1)} %constant_dynamic-update-slice_fusion.12, ...), kind=kOutput, calls=%fused_computation.10 | convolution fusion | flops 3227512832 | bytes 14176256 | tf_op jit(solution)/shard_map/dot_general | solution.py:37
  329.3 32.7 %shard_map.319 = (bf16[4096,1024]{1,0:T(8,128)(2,1)S(1)}, bf16[4096,1024]{1,0:T(8,128)(2,1)S(1)}, f32[1,1024]{1,0:T(1,128)S(1)}) custom-call(s32[1]{0:T(128)} %bitcast.22.place_ref, bf16[4096,2048]{1,0:T(8,128)(2,1)} %all-gather.6.cloned.1.call-done.refs_0_, bf16[2048,2048]{1,0:T(8,128)(2,1)} %refs_1_.1, ...), custom_call_target="tpu_custom_call" | custom-call | flops 17179869184 | bytes 46137344 | tf_op jit(solution)/shard_map/pallas_call | solution.py:150
  372.3 21.3 %convolution_convert_fusion.2.part_ref = bf16[1024,2048]{1,0:T(8,128)(2,1)} fusion(bf16[4096,1024]{1,0:T(8,128)(2,1)S(1)} %get-tuple-element.124, bf16[4096,2048]{1,0:T(8,128)(2,1)} %all-gather.4.cloned.1.call-done), kind=kOutput, calls=%fused_computation.15 | convolution fusion | flops 17181966336 | bytes 29360128 | tf_op jit(solution)/shard_map/dot_general | solution.py:39
  393.6 6.5 %reduce-scatter.2.cloned.1.call-done = bf16[4,64,2048]{2,1,0:T(8,128)(2,1)} async-done(((bf16[4,512,2048]{2,1,0:T(8,128)(2,1)}), bf16[4,64,2048]{2,1,0:T(8,128)(2,1)}) %reduce-scatter.2.cloned.1.call-update) | async-done | bytes 1048592 | tf_op jit(solution)/shard_map/reduce_scatter | solution.py:673
  414.9 23.7 %convolution_convert_fusion.1.part_ref = bf16[2048,1024]{1,0:T(8,128)(2,1)} fusion(bf16[4096,2048]{1,0:T(8,128)(2,1)} %all-gather.6.cloned.1.call-done.refs_0_, bf16[4096,1024]{1,0:T(8,128)(2,1)} %copy-done.20), kind=kOutput, calls=%fused_computation.14 | convolution fusion | flops 17181966336 | bytes 29360128 | tf_op jit(solution)/shard_map/dot_general | solution.py:39
  445.5 4.2 shard_map.320.refs_0_
  458.5 7.3 %shard_map.321.refs_0_ = f32[2048,2048]{1,0:T(8,128)} custom-call(s32[1]{0:T(128)} %bitcast.22.place_ref, bf16[2048,1024]{1,0:T(8,128)(2,1)} %convolution_convert_fusion.1.part_ref), custom_call_target="tpu_custom_call" | custom-call | bytes 12582912 | tf_op jit(solution)/shard_map/pallas_call | solution.py:289
  465.8 6.0 %shard_map.322 = f32[2048,2048]{1,0:T(8,128)} custom-call(s32[1]{0:T(128)S(6)} %sub.68.place_ref, bf16[1024,2048]{1,0:T(8,128)(2,1)} %collective-permute-done.38.part_ref, f32[2048,2048]{1,0:T(8,128)} %shard_map.320.refs_0_), custom_call_target="tpu_custom_call", output_to_operand_aliasing={{}: (2, {})} | custom-call | bytes 12582912 | tf_op jit(solution)/shard_map/pallas_call | solution.py:289
  472.4 7.4 %shard_map.323 = f32[2048,2048]{1,0:T(8,128)} custom-call(s32[1]{0:T(128)S(6)} %sub.68.place_ref, bf16[2048,1024]{1,0:T(8,128)(2,1)} %collective-permute-done.41.part_ref, f32[2048,2048]{1,0:T(8,128)} %shard_map.321.refs_0_), custom_call_target="tpu_custom_call", output_to_operand_aliasing={{}: (2, {})} | custom-call | bytes 12582912 | tf_op jit(solution)/shard_map/pallas_call | solution.py:289
  481.0 14.8 %all-gather.8.cloned.1.call-done.block_ref = bf16[4,512,2048]{2,1,0:T(8,128)(2,1)} async-done(((bf16[4,64,2048]{2,1,0:T(8,128)(2,1)}), bf16[4,512,2048]{2,1,0:T(8,128)(2,1)}) %all-gather.8.cloned.1.call-update) | async-done | bytes 8388624 | tf_op jit(solution)/shard_map/all_gather | solution.py:743
  499.2 6.2 %shard_map.324 = (f32[512,2048]{1,0:T(8,128)}, f32[512,2048]{1,0:T(8,128)}, f32[512,2048]{1,0:T(8,128)}, f32[512,2048]{1,0:T(8,128)}) custom-call(bf16[4,512,2048]{2,1,0:T(8,128)(2,1)S(1)} %copy-done.5), custom_call_target="tpu_custom_call" | custom-call | bytes 25165824 | tf_op jit(solution)/shard_map/pallas_call | solution.py:305
  (315 shorter events, 151.9 us)
Async XLA Ops:
  7.2 163.9 %all-gather.4.cloned.1.call-start = ((), (), s32[]{:S(2)}) async-start(), calls=%async_computation.1 | async-start | bytes 17301504 | tf_op jit(solution)/shard_map/all_gather | solution.py:612
  10.7 318.6 %all-gather.6.cloned.1.call-start = ((), (), s32[]{:S(2)}) async-start(), calls=%async_computation.2 | async-start | bytes 17301504 | tf_op jit(solution)/shard_map/all_gather | solution.py:629
  17.0 39.0 %collective-permute-start.2 = (bf16[130,2048]{1,0:T(8,128)(2,1)S(1)}, bf16[130,2048]{1,0:T(8,128)(2,1)}, u32[]{:S(2)}, u32[]{:S(2)}) collective-permute-start(bf16[130,2048]{1,0:T(8,128)(2,1)S(1)} %pad_maximum_fusion.5), channel_id=1, source_target_pairs={{0,3},{1,2},{2,1},{3,0},{4,7},{5,6},{6,5},{7,4},{8,11},{9,10},{10,... | collective-permute-start | bytes 1597448 | tf_op jit(solution)/shard_map/ppermute | solution.py:328
  21.0 33.2 %collective-permute-start.1 = (bf16[130,2048]{1,0:T(8,128)(2,1)S(1)}, bf16[130,2048]{1,0:T(8,128)(2,1)}, u32[]{:S(2)}, u32[]{:S(2)}) collective-permute-start(bf16[130,2048]{1,0:T(8,128)(2,1)S(1)} %pad_maximum_fusion.5), channel_id=1, source_target_pairs={{0,2},{1,3},{2,0},{3,1},{4,6},{5,7},{6,4},{7,5},{8,10},{9,11},{10,... | collective-permute-start | bytes 1597448 | tf_op jit(solution)/shard_map/ppermute | solution.py:328
  21.5 29.4 %collective-permute-start = (bf16[130,2048]{1,0:T(8,128)(2,1)S(1)}, bf16[130,2048]{1,0:T(8,128)(2,1)}, u32[]{:S(2)}, u32[]{:S(2)}) collective-permute-start(bf16[130,2048]{1,0:T(8,128)(2,1)S(1)} %pad_maximum_fusion.5), channel_id=1, source_target_pairs={{0,1},{1,0},{2,3},{3,2},{4,5},{5,4},{6,7},{7,6},{8,9},{9,8},{10,11... | collective-permute-start | bytes 1597448 | tf_op jit(solution)/shard_map/ppermute | solution.py:328
  28.3 69.8 %collective-permute-start.4 = (bf16[256,1536]{1,0:T(8,128)(2,1)}, bf16[256,1536]{1,0:T(8,128)(2,1)S(1)}, u32[]{:S(2)}, u32[]{:S(2)}) collective-permute-start(bf16[256,1536]{1,0:T(8,128)(2,1)} %pad_maximum_fusion.3), channel_id=1, source_target_pairs={{0,2},{1,3},{2,0},{3,1},{4,6},{5,7},{6,4},{7,5},{8,10},{9,11},{10,... | collective-permute-start | bytes 2359304 | tf_op jit(solution)/shard_map/ppermute | solution.py:328
  31.1 67.0 %collective-permute-start.3 = (bf16[256,1536]{1,0:T(8,128)(2,1)}, bf16[256,1536]{1,0:T(8,128)(2,1)}, u32[]{:S(2)}, u32[]{:S(2)}) collective-permute-start(bf16[256,1536]{1,0:T(8,128)(2,1)} %pad_maximum_fusion.2), channel_id=1, source_target_pairs={{0,1},{1,0},{2,3},{3,2},{4,5},{5,4},{6,7},{7,6},{8,9},{9,8},{10,11... | collective-permute-start | bytes 2359304 | tf_op jit(solution)/shard_map/ppermute | solution.py:328
  50.9 47.2 %collective-permute-start.5 = (bf16[256,1536]{1,0:T(8,128)(2,1)}, bf16[256,1536]{1,0:T(8,128)(2,1)}, u32[]{:S(2)}, u32[]{:S(2)}) collective-permute-start(bf16[256,1536]{1,0:T(8,128)(2,1)} %pad_maximum_fusion.4), channel_id=1, source_target_pairs={{0,3},{1,2},{2,1},{3,0},{4,7},{5,6},{6,5},{7,4},{8,11},{9,10},{10,... | collective-permute-start | bytes 2359304 | tf_op jit(solution)/shard_map/ppermute | solution.py:328
  122.9 23.7 %collective-permute-start.11 = (bf16[256,1024]{1,0:T(8,128)(2,1)S(1)}, bf16[256,1024]{1,0:T(8,128)(2,1)S(1)}, u32[]{:S(2)}, u32[]{:S(2)}) collective-permute-start(bf16[256,1024]{1,0:T(8,128)(2,1)S(1)} %pad_maximum_fusion.7), channel_id=1, source_target_pairs={{0,1},{1,0},{2,3},{3,2},{4,5},{5,4},{6,7},{7,6},{8,9},{9,8},{10,11... | collective-permute-start | bytes 1572872 | tf_op jit(solution)/shard_map/ppermute | solution.py:328
  124.9 23.3 %collective-permute-start.9 = (bf16[256,1024]{1,0:T(8,128)(2,1)S(1)}, bf16[256,1024]{1,0:T(8,128)(2,1)S(1)}, u32[]{:S(2)}, u32[]{:S(2)}) collective-permute-start(bf16[256,1024]{1,0:T(8,128)(2,1)S(1)} %pad_maximum_fusion.6), channel_id=1, source_target_pairs={{0,2},{1,3},{2,0},{3,1},{4,6},{5,7},{6,4},{7,5},{8,10},{9,11},{10,... | collective-permute-start | bytes 1572872 | tf_op jit(solution)/shard_map/ppermute | solution.py:328
  158.8 241.3 %reduce-scatter.2.cloned.1.call-start = ((), (), s32[]{:S(2)}) async-start(), calls=%async_computation.3 | async-start | bytes 9437184 | tf_op jit(solution)/shard_map/reduce_scatter | solution.py:673
  168.2 16.0 %collective-permute-start.16 = (bf16[256,1024]{1,0:T(8,128)(2,1)}, bf16[256,1024]{1,0:T(8,128)(2,1)}, u32[]{:S(2)}, u32[]{:S(2)}) collective-permute-start(bf16[256,1024]{1,0:T(8,128)(2,1)} %pad_maximum_fusion.9), channel_id=1, source_target_pairs={{0,1},{1,0},{2,3},{3,2},{4,5},{5,4},{6,7},{7,6},{8,9},{9,8},{10,11... | collective-permute-start | bytes 1572872 | tf_op jit(solution)/shard_map/ppermute | solution.py:328
  170.5 15.7 %collective-permute-start.14 = (bf16[256,1024]{1,0:T(8,128)(2,1)}, bf16[256,1024]{1,0:T(8,128)(2,1)}, u32[]{:S(2)}, u32[]{:S(2)}) collective-permute-start(bf16[256,1024]{1,0:T(8,128)(2,1)} %pad_maximum_fusion.8), channel_id=1, source_target_pairs={{0,2},{1,3},{2,0},{3,1},{4,6},{5,7},{6,4},{7,5},{8,10},{9,11},{10,... | collective-permute-start | bytes 1572872 | tf_op jit(solution)/shard_map/ppermute | solution.py:328
  210.8 24.7 %collective-permute-start.17 = (bf16[256,1024]{1,0:T(8,128)(2,1)S(1)}, bf16[256,1024]{1,0:T(8,128)(2,1)S(1)}, u32[]{:S(2)}, u32[]{:S(2)}) collective-permute-start(bf16[256,1024]{1,0:T(8,128)(2,1)S(1)} %pad_maximum_fusion.10), channel_id=1, source_target_pairs={{0,2},{1,3},{2,0},{3,1},{4,6},{5,7},{6,4},{7,5},{8,10},{9,11},{10,... | collective-permute-start | bytes 1572872 | tf_op jit(solution)/shard_map/ppermute | solution.py:328
  211.7 23.7 %collective-permute-start.18 = (bf16[256,1024]{1,0:T(8,128)(2,1)S(1)}, bf16[256,1024]{1,0:T(8,128)(2,1)S(1)}, u32[]{:S(2)}, u32[]{:S(2)}) collective-permute-start(bf16[256,1024]{1,0:T(8,128)(2,1)S(1)} %pad_maximum_fusion.11), channel_id=1, source_target_pairs={{0,1},{1,0},{2,3},{3,2},{4,5},{5,4},{6,7},{7,6},{8,9},{9,8},{10,11... | collective-permute-start | bytes 1572872 | tf_op jit(solution)/shard_map/ppermute | solution.py:328
  235.6 14.3 %collective-permute-start.20 = (bf16[128,1024]{1,0:T(8,128)(2,1)S(1)}, bf16[128,1024]{1,0:T(8,128)(2,1)S(1)}, u32[]{:S(2)}, u32[]{:S(2)}) collective-permute-start(bf16[128,1024]{1,0:T(8,128)(2,1)S(1)} %add_convert_fusion.2), channel_id=1, source_target_pairs={{0,2},{1,3},{2,0},{3,1},{4,6},{5,7},{6,4},{7,5},{8,10},{9,11},{10,... | collective-permute-start | bytes 786440 | tf_op jit(solution)/shard_map/ppermute | solution.py:328
  237.4 14.6 %collective-permute-start.19 = (bf16[128,1024]{1,0:T(8,128)(2,1)S(1)}, bf16[128,1024]{1,0:T(8,128)(2,1)S(1)}, u32[]{:S(2)}, u32[]{:S(2)}) collective-permute-start(bf16[128,1024]{1,0:T(8,128)(2,1)S(1)} %add_convert_fusion.3), channel_id=1, source_target_pairs={{0,1},{1,0},{2,3},{3,2},{4,5},{5,4},{6,7},{7,6},{8,9},{9,8},{10,11... | collective-permute-start | bytes 786440 | tf_op jit(solution)/shard_map/ppermute | solution.py:328
  254.7 15.7 %collective-permute-start.22 = (bf16[128,1024]{1,0:T(8,128)(2,1)S(1)}, bf16[128,1024]{1,0:T(8,128)(2,1)S(1)}, u32[]{:S(2)}, u32[]{:S(2)}) collective-permute-start(bf16[128,1024]{1,0:T(8,128)(2,1)S(1)} %get-tuple-element.199), channel_id=1, source_target_pairs={{0,2},{1,3},{2,0},{3,1},{4,6},{5,7},{6,4},{7,5},{8,10},{9,11},{10,... | collective-permute-start | bytes 786440 | tf_op jit(solution)/shard_map/ppermute | solution.py:328
  254.8 15.5 %collective-permute-start.21 = (bf16[128,1024]{1,0:T(8,128)(2,1)S(1)}, bf16[128,1024]{1,0:T(8,128)(2,1)S(1)}, u32[]{:S(2)}, u32[]{:S(2)}) collective-permute-start(bf16[128,1024]{1,0:T(8,128)(2,1)S(1)} %get-tuple-element.201), channel_id=1, source_target_pairs={{0,1},{1,0},{2,3},{3,2},{4,5},{5,4},{6,7},{7,6},{8,9},{9,8},{10,11... | collective-permute-start | bytes 786440 | tf_op jit(solution)/shard_map/ppermute | solution.py:328
  270.4 15.2 %collective-permute-start.24 = (bf16[256,1024]{1,0:T(8,128)(2,1)S(1)}, bf16[256,1024]{1,0:T(8,128)(2,1)S(1)}, u32[]{:S(2)}, u32[]{:S(2)}) collective-permute-start(bf16[256,1024]{1,0:T(8,128)(2,1)S(1)} %pad_maximum_fusion.13), channel_id=1, source_target_pairs={{0,1},{1,0},{2,3},{3,2},{4,5},{5,4},{6,7},{7,6},{8,9},{9,8},{10,11... | collective-permute-start | bytes 1572872 | tf_op jit(solution)/shard_map/ppermute | solution.py:328
  310.3 185.5 %all-gather.8.cloned.1.call-start = ((), (), s32[]{:S(2)}) async-start(), calls=%async_computation.4 | async-start | bytes 9437184 | tf_op jit(solution)/shard_map/all_gather | solution.py:743
  325.4 40.1 %collective-permute-start.30 = (bf16[128,2048]{1,0:T(8,128)(2,1)}, bf16[128,2048]{1,0:T(8,128)(2,1)}, u32[]{:S(2)}, u32[]{:S(2)}) collective-permute-start(bf16[128,2048]{1,0:T(8,128)(2,1)} %get-tuple-element.171), channel_id=1, source_target_pairs={{0,3},{1,2},{2,1},{3,0},{4,7},{5,6},{6,5},{7,4},{8,11},{9,10},{10,... | collective-permute-start | bytes 1572872 | tf_op jit(solution)/shard_map/ppermute | solution.py:328
  327.0 38.4 %collective-permute-start.29 = (bf16[128,2048]{1,0:T(8,128)(2,1)S(1)}, bf16[128,2048]{1,0:T(8,128)(2,1)}, u32[]{:S(2)}, u32[]{:S(2)}) collective-permute-start(bf16[128,2048]{1,0:T(8,128)(2,1)S(1)} %get-tuple-element.172), channel_id=1, source_target_pairs={{0,2},{1,3},{2,0},{3,1},{4,6},{5,7},{6,4},{7,5},{8,10},{9,11},{10,... | collective-permute-start | bytes 1572872 | tf_op jit(solution)/shard_map/ppermute | solution.py:328
  328.2 37.2 %collective-permute-start.28 = (bf16[128,2048]{1,0:T(8,128)(2,1)S(1)}, bf16[128,2048]{1,0:T(8,128)(2,1)}, u32[]{:S(2)}, u32[]{:S(2)}) collective-permute-start(bf16[128,2048]{1,0:T(8,128)(2,1)S(1)} %get-tuple-element.173), channel_id=1, source_target_pairs={{0,1},{1,0},{2,3},{3,2},{4,5},{5,4},{6,7},{7,6},{8,9},{9,8},{10,11... | collective-permute-start | bytes 1572872 | tf_op jit(solution)/shard_map/ppermute | solution.py:328
  368.8 24.8 %collective-permute-start.27 = (f32[4,512]{1,0:T(4,128)S(1)}, f32[4,512]{1,0:T(4,128)S(1)}, u32[]{:S(2)}, u32[]{:S(2)}) collective-permute-start(f32[4,512]{1,0:T(4,128)S(1)} %get-tuple-element.210), channel_id=1, source_target_pairs={{0,3},{1,2},{2,1},{3,0},{4,7},{5,6},{6,5},{7,4},{8,11},{9,10},{10,... | collective-permute-start | bytes 24584 | tf_op jit(solution)/shard_map/ppermute | solution.py:328
  370.4 23.1 %collective-permute-start.26 = (f32[4,512]{1,0:T(4,128)S(1)}, f32[4,512]{1,0:T(4,128)S(1)}, u32[]{:S(2)}, u32[]{:S(2)}) collective-permute-start(f32[4,512]{1,0:T(4,128)S(1)} %get-tuple-element.211), channel_id=1, source_target_pairs={{0,2},{1,3},{2,0},{3,1},{4,6},{5,7},{6,4},{7,5},{8,10},{9,11},{10,... | collective-permute-start | bytes 24584 | tf_op jit(solution)/shard_map/ppermute | solution.py:328
  371.7 21.9 %collective-permute-start.25 = (f32[4,512]{1,0:T(4,128)S(1)}, f32[4,512]{1,0:T(4,128)S(1)}, u32[]{:S(2)}, u32[]{:S(2)}) collective-permute-start(f32[4,512]{1,0:T(4,128)S(1)} %get-tuple-element.212), channel_id=1, source_target_pairs={{0,1},{1,0},{2,3},{3,2},{4,5},{5,4},{6,7},{7,6},{8,9},{9,8},{10,11... | collective-permute-start | bytes 24584 | tf_op jit(solution)/shard_map/ppermute | solution.py:328
  413.7 52.0 %collective-permute-start.38 = (bf16[1024,2048]{1,0:T(8,128)(2,1)}, bf16[1024,2048]{1,0:T(8,128)(2,1)}, u32[]{:S(2)}, u32[]{:S(2)}) collective-permute-start(bf16[1024,2048]{1,0:T(8,128)(2,1)} %convolution_convert_fusion.2.part_ref), channel_id=1, source_target_pairs={{0,4},{4,0},{8,12},{12,8},{16,20},{20,16},{24,28},{28,24},{1,5},{5... | collective-permute-start | bytes 12582920 | tf_op jit(solution)/shard_map/ppermute | solution.py:468
  438.6 33.7 %collective-permute-start.41 = (bf16[2048,1024]{1,0:T(8,128)(2,1)}, bf16[2048,1024]{1,0:T(8,128)(2,1)}, u32[]{:S(2)}, u32[]{:S(2)}) collective-permute-start(bf16[2048,1024]{1,0:T(8,128)(2,1)} %convolution_convert_fusion.1.part_ref), channel_id=1, source_target_pairs={{0,4},{4,0},{8,12},{12,8},{16,20},{20,16},{24,28},{28,24},{1,5},{5... | collective-permute-start | bytes 12582920 | tf_op jit(solution)/shard_map/ppermute | solution.py:468
  452.4 27.4 %collective-permute-start.37 = (bf16[128,2048]{1,0:T(8,128)(2,1)S(1)}, bf16[128,2048]{1,0:T(8,128)(2,1)S(1)}, u32[]{:S(2)}, u32[]{:S(2)}) collective-permute-start(bf16[128,2048]{1,0:T(8,128)(2,1)S(1)} %get-tuple-element.168), channel_id=1, source_target_pairs={{0,3},{1,2},{2,1},{3,0},{4,7},{5,6},{6,5},{7,4},{8,11},{9,10},{10,... | collective-permute-start | bytes 1572872 | tf_op jit(solution)/shard_map/ppermute | solution.py:328
  453.9 25.9 %collective-permute-start.36 = (bf16[128,2048]{1,0:T(8,128)(2,1)S(1)}, bf16[128,2048]{1,0:T(8,128)(2,1)S(1)}, u32[]{:S(2)}, u32[]{:S(2)}) collective-permute-start(bf16[128,2048]{1,0:T(8,128)(2,1)S(1)} %get-tuple-element.169), channel_id=1, source_target_pairs={{0,2},{1,3},{2,0},{3,1},{4,6},{5,7},{6,4},{7,5},{8,10},{9,11},{10,... | collective-permute-start | bytes 1572872 | tf_op jit(solution)/shard_map/ppermute | solution.py:328
  457.8 22.0 %collective-permute-start.35 = (bf16[128,2048]{1,0:T(8,128)(2,1)S(1)}, bf16[128,2048]{1,0:T(8,128)(2,1)S(1)}, u32[]{:S(2)}, u32[]{:S(2)}) collective-permute-start(bf16[128,2048]{1,0:T(8,128)(2,1)S(1)} %get-tuple-element.170), channel_id=1, source_target_pairs={{0,1},{1,0},{2,3},{3,2},{4,5},{5,4},{6,7},{7,6},{8,9},{9,8},{10,11... | collective-permute-start | bytes 1572872 | tf_op jit(solution)/shard_map/ppermute | solution.py:328
  (57 other events, 578.1 us)
Sparse Core Ops, SparseCore 0:
  11.5 153.9 all-gather.3
  168.9 134.6 all-gather.5
  310.5 89.5 reduce-scatter.1
  413.8 82.0 all-gather.7
